TPU v7x, 32 devices: a whole 2x2x4 slice. The times are simulated.
32 devices in a mesh: row: 4 (over y, x), col: 8 (over z, core).
Axes of the slice: x: 2, y: 2, z: 4, core: 2. Of those that a mesh axis runs over, the one named last changes fastest.
Arguments:
- velocity: float32 [3, 4, 256, 1024], P(None, None, 'row', 'col'), may hold values from -6 to 6
- stress: float32 [6, 4, 256, 1024], P(None, None, 'row', 'col'), may hold values from -6 to 6
- buoyancy: float32 [4, 256, 1024], P(None, 'row', 'col'), may hold values from 0.2 to 0.4
- lame: float32 [4, 256, 1024], P(None, 'row', 'col'), may hold values from 0.08 to 0.2
- shear: float32 [4, 256, 1024], P(None, 'row', 'col'), may hold values from 0.08 to 0.2
- kernel: bfloat16 [12, 3, 2, 1024, 256], P(None, None, None, ('row', 'col')), may hold values from -1.1953125 to 1.1953125
- history: bfloat16 [11, 3, 2, 1024, 256], P(None, None, None, ('row', 'col')), may hold values from -6 to 6
Outputs:
- new_velocity: float32 [3, 4, 256, 1024], P(None, None, 'row', 'col')
- new_stress: float32 [6, 4, 256, 1024], P(None, None, 'row', 'col')
- spectra: float32 [2, 3, 2, 1024, 256], P(None, None, None, ('row', 'col'))
All inputs are finite; a program needn't handle non-finite values.
Results may differ from a plain program's by a relative error of at most 0.0003.
Values sent between devices are 32-bit elements; how exact they have to be, the bound alone decides.
No kernel may reach another device: no remote copies, remote signals or barrier semaphores. Data moves between devices by JAX's collectives and lax.ppermute only.
A program may use at most 128 MiB of HBM per device.

v0:
```python
import functools
import math

import jax
import jax.numpy as jnp
from jax import lax
from jax.experimental import pallas as pl
from jax.experimental.pallas import tpu as pltpu
from jax.sharding import PartitionSpec as P

STEPS = 2
VMEM_LIMIT = 16 * 1024 * 1024
NEAR = 2.0 / 3.0
FAR = -1.0 / 12.0
F32 = jnp.float32
BF16 = jnp.bfloat16
NN = (((1,), (0,)), ((), ()))
NT = (((1,), (1,)), ((), ()))


def call(body, name, outs, *args, scratch=(), alias=None, flops=0):
    nbytes = sum(a.size * a.dtype.itemsize for a in args) + sum(
        math.prod(s) * jnp.dtype(d).itemsize for s, d in outs
    )
    results = pl.pallas_call(
        body,
        name=name,
        out_shape=[jax.ShapeDtypeStruct(s, d) for s, d in outs],
        in_specs=[
            pl.BlockSpec(memory_space=pltpu.SMEM if a.dtype == jnp.int32 else pltpu.VMEM)
            for a in args
        ],
        out_specs=[pl.BlockSpec(memory_space=pltpu.VMEM) for _ in outs],
        scratch_shapes=list(scratch),
        input_output_aliases=alias or {},
        compiler_params=pltpu.CompilerParams(vmem_limit_bytes=VMEM_LIMIT),
        cost_estimate=pl.CostEstimate(flops=flops, bytes_accessed=nbytes, transcendentals=0),
    )(*args)
    return list(results)


def split(x):
    hi = x.astype(BF16)
    return hi, (x - hi.astype(F32)).astype(BF16)


def dot3(a, b, dims):
    a_hi, a_lo = a
    b_hi, b_lo = b

    def one(u, v):
        return lax.dot_general(u, v, dims, preferred_element_type=F32)

    return one(a_hi, b_hi) + (one(a_lo, b_hi) + one(a_hi, b_lo))


def dot6(a, b, dims):
    return lax.dot_general(
        a, b, dims, precision=lax.Precision.HIGHEST, preferred_element_type=F32
    )


def iota(shape, dim):
    return lax.broadcasted_iota(jnp.int32, shape, dim)


def shift_perm(x, axis, shift):
    count = lax.axis_size(axis)
    return lax.ppermute(x, axis, [(i, (i + shift) % count) for i in range(count)])


def partner_perm(x):
    count = lax.axis_size("col")
    return lax.ppermute(x, "col", [(i, i ^ 1) for i in range(count)])


def tables(where, dims):
    rows, cols, xb, yb, kyb = dims
    nx, ny = rows * xb, cols * yb
    depth = cols // 2
    nk = rows * kyb

    def unit(phase, modulus):
        angle = (phase & (modulus - 1)).astype(F32) * (2.0 * math.pi / modulus)
        return jnp.cos(angle), jnp.sin(angle)

    def body(where_ref, oh, ol, ph, pl_, wh, wl):
        r, c = where_ref[0], where_ref[1]

        def put(hi_ref, lo_ref, index, value):
            hi, lo = split(value)
            hi_ref[index] = hi
            lo_ref[index] = lo

        for flip, hi_ref, lo_ref in ((0, oh, ol), (1, ph, pl_)):
            col = c ^ 1 if flip else c
            line = iota((nk, yb), 0)
            lane = iota((nk, yb), 1)
            wave = ((line // kyb + r) & (rows - 1)) * (cols * kyb) + col * kyb + line % kyb
            base_cos, base_sin = unit(wave * lane, ny)
            start = ((c - 2 * lane) & (cols - 1)) * yb
            turn_cos, turn_sin = unit(wave * start, ny)
            scale = 1.0 / math.sqrt(ny)
            for t in range(depth):
                tc, ts = turn_cos[:, t : t + 1] * scale, turn_sin[:, t : t + 1] * scale
                span = pl.ds(t * yb, yb)
                put(hi_ref, lo_ref, (pl.ds(0, nk), span), base_cos * tc - base_sin * ts)
                put(hi_ref, lo_ref, (pl.ds(nk, nk), span), -(base_sin * tc + base_cos * ts))
        base_cos, base_sin = unit(iota((xb, nx), 0) * iota((xb, nx), 1), nx)
        tall = max(8, rows)
        start = ((r - iota((tall, nx), 0)) & (rows - 1)) * xb
        turn_cos, turn_sin = unit(start * iota((tall, nx), 1), nx)
        scale = 1.0 / math.sqrt(nx)
        for s in range(rows):
            tc, ts = turn_cos[s : s + 1] * scale, turn_sin[s : s + 1] * scale
            cos = base_cos * tc - base_sin * ts
            sin = base_sin * tc + base_cos * ts
            top, low = pl.ds(2 * s * xb, xb), pl.ds((2 * s + 1) * xb, xb)
            put(wh, wl, (top, pl.ds(0, nx)), cos)
            put(wh, wl, (top, pl.ds(nx, nx)), -sin)
            put(wh, wl, (low, pl.ds(0, nx)), sin)
            put(wh, wl, (low, pl.ds(nx, nx)), cos)

    y_shape, x_shape = (2 * nk, depth * yb), (2 * nx, 2 * nx)
    outs = [(y_shape, BF16)] * 4 + [(x_shape, BF16)] * 2
    oh, ol, ph, pl_, wh, wl = call(body, "tables", outs, where)
    return (oh, ol), (ph, pl_), (wh, wl)


def past_sums(kernel, history):
    lags, comps, _, kyb, nx = kernel.shape

    def body(k_ref, h_ref, *out_refs):
        for comp in range(comps):
            line = pl.ds(comp * kyb, kyb)
            totals = [[None, None] for _ in range(STEPS)]
            for lag in range(1, lags):
                kr = k_ref[lag, comp, 0].astype(F32)
                ki = k_ref[lag, comp, 1].astype(F32)
                for step in range(STEPS):
                    if lag - 1 < step:
                        continue
                    hr = h_ref[lag - 1 - step, comp, 0].astype(F32)
                    hi = h_ref[lag - 1 - step, comp, 1].astype(F32)
                    for part, value in enumerate((kr * hr - ki * hi, kr * hi + ki * hr)):
                        old = totals[step][part]
                        totals[step][part] = value if old is None else old + value
            for step in range(STEPS):
                for part in range(2):
                    out_refs[step][line, pl.ds(part * nx, nx)] = totals[step][part]

    return call(body, "past", [((comps * kyb, 2 * nx), F32)] * STEPS, kernel, history)


ROW_PARTS = (0, 3, 4)
COL_PARTS = (3, 1, 5)


def edge_weights(yb):
    line, lane = iota((8, yb), 0), iota((8, yb), 1)
    target = jnp.where(line < 2, line, yb - 4 + line)
    return jnp.where((lane == target) & (line < 4), 1.0, 0.0).astype(F32)


def inner_weights(yb):
    gap = iota((yb, yb), 0) - iota((yb, yb), 1)
    value = jnp.where(gap == 1, NEAR, 0.0) - jnp.where(gap == -1, NEAR, 0.0)
    return value + jnp.where(gap == 2, FAR, 0.0) - jnp.where(gap == -2, FAR, 0.0)


def outer_weights(yb):
    line, lane = iota((8, yb), 0), iota((8, yb), 1)
    left_gap = jnp.where((line == 2) | (line == 3), line - 4 - lane, 99)
    right_gap = jnp.where(line < 2, yb + line - lane, 99)

    def value(gap):
        near = jnp.where(gap == 1, NEAR, 0.0) - jnp.where(gap == -1, NEAR, 0.0)
        return near + jnp.where(gap == 2, FAR, 0.0) - jnp.where(gap == -2, FAR, 0.0)

    return value(left_gap), value(right_gap)


def put_borders(planes, row_planes, col_planes, edge_ref, first_ref, last_ref):
    xb, yb = planes(row_planes[0]).shape
    for j, which in enumerate(row_planes):
        plane = planes(which)
        first_ref[2 * j : 2 * j + 2, :] = plane[:2]
        last_ref[2 * j : 2 * j + 2, :] = plane[xb - 2 :]
    stacked = jnp.concatenate([planes(which) for which in col_planes], axis=0)
    edge_ref[...] = dot6(edge_weights(yb), stacked, NT)


def row_deriv(pad_ref, plane, above, below):
    xb = plane.shape[0]
    pad_ref[8 : 8 + xb, :] = plane
    pad_ref[6:8, :] = above
    pad_ref[8 + xb : 10 + xb, :] = below
    near = pad_ref[9 : 9 + xb, :] - pad_ref[7 : 7 + xb, :]
    far = pad_ref[10 : 10 + xb, :] - pad_ref[6 : 6 + xb, :]
    return NEAR * near + FAR * far


def col_deriv(stacked, left, right):
    yb = stacked.shape[1]
    left_w, right_w = outer_weights(yb)
    inner = dot6(stacked, inner_weights(yb), NN)
    return inner + (dot6(left.T, left_w, NN) + dot6(right.T, right_w, NN))


def depth_deriv(at, layer, layers):
    total = None
    for step, weight in ((1, NEAR), (-1, -NEAR), (2, FAR), (-2, -FAR)):
        if 0 <= layer + step < layers:
            term = weight * at(layer + step)
            total = term if total is None else total + term
    return total


def borders_shapes(layers, xb, yb):
    planes = 3 * layers
    return [((8, planes * xb), F32), ((2 * planes, yb), F32), ((2 * planes, yb), F32)]


def first_borders(stress):
    _, layers, xb, yb = stress.shape

    def body(s_ref, *outs):
        rows = [(p, l) for p in ROW_PARTS for l in range(layers)]
        cols = [(p, l) for p in COL_PARTS for l in range(layers)]
        put_borders(lambda w: s_ref[w[0], w[1]], rows, cols, *outs)

    return call(body, "borders", borders_shapes(layers, xb, yb), stress)


def exchange(borders):
    edge, first, last = borders
    above = shift_perm(last, "row", 1)
    below = shift_perm(first, "row", -1)
    left = shift_perm(edge, "col", 1)
    right = shift_perm(edge, "col", -1)
    return above, below, left, right


def push_velocity(velocity, stress, buoyancy, halo):
    comps, layers, xb, yb = velocity.shape

    def body(v_ref, s_ref, b_ref, up, dn, lf, rt, nv_ref, top_ref, edge, first, last, pad):
        stacked = jnp.concatenate(
            [s_ref[p, l] for p in COL_PARTS for l in range(layers)], axis=0
        )
        along_y = col_deriv(stacked, lf[...], rt[...])
        depth_parts = (4, 5, 2)
        for comp in range(comps):
            for layer in range(layers):
                j = comp * layers + layer
                pair = slice(2 * j, 2 * j + 2)
                force = row_deriv(pad.at[j], s_ref[ROW_PARTS[comp], layer], up[pair, :], dn[pair, :])
                force = force + along_y[j * xb : (j + 1) * xb]
                force = force + depth_deriv(lambda l: s_ref[depth_parts[comp], l], layer, layers)
                new = v_ref[comp, layer] + b_ref[layer] * force
                nv_ref[comp, layer] = new
                if layer == 0:
                    top_ref[comp * xb : (comp + 1) * xb, :] = new
        planes = [(c, l) for c in range(comps) for l in range(layers)]
        put_borders(lambda w: nv_ref[w[0], w[1]], planes, planes, edge, first, last)

    outs = [(velocity.shape, F32), ((comps * xb, yb), F32)] + borders_shapes(layers, xb, yb)
    nv, top, *borders = call(
        body, "push_velocity", outs, velocity, stress, buoyancy, *halo,
        scratch=[pltpu.VMEM((comps * layers, xb + 16, yb), F32)],
    )
    return nv, top, borders


def push_stress(stress, velocity, lame, shear, halo):
    comps, layers, xb, yb = velocity.shape

    def body(s_ref, v_ref, l_ref, m_ref, up, dn, lf, rt, ns_ref, pad):
        stacked = jnp.concatenate(
            [v_ref[c, l] for c in range(comps) for l in range(layers)], axis=0
        )
        along_y = col_deriv(stacked, lf[...], rt[...])
        for layer in range(layers):
            gx, gy, gz = [], [], []
            for comp in range(comps):
                j = comp * layers + layer
                pair = slice(2 * j, 2 * j + 2)
                gx.append(row_deriv(pad.at[j], v_ref[comp, layer], up[pair, :], dn[pair, :]))
                gy.append(along_y[j * xb : (j + 1) * xb])
                gz.append(depth_deriv(lambda l: v_ref[comp, l], layer, layers))
            lam, mu = l_ref[layer], m_ref[layer]
            spread = lam * (gx[0] + gy[1] + gz[2])
            twice = 2.0 * mu
            ns_ref[0, layer] = s_ref[0, layer] + spread + twice * gx[0]
            ns_ref[1, layer] = s_ref[1, layer] + spread + twice * gy[1]
            ns_ref[2, layer] = s_ref[2, layer] + spread + twice * gz[2]
            ns_ref[3, layer] = s_ref[3, layer] + mu * (gy[0] + gx[1])
            ns_ref[4, layer] = s_ref[4, layer] + mu * (gz[0] + gx[2])
            ns_ref[5, layer] = s_ref[5, layer] + mu * (gz[1] + gy[2])

    return call(
        body, "push_stress", [(stress.shape, F32)], stress, velocity, lame, shear, *halo,
        scratch=[pltpu.VMEM((comps * layers, xb + 16, yb), F32)],
    )[0]


def add_traction(stress, pieces, with_borders):
    _, layers, xb, yb = stress.shape

    def body(s_ref, *refs):
        count = len(pieces)
        ns_ref, *outs = refs[count:]
        total = refs[0][...]
        for ref in refs[1:count]:
            total = total + ref[...]
        ns_ref[...] = s_ref[...]
        for comp, part in enumerate((4, 5, 2)):
            ns_ref[part, 0] = s_ref[part, 0] + total[comp * xb : (comp + 1) * xb]
        if with_borders:
            rows = [(p, l) for p in ROW_PARTS for l in range(layers)]
            cols = [(p, l) for p in COL_PARTS for l in range(layers)]
            put_borders(lambda w: ns_ref[w[0], w[1]], rows, cols, *outs)

    outs = [(stress.shape, F32)] + (borders_shapes(layers, xb, yb) if with_borders else [])
    new, *borders = call(body, "traction", outs, stress, *pieces)
    return new, borders


def part_forward(blocks, table, dims, name):
    rows, cols, xb, yb, kyb = dims
    nk = rows * kyb
    comps = blocks[0].shape[0] // xb

    def body(*refs):
        hi, lo, out = refs[-3:]
        data = jnp.concatenate([ref[...] for ref in refs[:-3]], axis=1)
        total = dot3((hi[...], lo[...]), split(data), NT)
        for s in range(rows):
            for comp in range(comps):
                lane = slice(comp * xb, (comp + 1) * xb)
                real = total[s * kyb : (s + 1) * kyb, lane]
                imag = total[nk + s * kyb : nk + (s + 1) * kyb, lane]
                at = (s * comps + comp) * kyb
                out[at : at + kyb, :] = jnp.concatenate([real, imag], axis=1)

    return call(body, name, [((rows * comps * kyb, 2 * xb), F32)], *blocks, *table)[0]


def join(mine, other, dims):
    rows = dims[0]
    height = mine.shape[0] // rows

    def body(a_ref, b_ref, *outs):
        for s, out in enumerate(outs):
            span = slice(s * height, (s + 1) * height)
            out[...] = a_ref[span, :] + b_ref[span, :]

    return call(body, "join", [((height, mine.shape[1]), F32)] * rows, mine, other)


def convolve(blocks, table, past, kernel, before, dims):
    rows, cols, xb, yb, kyb = dims
    nx = rows * xb
    comps = blocks[0].shape[0] // kyb
    step = len(before)

    def body(*refs):
        ins, outs = refs[: rows + 4 + step], refs[rows + 4 + step :]
        wide = (ins[rows][...], ins[rows + 1][...])
        past_ref, k_ref, olds = ins[rows + 2], ins[rows + 3], ins[rows + 4 :]
        data = jnp.concatenate([ref[...] for ref in ins[:rows]], axis=1)
        spec = dot3(split(data), wide, NN)
        spec_ref = outs[0]
        loads = []
        for comp in range(comps):
            line = slice(comp * kyb, (comp + 1) * kyb)
            now = (spec[line, :nx], spec[line, nx:])
            if step == STEPS - 1:
                for n in range(step):
                    spec_ref[n, comp] = olds[n][comp]
                spec_ref[step, comp, 0] = now[0]
                spec_ref[step, comp, 1] = now[1]
            else:
                spec_ref[comp, 0] = now[0]
                spec_ref[comp, 1] = now[1]
            real, imag = past_ref[line, :nx], past_ref[line, nx:]
            terms = [now] + [(old[comp, 0], old[comp, 1]) for old in reversed(olds)]
            for lag, (sr, si) in enumerate(terms):
                kr, ki = k_ref[lag, comp, 0].astype(F32), k_ref[lag, comp, 1].astype(F32)
                real = real + (kr * sr - ki * si)
                imag = imag + (kr * si + ki * sr)
            loads.append(jnp.concatenate([real, imag], axis=1))
        back = dot3(split(jnp.concatenate(loads, axis=0)), wide, NT)
        for s, out in enumerate(outs[1:]):
            out[...] = back[:, s * 2 * xb : (s + 1) * 2 * xb]

    one = (comps, 2, kyb, nx)
    spec_shape = (STEPS,) + one if step == STEPS - 1 else one
    outs = [(spec_shape, F32)] + [((comps * kyb, 2 * xb), F32)] * rows
    spec, *pieces = call(body, "convolve", outs, *blocks, *table, past, kernel, *before)
    return spec, pieces


def turn(blocks, dims):
    rows, cols, xb, yb, kyb = dims
    comps = blocks[0].shape[0] // kyb

    def body(*refs):
        out = refs[-1]
        for comp in range(comps):
            line = slice(comp * kyb, (comp + 1) * kyb)
            flat = jnp.concatenate([ref[line, :] for ref in refs[:-1]], axis=0).T
            out[comp * xb : (comp + 1) * xb, :] = jnp.concatenate([flat[:xb], flat[xb:]], axis=1)

    return call(body, "turn", [((comps * xb, 2 * rows * kyb), F32)], *blocks)[0]


def part_inverse(data, table, dims):
    cols, yb = dims[1], dims[3]

    def body(d_ref, hi, lo, out):
        out[...] = dot3(split(d_ref[...]), (hi[...], lo[...]), NN)

    shape = (data.shape[0], cols // 2 * yb)
    return call(body, "inverse_mine", [(shape, F32)], data, *table)[0]


def rest_inverse(mine, data, table, dims):
    cols, yb = dims[1], dims[3]

    def body(m_ref, d_ref, hi, lo, *outs):
        total = m_ref[...] + dot3(split(d_ref[...]), (hi[...], lo[...]), NN)
        for t, out in enumerate(outs):
            out[...] = total[:, t * yb : (t + 1) * yb]

    outs = [((data.shape[0], yb), F32)] * (cols // 2)
    return call(body, "inverse_other", outs, mine, data, *table)


def on_device(velocity, stress, buoyancy, lame, shear, kernel, history):
    rows, cols = lax.axis_size("row"), lax.axis_size("col")
    xb, yb = velocity.shape[2:]
    kyb = kernel.shape[3]
    dims = (rows, cols, xb, yb, kyb)
    where = jnp.stack([lax.axis_index("row"), lax.axis_index("col")]).astype(jnp.int32)

    halo = exchange(first_borders(stress))
    mine, other, wide = tables(where, dims)
    past = past_sums(kernel, history)
    recent = kernel[:STEPS]
    spectra = []
    for step in range(STEPS):
        velocity, top, borders = push_velocity(velocity, stress, buoyancy, halo)
        blocks = [top] + [shift_perm(top, "col", 2 * t) for t in range(1, cols // 2)]
        sent = part_forward(blocks, other, dims, "forward_other")
        came = partner_perm(sent)
        kept = part_forward(blocks, mine, dims, "forward_mine")
        pieces = join(kept, came, dims)
        pieces = pieces[:1] + [shift_perm(pieces[s], "row", s) for s in range(1, rows)]
        spec, pieces = convolve(pieces, wide, past[step], recent, spectra, dims)
        spectra.append(spec)
        pieces = pieces[:1] + [shift_perm(pieces[s], "row", -s) for s in range(1, rows)]
        flat = turn(pieces, dims)
        flat_other = partner_perm(flat)
        total = part_inverse(flat, mine, dims)
        pieces = rest_inverse(total, flat_other, other, dims)
        pieces = pieces[:1] + [shift_perm(pieces[t], "col", -2 * t) for t in range(1, cols // 2)]
        stress = push_stress(stress, velocity, lame, shear, exchange(borders))
        stress, borders = add_traction(stress, pieces, step < STEPS - 1)
        if step < STEPS - 1:
            halo = exchange(borders)
    return (velocity, stress, spectra[-1])


def solution(mesh):
    return jax.shard_map(
        on_device,
        mesh=mesh,
        in_specs=(
            P(None, None, "row", "col"),
            P(None, None, "row", "col"),
            P(None, "row", "col"),
            P(None, "row", "col"),
            P(None, "row", "col"),
            P(None, None, None, ("row", "col"), None),
            P(None, None, None, ("row", "col"), None),
        ),
        out_specs=(
            P(None, None, "row", "col"),
            P(None, None, "row", "col"),
            P(None, None, None, ("row", "col"), None),
        ),
        check_vma=False,
    )
```

profile of v0, /device:TPU:0, one launch (start us, length us, event | category | flops | bytes accessed | tf_op | source)
XLA Modules:
  0.0 120.4 jit_solution(16584328050393922060)
XLA Ops:
  2.2 4.5 %collective-permute-start.3 = (f32[8,768]{1,0:T(8,128)S(1)}, f32[8,768]{1,0:T(8,128)S(1)}, u32[]{:S(2)}, u32[]{:S(2)}) collective-permute-start(f32[8,768]{1,0:T(8,128)S(1)} %get-tuple-element.56), channel_id=1, source_target_pairs={{0,7},{1,0},{2,1},{3,2},{4,3},{5,4},{6,5},{7,6},{8,15},{9,8},{10,9... | collective-permute-start | bytes 73736 | tf_op jit(solution)/shard_map/ppermute | solution.py:69
  6.7 1.5 %collective-permute-start = (f32[24,128]{1,0:T(8,128)S(1)}, f32[24,128]{1,0:T(8,128)S(1)}, u32[]{:S(2)}, u32[]{:S(2)}) collective-permute-start(f32[24,128]{1,0:T(8,128)S(1)} %get-tuple-element.54), channel_id=1, source_target_pairs={{0,8},{8,16},{16,24},{24,0},{1,9},{9,17},{17,25},{25,1},{2,10},{10... | collective-permute-start | bytes 36872 | tf_op jit(solution)/shard_map/ppermute | solution.py:69
  9.6 1.7 %collective-permute-done.up = f32[24,128]{1,0:T(8,128)S(1)} collective-permute-done((f32[24,128]{1,0:T(8,128)S(1)}, f32[24,128]{1,0:T(8,128)S(1)}, u32[]{:S(2)}, u32[]{:S(2)}) %collective-permute-start) | collective-permute-done | bytes 12320 | tf_op jit(solution)/shard_map/ppermute | solution.py:69
  13.8 2.2 %push_velocity.2 = (f32[3,4,64,128]{3,2,1,0:T(8,128)S(1)}, f32[192,128]{1,0:T(8,128)S(1)}, f32[8,768]{1,0:T(8,128)S(1)}, f32[24,128]{1,0:T(8,128)S(1)}, f32[24,128]{1,0:T(8,128)S(1)}) custom-call(f32[3,4,64,128]{3,2,1,0:T(8,128)S(1)} %copy-done.9, f32[6,4,64,128]{3,2,1,0:T(8,128)S(1)} %copy-done.1, f32[4,64,128]{2,1,0:T(8,128)S(1)} %copy-done.6, ...), custom_call_target="tpu_custom_call" | custom-call | bytes 1925120 | tf_op jit(solution)/shard_map/push_velocity/pallas_call | solution.py:25
  18.3 2.3 %tables.1 = (bf16[256,512]{1,0:T(8,128)(2,1)S(1)}, bf16[256,512]{1,0:T(8,128)(2,1)S(1)}, bf16[256,512]{1,0:T(8,128)(2,1)S(1)}, bf16[256,512]{1,0:T(8,128)(2,1)S(...) custom-call(s32[2]{0:T(128)S(1)} %pad_add_fusion.where_ref), custom_call_target="tpu_custom_call" | custom-call | bytes 2097160 | tf_op jit(solution)/shard_map/tables/pallas_call | solution.py:25
  20.7 6.9 %collective-permute-done.9.refs_2_ = f32[192,128]{1,0:T(8,128)S(1)} collective-permute-done((f32[192,128]{1,0:T(8,128)S(1)}, f32[192,128]{1,0:T(8,128)S(1)}, u32[]{:S(2)}, u32[]{:S(2)}) %collective-permute-start.9) | collective-permute-done | bytes 98336 | tf_op jit(solution)/shard_map/ppermute | solution.py:69
  29.6 2.4 %collective-permute-start.12 = (f32[96,128]{1,0:T(8,128)S(1)}, f32[96,128]{1,0:T(8,128)S(1)}, u32[]{:S(2)}, u32[]{:S(2)}) collective-permute-start(f32[96,128]{1,0:T(8,128)S(1)} %get-tuple-element.67), channel_id=1, source_target_pairs={{0,8},{8,16},{16,24},{24,0},{1,9},{9,17},{17,25},{25,1},{2,10},{10... | collective-permute-start | bytes 147464 | tf_op jit(solution)/shard_map/ppermute | solution.py:69
  32.6 1.6 %collective-permute-start.14 = (f32[96,128]{1,0:T(8,128)S(1)}, f32[96,128]{1,0:T(8,128)S(1)}, u32[]{:S(2)}, u32[]{:S(2)}) collective-permute-start(f32[96,128]{1,0:T(8,128)S(1)} %get-tuple-element.69), channel_id=1, source_target_pairs={{0,24},{8,0},{16,8},{24,16},{1,25},{9,1},{17,9},{25,17},{2,26},{10... | collective-permute-start | bytes 147464 | tf_op jit(solution)/shard_map/ppermute | solution.py:69
  37.6 2.5 %collective-permute-start.15 = (f32[96,128]{1,0:T(8,128)S(1)}, f32[96,128]{1,0:T(8,128)S(1)}, u32[]{:S(2)}, u32[]{:S(2)}) collective-permute-start(f32[96,128]{1,0:T(8,128)S(1)} %get-tuple-element.74), channel_id=1, source_target_pairs={{0,24},{8,0},{16,8},{24,16},{1,25},{9,1},{17,9},{25,17},{2,26},{10... | collective-permute-start | bytes 147464 | tf_op jit(solution)/shard_map/ppermute | solution.py:69
  41.8 2.3 %collective-permute-done.16.refs_2_ = f32[96,128]{1,0:T(8,128)S(1)} collective-permute-done((f32[96,128]{1,0:T(8,128)S(1)}, f32[96,128]{1,0:T(8,128)S(1)}, u32[]{:S(2)}, u32[]{:S(2)}) %collective-permute-start.16) | collective-permute-done | bytes 49184 | tf_op jit(solution)/shard_map/ppermute | solution.py:69
  49.7 1.9 %collective-permute-start.21 = (f32[192,128]{1,0:T(8,128)S(1)}, f32[192,128]{1,0:T(8,128)S(1)}, u32[]{:S(2)}, u32[]{:S(2)}) collective-permute-start(f32[192,128]{1,0:T(8,128)S(1)} %get-tuple-element.80), channel_id=1, source_target_pairs={{0,2},{1,3},{2,4},{3,5},{4,6},{5,7},{6,0},{7,1},{8,10},{9,11},{10,... | collective-permute-start | bytes 294920 | tf_op jit(solution)/shard_map/ppermute | solution.py:69
  51.6 2.9 %collective-permute-start.5 = (f32[24,128]{1,0:T(8,128)S(1)}, f32[24,128]{1,0:T(8,128)S(1)}, u32[]{:S(2)}, u32[]{:S(2)}) collective-permute-start(f32[24,128]{1,0:T(8,128)S(1)} %get-tuple-element.59), channel_id=1, source_target_pairs={{0,24},{8,0},{16,8},{24,16},{1,25},{9,1},{17,9},{25,17},{2,26},{10... | collective-permute-start | bytes 36872 | tf_op jit(solution)/shard_map/ppermute | solution.py:69
  54.6 1.7 %collective-permute-done.4.up = f32[24,128]{1,0:T(8,128)S(1)} collective-permute-done((f32[24,128]{1,0:T(8,128)S(1)}, f32[24,128]{1,0:T(8,128)S(1)}, u32[]{:S(2)}, u32[]{:S(2)}) %collective-permute-start.4) | collective-permute-done | bytes 12320 | tf_op jit(solution)/shard_map/ppermute | solution.py:69
  58.0 3.5 %collective-permute-done.6.lf = f32[8,768]{1,0:T(8,128)S(1)} collective-permute-done((f32[8,768]{1,0:T(8,128)S(1)}, f32[8,768]{1,0:T(8,128)S(1)}, u32[]{:S(2)}, u32[]{:S(2)}) %collective-permute-start.6) | collective-permute-done | bytes 24608 | tf_op jit(solution)/shard_map/ppermute | solution.py:69
  63.9 2.8 %collective-permute-start.22 = (f32[24,128]{1,0:T(8,128)S(1)}, f32[24,128]{1,0:T(8,128)S(1)}, u32[]{:S(2)}, u32[]{:S(2)}) collective-permute-start(f32[24,128]{1,0:T(8,128)S(1)} %get-tuple-element.82), channel_id=1, source_target_pairs={{0,8},{8,16},{16,24},{24,0},{1,9},{9,17},{17,25},{25,1},{2,10},{10... | collective-permute-start | bytes 36872 | tf_op jit(solution)/shard_map/ppermute | solution.py:69
  66.8 1.7 %collective-permute-done.22.up = f32[24,128]{1,0:T(8,128)S(1)} collective-permute-done((f32[24,128]{1,0:T(8,128)S(1)}, f32[24,128]{1,0:T(8,128)S(1)}, u32[]{:S(2)}, u32[]{:S(2)}) %collective-permute-start.22) | collective-permute-done | bytes 12320 | tf_op jit(solution)/shard_map/ppermute | solution.py:69
  68.5 1.9 %collective-permute-done.23.dn = f32[24,128]{1,0:T(8,128)S(1)} collective-permute-done((f32[24,128]{1,0:T(8,128)S(1)}, f32[24,128]{1,0:T(8,128)S(1)}, u32[]{:S(2)}, u32[]{:S(2)}) %collective-permute-start.23) | collective-permute-done | bytes 12320 | tf_op jit(solution)/shard_map/ppermute | solution.py:69
  70.4 2.3 %push_velocity.3 = (f32[3,4,64,128]{3,2,1,0:T(8,128)}, f32[192,128]{1,0:T(8,128)S(1)}, f32[8,768]{1,0:T(8,128)S(1)}, f32[24,128]{1,0:T(8,128)S(1)}, f32[24,128]{1,0:T(8,128)S(1)}) custom-call(f32[3,4,64,128]{3,2,1,0:T(8,128)S(1)} %get-tuple-element.57.v_ref, f32[6,4,64,128]{3,2,1,0:T(8,128)S(1)} %get-tuple-element.81.s_ref, f32[4,64,128]{2,1,0:T(8,128)S(1)} %copy-done.7, ...), custom_call_target="tpu_custom_call" | custom-call | bytes 1925120 | tf_op jit(solution)/shard_map/push_velocity/pallas_call | solution.py:25
  72.8 1.9 %collective-permute-start.30 = (f32[192,128]{1,0:T(8,128)S(1)}, f32[192,128]{1,0:T(8,128)S(1)}, u32[]{:S(2)}, u32[]{:S(2)}) collective-permute-start(f32[192,128]{1,0:T(8,128)S(1)} %get-tuple-element.89.refs_0_), channel_id=1, source_target_pairs={{0,2},{1,3},{2,4},{3,5},{4,6},{5,7},{6,0},{7,1},{8,10},{9,11},{10,... | collective-permute-start | bytes 294920 | tf_op jit(solution)/shard_map/ppermute | solution.py:69
  74.7 2.6 %collective-permute-done.32.refs_3_ = f32[192,128]{1,0:T(8,128)S(1)} collective-permute-done((f32[192,128]{1,0:T(8,128)S(1)}, f32[192,128]{1,0:T(8,128)S(1)}, u32[]{:S(2)}, u32[]{:S(2)}) %collective-permute-start.32) | collective-permute-done | bytes 98336 | tf_op jit(solution)/shard_map/ppermute | solution.py:69
  77.3 5.9 %collective-permute-done.31.refs_2_ = f32[192,128]{1,0:T(8,128)S(1)} collective-permute-done((f32[192,128]{1,0:T(8,128)S(1)}, f32[192,128]{1,0:T(8,128)S(1)}, u32[]{:S(2)}, u32[]{:S(2)}) %collective-permute-start.31) | collective-permute-done | bytes 98336 | tf_op jit(solution)/shard_map/ppermute | solution.py:69
  87.1 1.6 %collective-permute-start.36 = (f32[96,128]{1,0:T(8,128)S(1)}, f32[96,128]{1,0:T(8,128)S(1)}, u32[]{:S(2)}, u32[]{:S(2)}) collective-permute-start(f32[96,128]{1,0:T(8,128)S(1)} %get-tuple-element.93), channel_id=1, source_target_pairs={{0,24},{8,0},{16,8},{24,16},{1,25},{9,1},{17,9},{25,17},{2,26},{10... | collective-permute-start | bytes 147464 | tf_op jit(solution)/shard_map/ppermute | solution.py:69
  88.7 1.7 %collective-permute-done.34.refs_1_ = f32[96,128]{1,0:T(8,128)S(1)} collective-permute-done((f32[96,128]{1,0:T(8,128)S(1)}, f32[96,128]{1,0:T(8,128)S(1)}, u32[]{:S(2)}, u32[]{:S(2)}) %collective-permute-start.34) | collective-permute-done | bytes 49184 | tf_op jit(solution)/shard_map/ppermute | solution.py:69
  91.2 1.5 %convolve.3 = (f32[2,3,2,32,256]{4,3,2,1,0:T(8,128)}, f32[96,128]{1,0:T(8,128)S(1)}, f32[96,128]{1,0:T(8,128)S(1)}, f32[96,128]{1,0:T(8,128)S(1)}, f32[96,128]{1,0:T(8,128)S(1)}) custom-call(f32[96,128]{1,0:T(8,128)S(1)} %get-tuple-element.90.refs_0_, f32[96,128]{1,0:T(8,128)S(1)} %collective-permute-done.34.refs_1_, ...), custom_call_target="tpu_custom_call" | custom-call | bytes 2424832 | tf_op jit(solution)/shard_map/convolve/pallas_call | solution.py:25
  92.7 2.5 %collective-permute-start.37 = (f32[96,128]{1,0:T(8,128)S(1)}, f32[96,128]{1,0:T(8,128)S(1)}, u32[]{:S(2)}, u32[]{:S(2)}) collective-permute-start(f32[96,128]{1,0:T(8,128)S(1)} %get-tuple-element.97), channel_id=1, source_target_pairs={{0,24},{8,0},{16,8},{24,16},{1,25},{9,1},{17,9},{25,17},{2,26},{10... | collective-permute-start | bytes 147464 | tf_op jit(solution)/shard_map/ppermute | solution.py:69
  95.2 1.5 %collective-permute-start.38 = (f32[96,128]{1,0:T(8,128)S(1)}, f32[96,128]{1,0:T(8,128)S(1)}, u32[]{:S(2)}, u32[]{:S(2)}) collective-permute-start(f32[96,128]{1,0:T(8,128)S(1)} %get-tuple-element.98), channel_id=1, source_target_pairs={{0,16},{8,24},{16,0},{24,8},{1,17},{9,25},{17,1},{25,9},{2,18},{10... | collective-permute-start | bytes 147464 | tf_op jit(solution)/shard_map/ppermute | solution.py:69
  97.4 1.9 %collective-permute-done.38.refs_2_ = f32[96,128]{1,0:T(8,128)S(1)} collective-permute-done((f32[96,128]{1,0:T(8,128)S(1)}, f32[96,128]{1,0:T(8,128)S(1)}, u32[]{:S(2)}, u32[]{:S(2)}) %collective-permute-start.38) | collective-permute-done | bytes 49184 | tf_op jit(solution)/shard_map/ppermute | solution.py:69
  99.3 2.4 %collective-permute-done.39.refs_3_ = f32[96,128]{1,0:T(8,128)S(1)} collective-permute-done((f32[96,128]{1,0:T(8,128)S(1)}, f32[96,128]{1,0:T(8,128)S(1)}, u32[]{:S(2)}, u32[]{:S(2)}) %collective-permute-start.39) | collective-permute-done | bytes 49184 | tf_op jit(solution)/shard_map/ppermute | solution.py:69
  106.3 1.9 %collective-permute-start.43 = (f32[192,128]{1,0:T(8,128)S(1)}, f32[192,128]{1,0:T(8,128)S(1)}, u32[]{:S(2)}, u32[]{:S(2)}) collective-permute-start(f32[192,128]{1,0:T(8,128)S(1)} %get-tuple-element.103), channel_id=1, source_target_pairs={{0,2},{1,3},{2,4},{3,5},{4,6},{5,7},{6,0},{7,1},{8,10},{9,11},{10,... | collective-permute-start | bytes 294920 | tf_op jit(solution)/shard_map/ppermute | solution.py:69
  108.2 2.9 %collective-permute-start.27 = (f32[24,128]{1,0:T(8,128)S(1)}, f32[24,128]{1,0:T(8,128)S(1)}, u32[]{:S(2)}, u32[]{:S(2)}) collective-permute-start(f32[24,128]{1,0:T(8,128)S(1)} %get-tuple-element.87), channel_id=1, source_target_pairs={{0,24},{8,0},{16,8},{24,16},{1,25},{9,1},{17,9},{25,17},{2,26},{10... | collective-permute-start | bytes 36872 | tf_op jit(solution)/shard_map/ppermute | solution.py:69
  111.1 1.7 %collective-permute-done.26.up = f32[24,128]{1,0:T(8,128)S(1)} collective-permute-done((f32[24,128]{1,0:T(8,128)S(1)}, f32[24,128]{1,0:T(8,128)S(1)}, u32[]{:S(2)}, u32[]{:S(2)}) %collective-permute-start.26) | collective-permute-done | bytes 12320 | tf_op jit(solution)/shard_map/ppermute | solution.py:69
  114.5 3.5 %collective-permute-done.28.lf = f32[8,768]{1,0:T(8,128)S(1)} collective-permute-done((f32[8,768]{1,0:T(8,128)S(1)}, f32[8,768]{1,0:T(8,128)S(1)}, u32[]{:S(2)}, u32[]{:S(2)}) %collective-permute-start.28) | collective-permute-done | bytes 24608 | tf_op jit(solution)/shard_map/ppermute | solution.py:69
  (101 shorter events, 39.3 us)
Async XLA Ops:
  2.2 9.7 %collective-permute-start.3 = (f32[8,768]{1,0:T(8,128)S(1)}, f32[8,768]{1,0:T(8,128)S(1)}, u32[]{:S(2)}, u32[]{:S(2)}) collective-permute-start(f32[8,768]{1,0:T(8,128)S(1)} %get-tuple-element.56), channel_id=1, source_target_pairs={{0,7},{1,0},{2,1},{3,2},{4,3},{5,4},{6,5},{7,6},{8,15},{9,8},{10,9... | collective-permute-start | bytes 73736 | tf_op jit(solution)/shard_map/ppermute | solution.py:69
  6.7 5.2 %collective-permute-start.2 = (f32[8,768]{1,0:T(8,128)S(1)}, f32[8,768]{1,0:T(8,128)S(1)}, u32[]{:S(2)}, u32[]{:S(2)}) collective-permute-start(f32[8,768]{1,0:T(8,128)S(1)} %get-tuple-element.56), channel_id=1, source_target_pairs={{0,1},{1,2},{2,3},{3,4},{4,5},{5,6},{6,7},{7,0},{8,9},{9,10},{10,1... | collective-permute-start | bytes 73736 | tf_op jit(solution)/shard_map/ppermute | solution.py:69
  6.7 4.6 %collective-permute-start = (f32[24,128]{1,0:T(8,128)S(1)}, f32[24,128]{1,0:T(8,128)S(1)}, u32[]{:S(2)}, u32[]{:S(2)}) collective-permute-start(f32[24,128]{1,0:T(8,128)S(1)} %get-tuple-element.54), channel_id=1, source_target_pairs={{0,8},{8,16},{16,24},{24,0},{1,9},{9,17},{17,25},{25,1},{2,10},{10... | collective-permute-start | bytes 36872 | tf_op jit(solution)/shard_map/ppermute | solution.py:69
  16.0 4.6 %collective-permute-start.10 = (f32[192,128]{1,0:T(8,128)S(1)}, f32[192,128]{1,0:T(8,128)S(1)}, u32[]{:S(2)}, u32[]{:S(2)}) collective-permute-start(f32[192,128]{1,0:T(8,128)S(1)} %get-tuple-element.61.refs_0_), channel_id=1, source_target_pairs={{0,6},{1,7},{2,0},{3,1},{4,2},{5,3},{6,4},{7,5},{8,14},{9,15},{10,... | collective-permute-start | bytes 294920 | tf_op jit(solution)/shard_map/ppermute | solution.py:69
  17.1 10.5 %collective-permute-start.9 = (f32[192,128]{1,0:T(8,128)S(1)}, f32[192,128]{1,0:T(8,128)S(1)}, u32[]{:S(2)}, u32[]{:S(2)}) collective-permute-start(f32[192,128]{1,0:T(8,128)S(1)} %get-tuple-element.61.refs_0_), channel_id=1, source_target_pairs={{0,4},{1,5},{2,6},{3,7},{4,0},{5,1},{6,2},{7,3},{8,12},{9,13},{10,... | collective-permute-start | bytes 294920 | tf_op jit(solution)/shard_map/ppermute | solution.py:69
  17.1 10.5 %collective-permute-start.8 = (f32[192,128]{1,0:T(8,128)S(1)}, f32[192,128]{1,0:T(8,128)S(1)}, u32[]{:S(2)}, u32[]{:S(2)}) collective-permute-start(f32[192,128]{1,0:T(8,128)S(1)} %get-tuple-element.61.refs_0_), channel_id=1, source_target_pairs={{0,2},{1,3},{2,4},{3,5},{4,6},{5,7},{6,0},{7,1},{8,10},{9,11},{10,... | collective-permute-start | bytes 294920 | tf_op jit(solution)/shard_map/ppermute | solution.py:69
  29.6 5.3 %collective-permute-start.12 = (f32[96,128]{1,0:T(8,128)S(1)}, f32[96,128]{1,0:T(8,128)S(1)}, u32[]{:S(2)}, u32[]{:S(2)}) collective-permute-start(f32[96,128]{1,0:T(8,128)S(1)} %get-tuple-element.67), channel_id=1, source_target_pairs={{0,8},{8,16},{16,24},{24,0},{1,9},{9,17},{17,25},{25,1},{2,10},{10... | collective-permute-start | bytes 147464 | tf_op jit(solution)/shard_map/ppermute | solution.py:69
  32.1 4.1 %collective-permute-start.13 = (f32[96,128]{1,0:T(8,128)S(1)}, f32[96,128]{1,0:T(8,128)S(1)}, u32[]{:S(2)}, u32[]{:S(2)}) collective-permute-start(f32[96,128]{1,0:T(8,128)S(1)} %get-tuple-element.68), channel_id=1, source_target_pairs={{0,16},{8,24},{16,0},{24,8},{1,17},{9,25},{17,1},{25,9},{2,18},{10... | collective-permute-start | bytes 147464 | tf_op jit(solution)/shard_map/ppermute | solution.py:69
  37.6 4.3 %collective-permute-start.15 = (f32[96,128]{1,0:T(8,128)S(1)}, f32[96,128]{1,0:T(8,128)S(1)}, u32[]{:S(2)}, u32[]{:S(2)}) collective-permute-start(f32[96,128]{1,0:T(8,128)S(1)} %get-tuple-element.74), channel_id=1, source_target_pairs={{0,24},{8,0},{16,8},{24,16},{1,25},{9,1},{17,9},{25,17},{2,26},{10... | collective-permute-start | bytes 147464 | tf_op jit(solution)/shard_map/ppermute | solution.py:69
  40.6 5.0 %collective-permute-start.17 = (f32[96,128]{1,0:T(8,128)S(1)}, f32[96,128]{1,0:T(8,128)S(1)}, u32[]{:S(2)}, u32[]{:S(2)}) collective-permute-start(f32[96,128]{1,0:T(8,128)S(1)} %get-tuple-element.76), channel_id=1, source_target_pairs={{0,8},{8,16},{16,24},{24,0},{1,9},{9,17},{17,25},{25,1},{2,10},{10... | collective-permute-start | bytes 147464 | tf_op jit(solution)/shard_map/ppermute | solution.py:69
  47.6 15.3 %collective-permute-start.19 = (f32[192,128]{1,0:T(8,128)S(1)}, f32[192,128]{1,0:T(8,128)S(1)}, u32[]{:S(2)}, u32[]{:S(2)}) collective-permute-start(f32[192,128]{1,0:T(8,128)S(1)} %get-tuple-element.78), channel_id=1, source_target_pairs={{0,6},{1,7},{2,0},{3,1},{4,2},{5,3},{6,4},{7,5},{8,14},{9,15},{10,... | collective-permute-start | bytes 294920 | tf_op jit(solution)/shard_map/ppermute | solution.py:69
  48.4 14.4 %collective-permute-start.20 = (f32[192,128]{1,0:T(8,128)S(1)}, f32[192,128]{1,0:T(8,128)S(1)}, u32[]{:S(2)}, u32[]{:S(2)}) collective-permute-start(f32[192,128]{1,0:T(8,128)S(1)} %get-tuple-element.79), channel_id=1, source_target_pairs={{0,4},{1,5},{2,6},{3,7},{4,0},{5,1},{6,2},{7,3},{8,12},{9,13},{10,... | collective-permute-start | bytes 294920 | tf_op jit(solution)/shard_map/ppermute | solution.py:69
  49.7 13.2 %collective-permute-start.21 = (f32[192,128]{1,0:T(8,128)S(1)}, f32[192,128]{1,0:T(8,128)S(1)}, u32[]{:S(2)}, u32[]{:S(2)}) collective-permute-start(f32[192,128]{1,0:T(8,128)S(1)} %get-tuple-element.80), channel_id=1, source_target_pairs={{0,2},{1,3},{2,4},{3,5},{4,6},{5,7},{6,0},{7,1},{8,10},{9,11},{10,... | collective-permute-start | bytes 294920 | tf_op jit(solution)/shard_map/ppermute | solution.py:69
  51.6 4.6 %collective-permute-start.4 = (f32[24,128]{1,0:T(8,128)S(1)}, f32[24,128]{1,0:T(8,128)S(1)}, u32[]{:S(2)}, u32[]{:S(2)}) collective-permute-start(f32[24,128]{1,0:T(8,128)S(1)} %get-tuple-element.58), channel_id=1, source_target_pairs={{0,8},{8,16},{16,24},{24,0},{1,9},{9,17},{17,25},{25,1},{2,10},{10... | collective-permute-start | bytes 36872 | tf_op jit(solution)/shard_map/ppermute | solution.py:69
  51.6 4.8 %collective-permute-start.5 = (f32[24,128]{1,0:T(8,128)S(1)}, f32[24,128]{1,0:T(8,128)S(1)}, u32[]{:S(2)}, u32[]{:S(2)}) collective-permute-start(f32[24,128]{1,0:T(8,128)S(1)} %get-tuple-element.59), channel_id=1, source_target_pairs={{0,24},{8,0},{16,8},{24,16},{1,25},{9,1},{17,9},{25,17},{2,26},{10... | collective-permute-start | bytes 36872 | tf_op jit(solution)/shard_map/ppermute | solution.py:69
  56.4 5.1 %collective-permute-start.6 = (f32[8,768]{1,0:T(8,128)S(1)}, f32[8,768]{1,0:T(8,128)S(1)}, u32[]{:S(2)}, u32[]{:S(2)}) collective-permute-start(f32[8,768]{1,0:T(8,128)S(1)} %get-tuple-element.60), channel_id=1, source_target_pairs={{0,1},{1,2},{2,3},{3,4},{4,5},{5,6},{6,7},{7,0},{8,9},{9,10},{10,1... | collective-permute-start | bytes 73736 | tf_op jit(solution)/shard_map/ppermute | solution.py:69
  63.4 7.0 %collective-permute-start.25 = (f32[8,768]{1,0:T(8,128)S(1)}, f32[8,768]{1,0:T(8,128)S(1)}, u32[]{:S(2)}, u32[]{:S(2)}) collective-permute-start(f32[8,768]{1,0:T(8,128)S(1)} %get-tuple-element.84), channel_id=1, source_target_pairs={{0,7},{1,0},{2,1},{3,2},{4,3},{5,4},{6,5},{7,6},{8,15},{9,8},{10,9... | collective-permute-start | bytes 73736 | tf_op jit(solution)/shard_map/ppermute | solution.py:69
  63.4 7.0 %collective-permute-start.24 = (f32[8,768]{1,0:T(8,128)S(1)}, f32[8,768]{1,0:T(8,128)S(1)}, u32[]{:S(2)}, u32[]{:S(2)}) collective-permute-start(f32[8,768]{1,0:T(8,128)S(1)} %get-tuple-element.84), channel_id=1, source_target_pairs={{0,1},{1,2},{2,3},{3,4},{4,5},{5,6},{6,7},{7,0},{8,9},{9,10},{10,1... | collective-permute-start | bytes 73736 | tf_op jit(solution)/shard_map/ppermute | solution.py:69
  63.9 4.6 %collective-permute-start.22 = (f32[24,128]{1,0:T(8,128)S(1)}, f32[24,128]{1,0:T(8,128)S(1)}, u32[]{:S(2)}, u32[]{:S(2)}) collective-permute-start(f32[24,128]{1,0:T(8,128)S(1)} %get-tuple-element.82), channel_id=1, source_target_pairs={{0,8},{8,16},{16,24},{24,0},{1,9},{9,17},{17,25},{25,1},{2,10},{10... | collective-permute-start | bytes 36872 | tf_op jit(solution)/shard_map/ppermute | solution.py:69
  72.7 4.6 %collective-permute-start.32 = (f32[192,128]{1,0:T(8,128)S(1)}, f32[192,128]{1,0:T(8,128)S(1)}, u32[]{:S(2)}, u32[]{:S(2)}) collective-permute-start(f32[192,128]{1,0:T(8,128)S(1)} %get-tuple-element.89.refs_0_), channel_id=1, source_target_pairs={{0,6},{1,7},{2,0},{3,1},{4,2},{5,3},{6,4},{7,5},{8,14},{9,15},{10,... | collective-permute-start | bytes 294920 | tf_op jit(solution)/shard_map/ppermute | solution.py:69
  72.8 10.4 %collective-permute-start.31 = (f32[192,128]{1,0:T(8,128)S(1)}, f32[192,128]{1,0:T(8,128)S(1)}, u32[]{:S(2)}, u32[]{:S(2)}) collective-permute-start(f32[192,128]{1,0:T(8,128)S(1)} %get-tuple-element.89.refs_0_), channel_id=1, source_target_pairs={{0,4},{1,5},{2,6},{3,7},{4,0},{5,1},{6,2},{7,3},{8,12},{9,13},{10,... | collective-permute-start | bytes 294920 | tf_op jit(solution)/shard_map/ppermute | solution.py:69
  72.8 10.4 %collective-permute-start.30 = (f32[192,128]{1,0:T(8,128)S(1)}, f32[192,128]{1,0:T(8,128)S(1)}, u32[]{:S(2)}, u32[]{:S(2)}) collective-permute-start(f32[192,128]{1,0:T(8,128)S(1)} %get-tuple-element.89.refs_0_), channel_id=1, source_target_pairs={{0,2},{1,3},{2,4},{3,5},{4,6},{5,7},{6,0},{7,1},{8,10},{9,11},{10,... | collective-permute-start | bytes 294920 | tf_op jit(solution)/shard_map/ppermute | solution.py:69
  85.2 5.2 %collective-permute-start.34 = (f32[96,128]{1,0:T(8,128)S(1)}, f32[96,128]{1,0:T(8,128)S(1)}, u32[]{:S(2)}, u32[]{:S(2)}) collective-permute-start(f32[96,128]{1,0:T(8,128)S(1)} %get-tuple-element.91), channel_id=1, source_target_pairs={{0,8},{8,16},{16,24},{24,0},{1,9},{9,17},{17,25},{25,1},{2,10},{10... | collective-permute-start | bytes 147464 | tf_op jit(solution)/shard_map/ppermute | solution.py:69
  86.5 4.5 %collective-permute-start.35 = (f32[96,128]{1,0:T(8,128)S(1)}, f32[96,128]{1,0:T(8,128)S(1)}, u32[]{:S(2)}, u32[]{:S(2)}) collective-permute-start(f32[96,128]{1,0:T(8,128)S(1)} %get-tuple-element.92), channel_id=1, source_target_pairs={{0,16},{8,24},{16,0},{24,8},{1,17},{9,25},{17,1},{25,9},{2,18},{10... | collective-permute-start | bytes 147464 | tf_op jit(solution)/shard_map/ppermute | solution.py:69
  92.7 4.7 %collective-permute-start.37 = (f32[96,128]{1,0:T(8,128)S(1)}, f32[96,128]{1,0:T(8,128)S(1)}, u32[]{:S(2)}, u32[]{:S(2)}) collective-permute-start(f32[96,128]{1,0:T(8,128)S(1)} %get-tuple-element.97), channel_id=1, source_target_pairs={{0,24},{8,0},{16,8},{24,16},{1,25},{9,1},{17,9},{25,17},{2,26},{10... | collective-permute-start | bytes 147464 | tf_op jit(solution)/shard_map/ppermute | solution.py:69
  96.7 5.0 %collective-permute-start.39 = (f32[96,128]{1,0:T(8,128)S(1)}, f32[96,128]{1,0:T(8,128)S(1)}, u32[]{:S(2)}, u32[]{:S(2)}) collective-permute-start(f32[96,128]{1,0:T(8,128)S(1)} %get-tuple-element.99), channel_id=1, source_target_pairs={{0,8},{8,16},{16,24},{24,0},{1,9},{9,17},{17,25},{25,1},{2,10},{10... | collective-permute-start | bytes 147464 | tf_op jit(solution)/shard_map/ppermute | solution.py:69
  103.7 15.8 %collective-permute-start.41 = (f32[192,128]{1,0:T(8,128)S(1)}, f32[192,128]{1,0:T(8,128)S(1)}, u32[]{:S(2)}, u32[]{:S(2)}) collective-permute-start(f32[192,128]{1,0:T(8,128)S(1)} %get-tuple-element.101), channel_id=1, source_target_pairs={{0,6},{1,7},{2,0},{3,1},{4,2},{5,3},{6,4},{7,5},{8,14},{9,15},{10,... | collective-permute-start | bytes 294920 | tf_op jit(solution)/shard_map/ppermute | solution.py:69
  105.0 14.4 %collective-permute-start.42 = (f32[192,128]{1,0:T(8,128)S(1)}, f32[192,128]{1,0:T(8,128)S(1)}, u32[]{:S(2)}, u32[]{:S(2)}) collective-permute-start(f32[192,128]{1,0:T(8,128)S(1)} %get-tuple-element.102), channel_id=1, source_target_pairs={{0,4},{1,5},{2,6},{3,7},{4,0},{5,1},{6,2},{7,3},{8,12},{9,13},{10,... | collective-permute-start | bytes 294920 | tf_op jit(solution)/shard_map/ppermute | solution.py:69
  106.3 13.2 %collective-permute-start.43 = (f32[192,128]{1,0:T(8,128)S(1)}, f32[192,128]{1,0:T(8,128)S(1)}, u32[]{:S(2)}, u32[]{:S(2)}) collective-permute-start(f32[192,128]{1,0:T(8,128)S(1)} %get-tuple-element.103), channel_id=1, source_target_pairs={{0,2},{1,3},{2,4},{3,5},{4,6},{5,7},{6,0},{7,1},{8,10},{9,11},{10,... | collective-permute-start | bytes 294920 | tf_op jit(solution)/shard_map/ppermute | solution.py:69
  108.2 4.6 %collective-permute-start.26 = (f32[24,128]{1,0:T(8,128)S(1)}, f32[24,128]{1,0:T(8,128)S(1)}, u32[]{:S(2)}, u32[]{:S(2)}) collective-permute-start(f32[24,128]{1,0:T(8,128)S(1)} %get-tuple-element.86), channel_id=1, source_target_pairs={{0,8},{8,16},{16,24},{24,0},{1,9},{9,17},{17,25},{25,1},{2,10},{10... | collective-permute-start | bytes 36872 | tf_op jit(solution)/shard_map/ppermute | solution.py:69
  108.2 4.8 %collective-permute-start.27 = (f32[24,128]{1,0:T(8,128)S(1)}, f32[24,128]{1,0:T(8,128)S(1)}, u32[]{:S(2)}, u32[]{:S(2)}) collective-permute-start(f32[24,128]{1,0:T(8,128)S(1)} %get-tuple-element.87), channel_id=1, source_target_pairs={{0,24},{8,0},{16,8},{24,16},{1,25},{9,1},{17,9},{25,17},{2,26},{10... | collective-permute-start | bytes 36872 | tf_op jit(solution)/shard_map/ppermute | solution.py:69
  113.0 5.1 %collective-permute-start.28 = (f32[8,768]{1,0:T(8,128)S(1)}, f32[8,768]{1,0:T(8,128)S(1)}, u32[]{:S(2)}, u32[]{:S(2)}) collective-permute-start(f32[8,768]{1,0:T(8,128)S(1)} %get-tuple-element.88), channel_id=1, source_target_pairs={{0,1},{1,2},{2,3},{3,4},{4,5},{5,6},{6,7},{7,0},{8,9},{9,10},{10,1... | collective-permute-start | bytes 73736 | tf_op jit(solution)/shard_map/ppermute | solution.py:69
  (22 other events, 115.7 us)
where the time goes:
time: 121 us; the launch traced here: 120 us
  waiting for transfers between devices  51.7 us (43%)
  starting transfers between devices  46.7 us (39%)
  Pallas kernels  18 us (15%)
  local copies, waits for them, and re-layouts  3.07 us (3%)
    ppermute x40, waiting for transfers between devices, shift_perm(): lax.ppermute(x, axis, [(i, (i + shift) % count) for i in range(count)])  47.7 us
    ppermute x40, starting transfers between devices, shift_perm(): lax.ppermute(x, axis, [(i, (i + shift) % count) for i in range(count)])  46.2 us
    pallas_call x23, Pallas kernels, call(): pl.pallas_call(body, name=name, out_shape=[jax.ShapeDtypeStruct(s, d) for...  18 us
    ppermute x4, waiting for transfers between devices, partner_perm(): return lax.ppermute(x, 'col', [(i, i ^ 1) for i in range(count)])  3.94 us
    unnamed x20, local copies, waits for them, and re-layouts  3.06 us
  transfers between devices with their start and end apart: 44, of which 29 were waited for; matrix products, arithmetic and copies ran while one was open for 0% of the time, Pallas kernels for 6%

commit v1 on v0

--- a/solution.py
+++ b/solution.py
@@ -18,24 +18,29 @@
 NT = (((1,), (1,)), ((), ()))
 
 
-def call(body, name, outs, *args, scratch=(), alias=None, flops=0):
+def call(body, name, outs, *args, scratch=(), after=()):
     nbytes = sum(a.size * a.dtype.itemsize for a in args) + sum(
         math.prod(s) * jnp.dtype(d).itemsize for s, d in outs
     )
+    count = len(args)
+
+    def run(*refs):
+        body(*refs[:count], *refs[count + len(after) :])
+
     results = pl.pallas_call(
-        body,
+        run,
         name=name,
         out_shape=[jax.ShapeDtypeStruct(s, d) for s, d in outs],
         in_specs=[
             pl.BlockSpec(memory_space=pltpu.SMEM if a.dtype == jnp.int32 else pltpu.VMEM)
             for a in args
-        ],
+        ]
+        + [pl.BlockSpec(memory_space=pl.ANY) for _ in after],
         out_specs=[pl.BlockSpec(memory_space=pltpu.VMEM) for _ in outs],
         scratch_shapes=list(scratch),
-        input_output_aliases=alias or {},
         compiler_params=pltpu.CompilerParams(vmem_limit_bytes=VMEM_LIMIT),
-        cost_estimate=pl.CostEstimate(flops=flops, bytes_accessed=nbytes, transcendentals=0),
-    )(*args)
+        cost_estimate=pl.CostEstimate(flops=0, bytes_accessed=nbytes, transcendentals=0),
+    )(*args, *after)
     return list(results)
 
 
@@ -72,6 +77,10 @@
 def partner_perm(x):
     count = lax.axis_size("col")
     return lax.ppermute(x, "col", [(i, i ^ 1) for i in range(count)])
+
+
+def beyond(index, length):
+    return jnp.where(index < 2, index - 2, index - 2 + length)
 
 
 def tables(where, dims):
@@ -84,7 +93,7 @@
         angle = (phase & (modulus - 1)).astype(F32) * (2.0 * math.pi / modulus)
         return jnp.cos(angle), jnp.sin(angle)
 
-    def body(where_ref, oh, ol, ph, pl_, wh, wl):
+    def body(where_ref, oh, ol, ph, pl_, wh, wl, eo, ep, we):
         r, c = where_ref[0], where_ref[1]
 
         def put(hi_ref, lo_ref, index, value):
@@ -92,7 +101,7 @@
             hi_ref[index] = hi
             lo_ref[index] = lo
 
-        for flip, hi_ref, lo_ref in ((0, oh, ol), (1, ph, pl_)):
+        for flip, hi_ref, lo_ref, side_ref in ((0, oh, ol, eo), (1, ph, pl_, ep)):
             col = c ^ 1 if flip else c
             line = iota((nk, yb), 0)
             lane = iota((nk, yb), 1)
@@ -106,6 +115,12 @@
                 span = pl.ds(t * yb, yb)
                 put(hi_ref, lo_ref, (pl.ds(0, nk), span), base_cos * tc - base_sin * ts)
                 put(hi_ref, lo_ref, (pl.ds(nk, nk), span), -(base_sin * tc + base_cos * ts))
+            line, lane = iota((depth * 8, nk), 0), iota((depth * 8, nk), 1)
+            wave = ((lane // kyb + r) & (rows - 1)) * (cols * kyb) + col * kyb + lane % kyb
+            spot = ((c - 2 * (line // 8)) & (cols - 1)) * yb + beyond(line % 8, yb)
+            side_cos, side_sin = unit(wave * spot, ny)
+            side_ref[:, :nk] = side_cos * scale
+            side_ref[:, nk:] = -side_sin * scale
         base_cos, base_sin = unit(iota((xb, nx), 0) * iota((xb, nx), 1), nx)
         tall = max(8, rows)
         start = ((r - iota((tall, nx), 0)) & (rows - 1)) * xb
@@ -120,11 +135,18 @@
             put(wh, wl, (top, pl.ds(nx, nx)), -sin)
             put(wh, wl, (low, pl.ds(0, nx)), sin)
             put(wh, wl, (low, pl.ds(nx, nx)), cos)
+        line, lane = iota((rows * 8, nx), 0), iota((rows * 8, nx), 1)
+        spot = ((r - line // 8) & (rows - 1)) * xb + beyond(line % 4, xb)
+        cos, sin = unit(spot * lane, nx)
+        real = line % 8 < 4
+        we[:, :nx] = jnp.where(real, cos, sin) * scale
+        we[:, nx:] = jnp.where(real, -sin, cos) * scale
 
     y_shape, x_shape = (2 * nk, depth * yb), (2 * nx, 2 * nx)
     outs = [(y_shape, BF16)] * 4 + [(x_shape, BF16)] * 2
-    oh, ol, ph, pl_, wh, wl = call(body, "tables", outs, where)
-    return (oh, ol), (ph, pl_), (wh, wl)
+    outs += [((depth * 8, 2 * nk), F32)] * 2 + [((rows * 8, 2 * nx), F32)]
+    oh, ol, ph, pl_, wh, wl, eo, ep, we = call(body, "tables", outs, where)
+    return (oh, ol), (ph, pl_), (wh, wl), (eo, ep, we)
 
 
 def past_sums(kernel, history):
@@ -221,119 +243,257 @@
     return [((8, planes * xb), F32), ((2 * planes, yb), F32), ((2 * planes, yb), F32)]
 
 
+def row_patch(above, below, xb):
+    line, lane = iota((xb, 4), 0), iota((xb, 4), 1)
+    gap = beyond(lane, xb) - line
+    near = jnp.where(gap == 1, NEAR, 0.0) - jnp.where(gap == -1, NEAR, 0.0)
+    weights = near + jnp.where(gap == 2, FAR, 0.0) - jnp.where(gap == -2, FAR, 0.0)
+    total = weights[:, 0:1] * above[0:1] + weights[:, 1:2] * above[1:2]
+    return total + (weights[:, 2:3] * below[0:1] + weights[:, 3:4] * below[1:2])
+
+
+def plane_list(parts, layers):
+    return [(p, l) for p in parts for l in range(layers)]
+
+
 def first_borders(stress):
     _, layers, xb, yb = stress.shape
 
     def body(s_ref, *outs):
-        rows = [(p, l) for p in ROW_PARTS for l in range(layers)]
-        cols = [(p, l) for p in COL_PARTS for l in range(layers)]
+        rows, cols = plane_list(ROW_PARTS, layers), plane_list(COL_PARTS, layers)
         put_borders(lambda w: s_ref[w[0], w[1]], rows, cols, *outs)
 
     return call(body, "borders", borders_shapes(layers, xb, yb), stress)
+
+
+def exchange_edges(edge):
+    return shift_perm(edge, "col", 1), shift_perm(edge, "col", -1)
 
 
 def exchange(borders):
     edge, first, last = borders
     above = shift_perm(last, "row", 1)
     below = shift_perm(first, "row", -1)
-    left = shift_perm(edge, "col", 1)
-    right = shift_perm(edge, "col", -1)
-    return above, below, left, right
+    return (above, below, *exchange_edges(edge))
+
+
+DEPTH_PARTS = (4, 5, 2)
+
+
+def push_inner(velocity, stress, buoyancy):
+    comps, layers, xb, yb = velocity.shape
+
+    def body(v_ref, s_ref, b_ref, nv_ref, pad):
+        none = jnp.zeros((2, yb), F32)
+        stacked = jnp.concatenate(
+            [s_ref[p, l] for p, l in plane_list(COL_PARTS, layers)], axis=0
+        )
+        along_y = dot6(stacked, inner_weights(yb), NN)
+        for comp in range(comps):
+            for layer in range(layers):
+                j = comp * layers + layer
+                force = row_deriv(pad.at[j], s_ref[ROW_PARTS[comp], layer], none, none)
+                force = force + along_y[j * xb : (j + 1) * xb]
+                force = force + depth_deriv(lambda l: s_ref[DEPTH_PARTS[comp], l], layer, layers)
+                nv_ref[comp, layer] = v_ref[comp, layer] + b_ref[layer] * force
+
+    return call(
+        body, "push_inner", [(velocity.shape, F32)], velocity, stress, buoyancy,
+        scratch=[pltpu.VMEM((comps * layers, xb + 16, yb), F32)],
+    )[0]
+
+
+def push_top(inner, buoyancy, halo):
+    comps, layers, xb, yb = inner.shape
+
+    def body(v_ref, b_ref, up, dn, lf, rt, top_ref):
+        left_w, right_w = outer_weights(yb)
+        for comp in range(comps):
+            j = comp * layers
+            pair, lane = slice(2 * j, 2 * j + 2), slice(j * xb, (j + 1) * xb)
+            patch = row_patch(up[pair, :], dn[pair, :], xb)
+            patch = patch + dot6(lf[:, lane].T, left_w, NN) + dot6(rt[:, lane].T, right_w, NN)
+            top_ref[comp * xb : (comp + 1) * xb, :] = v_ref[comp, 0] + b_ref[0] * patch
+
+    return call(body, "push_top", [((comps * xb, yb), F32)], inner, buoyancy, *halo)[0]
+
+
+def push_rest(inner, buoyancy, halo, top):
+    comps, layers, xb, yb = inner.shape
+
+    def body(v_ref, b_ref, up, dn, lf, rt, top_ref, nv_ref, edge, first, last):
+        left_w, right_w = outer_weights(yb)
+        along_y = dot6(lf[...].T, left_w, NN) + dot6(rt[...].T, right_w, NN)
+        for comp in range(comps):
+            nv_ref[comp, 0] = top_ref[comp * xb : (comp + 1) * xb, :]
+            for layer in range(1, layers):
+                j = comp * layers + layer
+                pair = slice(2 * j, 2 * j + 2)
+                patch = row_patch(up[pair, :], dn[pair, :], xb) + along_y[j * xb : (j + 1) * xb]
+                nv_ref[comp, layer] = v_ref[comp, layer] + b_ref[layer] * patch
+        planes = plane_list(range(comps), layers)
+        put_borders(lambda w: nv_ref[w[0], w[1]], planes, planes, edge, first, last)
+
+    outs = [(inner.shape, F32)] + borders_shapes(layers, xb, yb)
+    new, *borders = call(body, "push_rest", outs, inner, buoyancy, *halo, top)
+    return new, borders
 
 
 def push_velocity(velocity, stress, buoyancy, halo):
     comps, layers, xb, yb = velocity.shape
 
-    def body(v_ref, s_ref, b_ref, up, dn, lf, rt, nv_ref, top_ref, edge, first, last, pad):
+    def body(v_ref, s_ref, b_ref, up, dn, lf, rt, nv_ref, top_ref, pad):
         stacked = jnp.concatenate(
-            [s_ref[p, l] for p in COL_PARTS for l in range(layers)], axis=0
+            [s_ref[p, l] for p, l in plane_list(COL_PARTS, layers)], axis=0
         )
         along_y = col_deriv(stacked, lf[...], rt[...])
-        depth_parts = (4, 5, 2)
         for comp in range(comps):
             for layer in range(layers):
                 j = comp * layers + layer
                 pair = slice(2 * j, 2 * j + 2)
                 force = row_deriv(pad.at[j], s_ref[ROW_PARTS[comp], layer], up[pair, :], dn[pair, :])
                 force = force + along_y[j * xb : (j + 1) * xb]
-                force = force + depth_deriv(lambda l: s_ref[depth_parts[comp], l], layer, layers)
+                force = force + depth_deriv(lambda l: s_ref[DEPTH_PARTS[comp], l], layer, layers)
                 new = v_ref[comp, layer] + b_ref[layer] * force
                 nv_ref[comp, layer] = new
-                if layer == 0:
+                if layer == 0 and comp < comps - 1:
                     top_ref[comp * xb : (comp + 1) * xb, :] = new
-        planes = [(c, l) for c in range(comps) for l in range(layers)]
-        put_borders(lambda w: nv_ref[w[0], w[1]], planes, planes, edge, first, last)
-
-    outs = [(velocity.shape, F32), ((comps * xb, yb), F32)] + borders_shapes(layers, xb, yb)
-    nv, top, *borders = call(
+
+    outs = [(velocity.shape, F32), (((comps - 1) * xb, yb), F32)]
+    return call(
         body, "push_velocity", outs, velocity, stress, buoyancy, *halo,
         scratch=[pltpu.VMEM((comps * layers, xb + 16, yb), F32)],
     )
-    return nv, top, borders
-
-
-def push_stress(stress, velocity, lame, shear, halo):
+
+
+def push_stress(stress, velocity, lame, shear, halo, traction=None):
     comps, layers, xb, yb = velocity.shape
 
-    def body(s_ref, v_ref, l_ref, m_ref, up, dn, lf, rt, ns_ref, pad):
+    def body(s_ref, v_ref, l_ref, m_ref, up, dn, lf, rt, *refs):
         stacked = jnp.concatenate(
-            [v_ref[c, l] for c in range(comps) for l in range(layers)], axis=0
+            [v_ref[c, l] for c, l in plane_list(range(comps), layers)], axis=0
         )
+        if traction is None:
+            ns_ref, *outs, pad = refs
+        else:
+            t_ref, ns_ref, pad = refs
         along_y = col_deriv(stacked, lf[...], rt[...])
+        skip = up.shape[0] - 2 * comps * layers
         for layer in range(layers):
             gx, gy, gz = [], [], []
             for comp in range(comps):
                 j = comp * layers + layer
-                pair = slice(2 * j, 2 * j + 2)
+                pair = slice(skip + 2 * j, skip + 2 * j + 2)
                 gx.append(row_deriv(pad.at[j], v_ref[comp, layer], up[pair, :], dn[pair, :]))
                 gy.append(along_y[j * xb : (j + 1) * xb])
                 gz.append(depth_deriv(lambda l: v_ref[comp, l], layer, layers))
             lam, mu = l_ref[layer], m_ref[layer]
             spread = lam * (gx[0] + gy[1] + gz[2])
             twice = 2.0 * mu
-            ns_ref[0, layer] = s_ref[0, layer] + spread + twice * gx[0]
-            ns_ref[1, layer] = s_ref[1, layer] + spread + twice * gy[1]
-            ns_ref[2, layer] = s_ref[2, layer] + spread + twice * gz[2]
-            ns_ref[3, layer] = s_ref[3, layer] + mu * (gy[0] + gx[1])
-            ns_ref[4, layer] = s_ref[4, layer] + mu * (gz[0] + gx[2])
-            ns_ref[5, layer] = s_ref[5, layer] + mu * (gz[1] + gy[2])
+            old = [s_ref[part, layer] for part in range(6)]
+            if traction is not None and layer == 0:
+                for comp, part in enumerate(DEPTH_PARTS):
+                    old[part] = old[part] + t_ref[comp * xb : (comp + 1) * xb, :]
+            ns_ref[0, layer] = old[0] + spread + twice * gx[0]
+            ns_ref[1, layer] = old[1] + spread + twice * gy[1]
+            ns_ref[2, layer] = old[2] + spread + twice * gz[2]
+            ns_ref[3, layer] = old[3] + mu * (gy[0] + gx[1])
+            ns_ref[4, layer] = old[4] + mu * (gz[0] + gx[2])
+            ns_ref[5, layer] = old[5] + mu * (gz[1] + gy[2])
+        if traction is None:
+            rows, cols = plane_list(ROW_PARTS, layers), plane_list(COL_PARTS, layers)
+            put_borders(lambda w: ns_ref[w[0], w[1]], rows, cols, *outs)
+
+    args = [stress, velocity, lame, shear, *halo] + ([] if traction is None else [traction])
+    outs = [(stress.shape, F32)] + (borders_shapes(layers, xb, yb) if traction is None else [])
+    new, *borders = call(
+        body, "push_stress", outs, *args,
+        scratch=[pltpu.VMEM((comps * layers, xb + 16, yb), F32)],
+    )
+    return new, borders
+
+
+def total_of(refs):
+    total = refs[0][...]
+    for ref in refs[1:]:
+        total = total + ref[...]
+    return total
+
+
+def top_after(pieces, velocity, buoyancy):
+    comps, layers, xb, yb = velocity.shape
+    height = pieces[0].shape[0]
+
+    def body(v_ref, b_ref, *refs):
+        *piece_refs, sum_ref, face_ref, pad = refs
+        total = total_of(piece_refs)
+        sum_ref[...] = total
+        main = comps * xb
+        force = row_deriv(pad, total[:xb], total[main : main + 2], total[main + 2 : main + 4])
+        side = total[main + 8 : main + 16, :xb].T
+        line, lane = iota((8, yb), 0), iota((8, yb), 1)
+        gap = jnp.where(line < 4, beyond(line, yb) - lane, 99)
+        near = jnp.where(gap == 1, NEAR, 0.0) - jnp.where(gap == -1, NEAR, 0.0)
+        outer = near + jnp.where(gap == 2, FAR, 0.0) - jnp.where(gap == -2, FAR, 0.0)
+        force = force + (dot6(total[xb : 2 * xb], inner_weights(yb), NN) + dot6(side, outer, NN))
+        face_ref[...] = v_ref[comps - 1, 0] + b_ref[0] * force
 
     return call(
-        body, "push_stress", [(stress.shape, F32)], stress, velocity, lame, shear, *halo,
-        scratch=[pltpu.VMEM((comps * layers, xb + 16, yb), F32)],
-    )[0]
-
-
-def add_traction(stress, pieces, with_borders):
-    _, layers, xb, yb = stress.shape
+        body, "top_after", [((height, yb), F32), ((xb, yb), F32)], velocity, buoyancy, *pieces,
+        scratch=[pltpu.VMEM((xb + 16, yb), F32)],
+    )
+
+
+def finish_velocity(velocity, buoyancy, traction, face):
+    comps, layers, xb, yb = velocity.shape
+
+    def body(v_ref, b_ref, t_ref, f_ref, nv_ref, edge, first, last):
+        for comp in range(comps):
+            push = t_ref[comp * xb : (comp + 1) * xb, :]
+            for layer in range(layers):
+                new = v_ref[comp, layer]
+                if layer == 0 and comp == comps - 1:
+                    new = f_ref[...]
+                if layer in (1, 2):
+                    weight = -NEAR if layer == 1 else -FAR
+                    new = new + b_ref[layer] * (weight * push)
+                nv_ref[comp, layer] = new
+        planes = plane_list(range(comps), layers)
+        put_borders(lambda w: nv_ref[w[0], w[1]], planes, planes, edge, first, last)
+
+    outs = [(velocity.shape, F32)] + borders_shapes(layers, xb, yb)
+    new, *borders = call(body, "finish_velocity", outs, velocity, buoyancy, traction, face)
+    return new, borders
+
+
+def add_traction(stress, pieces):
+    xb = stress.shape[2]
 
     def body(s_ref, *refs):
-        count = len(pieces)
-        ns_ref, *outs = refs[count:]
-        total = refs[0][...]
-        for ref in refs[1:count]:
-            total = total + ref[...]
+        *piece_refs, ns_ref = refs
+        total = total_of(piece_refs)
         ns_ref[...] = s_ref[...]
-        for comp, part in enumerate((4, 5, 2)):
+        for comp, part in enumerate(DEPTH_PARTS):
             ns_ref[part, 0] = s_ref[part, 0] + total[comp * xb : (comp + 1) * xb]
-        if with_borders:
-            rows = [(p, l) for p in ROW_PARTS for l in range(layers)]
-            cols = [(p, l) for p in COL_PARTS for l in range(layers)]
-            put_borders(lambda w: ns_ref[w[0], w[1]], rows, cols, *outs)
-
-    outs = [(stress.shape, F32)] + (borders_shapes(layers, xb, yb) if with_borders else [])
-    new, *borders = call(body, "traction", outs, stress, *pieces)
-    return new, borders
-
-
-def part_forward(blocks, table, dims, name):
+
+    return call(body, "traction", [(stress.shape, F32)], stress, *pieces)[0]
+
+
+def part_forward(groups, table, dims, name, after=()):
     rows, cols, xb, yb, kyb = dims
     nk = rows * kyb
-    comps = blocks[0].shape[0] // xb
+    comps = sum(blocks[0].shape[0] for blocks in groups) // xb
+    depth = cols // 2
 
     def body(*refs):
         hi, lo, out = refs[-3:]
-        data = jnp.concatenate([ref[...] for ref in refs[:-3]], axis=1)
+        data = jnp.concatenate(
+            [
+                jnp.concatenate([ref[...] for ref in refs[g * depth : (g + 1) * depth]], axis=1)
+                for g in range(len(groups))
+            ],
+            axis=0,
+        )
         total = dot3((hi[...], lo[...]), split(data), NT)
         for s in range(rows):
             for comp in range(comps):
@@ -343,32 +503,40 @@
                 at = (s * comps + comp) * kyb
                 out[at : at + kyb, :] = jnp.concatenate([real, imag], axis=1)
 
-    return call(body, name, [((rows * comps * kyb, 2 * xb), F32)], *blocks, *table)[0]
-
-
-def join(mine, other, dims):
+    blocks = [block for group in groups for block in group]
+    return call(body, name, [((rows * comps * kyb, 2 * xb), F32)], *blocks, *table, after=after)[0]
+
+
+def join(mine, other, first, last, dims, after):
     rows = dims[0]
-    height = mine.shape[0] // rows
-
-    def body(a_ref, b_ref, *outs):
+    height, extra = mine.shape[0] // rows, first.shape[0]
+    riders = {1: 1, rows - 1: 0}
+
+    def body(a_ref, b_ref, *refs):
+        borders, outs = refs[:2], refs[2:]
         for s, out in enumerate(outs):
             span = slice(s * height, (s + 1) * height)
-            out[...] = a_ref[span, :] + b_ref[span, :]
-
-    return call(body, "join", [((height, mine.shape[1]), F32)] * rows, mine, other)
-
-
-def convolve(blocks, table, past, kernel, before, dims):
+            out[:height, :] = a_ref[span, :] + b_ref[span, :]
+            if s in riders:
+                out[height:, :] = borders[riders[s]][...]
+
+    outs = [((height + (extra if s in riders else 0), mine.shape[1]), F32) for s in range(rows)]
+    return call(body, "join", outs, mine, other, first, last, after=after)
+
+
+def convolve(blocks, table, past, kernel, before, dims, side=None):
     rows, cols, xb, yb, kyb = dims
     nx = rows * xb
     comps = blocks[0].shape[0] // kyb
     step = len(before)
 
     def body(*refs):
+        if side is not None:
+            side_ref, *refs = refs
         ins, outs = refs[: rows + 4 + step], refs[rows + 4 + step :]
         wide = (ins[rows][...], ins[rows + 1][...])
         past_ref, k_ref, olds = ins[rows + 2], ins[rows + 3], ins[rows + 4 :]
-        data = jnp.concatenate([ref[...] for ref in ins[:rows]], axis=1)
+        data = jnp.concatenate([ref[: comps * kyb, :] for ref in ins[:rows]], axis=1)
         spec = dot3(split(data), wide, NN)
         spec_ref = outs[0]
         loads = []
@@ -391,50 +559,104 @@
                 imag = imag + (kr * si + ki * sr)
             loads.append(jnp.concatenate([real, imag], axis=1))
         back = dot3(split(jnp.concatenate(loads, axis=0)), wide, NT)
+        if side is not None:
+            halo = dot6(side_ref[...], loads[0], NT)
         for s, out in enumerate(outs[1:]):
-            out[...] = back[:, s * 2 * xb : (s + 1) * 2 * xb]
+            out[: comps * kyb, :] = back[:, s * 2 * xb : (s + 1) * 2 * xb]
+            if side is not None:
+                out[comps * kyb :, :] = jnp.zeros((8, 2 * xb), F32)
+                out[comps * kyb :, :kyb] = halo[8 * s : 8 * s + 8]
 
     one = (comps, 2, kyb, nx)
     spec_shape = (STEPS,) + one if step == STEPS - 1 else one
-    outs = [(spec_shape, F32)] + [((comps * kyb, 2 * xb), F32)] * rows
-    spec, *pieces = call(body, "convolve", outs, *blocks, *table, past, kernel, *before)
+    height = comps * kyb + (0 if side is None else 8)
+    outs = [(spec_shape, F32)] + [((height, 2 * xb), F32)] * rows
+    args = ([] if side is None else [side]) + [*blocks, *table, past, kernel, *before]
+    spec, *pieces = call(body, "convolve", outs, *args)
     return spec, pieces
 
 
-def turn(blocks, dims):
+def turn(blocks, dims, comps, after):
     rows, cols, xb, yb, kyb = dims
-    comps = blocks[0].shape[0] // kyb
+    main, wide = comps * xb, 2 * rows * kyb
+    sides = blocks[0].shape[0] > comps * kyb
 
     def body(*refs):
-        out = refs[-1]
+        *blocks, out = refs
         for comp in range(comps):
             line = slice(comp * kyb, (comp + 1) * kyb)
-            flat = jnp.concatenate([ref[line, :] for ref in refs[:-1]], axis=0).T
+            flat = jnp.concatenate([ref[line, :] for ref in blocks], axis=0).T
             out[comp * xb : (comp + 1) * xb, :] = jnp.concatenate([flat[:xb], flat[xb:]], axis=1)
-
-    return call(body, "turn", [((comps * xb, 2 * rows * kyb), F32)], *blocks)[0]
-
-
-def part_inverse(data, table, dims):
+        if sides:
+            low = comps * kyb
+            parts = [ref[low + 4 * p : low + 4 * p + 4, :kyb] for p in range(2) for ref in blocks]
+            out[main : main + 8, :] = jnp.zeros((8, wide), F32)
+            out[main : main + 4, :] = jnp.concatenate(parts, axis=1)
+
+    return call(body, "turn", [((main + (8 if sides else 0), wide), F32)], *blocks, after=after)[0]
+
+
+def y_inverse(d_ref, hi, lo, dims, side_ref):
+    xb, yb, depth = dims[2], dims[3], dims[1] // 2
+    total = dot3(split(d_ref[...]), (hi[...], lo[...]), NN)
+    if side_ref is None:
+        return total
+    beside = dot6(side_ref[...], d_ref[xb : 2 * xb, :], NT)
+    gap = jnp.zeros((8, yb - xb), F32)
+    parts = [jnp.concatenate([beside[8 * t : 8 * t + 8], gap], axis=1) for t in range(depth)]
+    return jnp.concatenate([total, jnp.concatenate(parts, axis=1)], axis=0)
+
+
+def part_inverse(data, table, dims, side=None):
+    def body(d_ref, hi, lo, *refs):
+        out = refs[-1]
+        out[...] = y_inverse(d_ref, hi, lo, dims, refs[0] if side is not None else None)
+
+    shape = (data.shape[0] + (0 if side is None else 8), dims[1] // 2 * dims[3])
+    extra = [] if side is None else [side]
+    return call(body, "inverse_mine", [(shape, F32)], data, *table, *extra)[0]
+
+
+def rest_inverse(mine, data, table, dims, side=None):
     cols, yb = dims[1], dims[3]
 
-    def body(d_ref, hi, lo, out):
-        out[...] = dot3(split(d_ref[...]), (hi[...], lo[...]), NN)
-
-    shape = (data.shape[0], cols // 2 * yb)
-    return call(body, "inverse_mine", [(shape, F32)], data, *table)[0]
-
-
-def rest_inverse(mine, data, table, dims):
-    cols, yb = dims[1], dims[3]
-
-    def body(m_ref, d_ref, hi, lo, *outs):
-        total = m_ref[...] + dot3(split(d_ref[...]), (hi[...], lo[...]), NN)
+    def body(m_ref, d_ref, hi, lo, *refs):
+        side_ref, outs = (None, refs) if side is None else (refs[0], refs[1:])
+        total = m_ref[...] + y_inverse(d_ref, hi, lo, dims, side_ref)
         for t, out in enumerate(outs):
             out[...] = total[:, t * yb : (t + 1) * yb]
 
-    outs = [((data.shape[0], yb), F32)] * (cols // 2)
-    return call(body, "inverse_other", outs, mine, data, *table)
+    outs = [((mine.shape[0], yb), F32)] * (cols // 2)
+    extra = [] if side is None else [side]
+    return call(body, "inverse_other", outs, mine, data, *table, *extra)
+
+
+def gather_depth(block):
+    count = lax.axis_size("col") // 2
+    return [block] + [shift_perm(block, "col", 2 * t) for t in range(1, count)]
+
+
+def forward(groups, borders, tables_, dims):
+    mine, other = tables_[:2]
+    edge, first, last = borders
+    sent = part_forward(groups, other, dims, "forward_other", after=(first,))
+    came = partner_perm(sent)
+    kept = part_forward(groups, mine, dims, "forward_mine")
+    beside = exchange_edges(edge)
+    pieces = join(kept, came, first, last, dims, beside)
+    pieces = pieces[:1] + [shift_perm(pieces[s], "row", s) for s in range(1, dims[0])]
+    return pieces, (pieces[1], pieces[-1], *beside)
+
+
+def inverse(pieces, tables_, dims, comps, last, token):
+    mine, other, _, (side_mine, side_other, _) = tables_
+    rows, cols = dims[:2]
+    pieces = pieces[:1] + [shift_perm(pieces[s], "row", -s) for s in range(1, rows)]
+    flat = turn(pieces, dims, comps, (token,))
+    flat_other = partner_perm(flat)
+    total = part_inverse(flat, mine, dims, None if last else side_mine)
+    pieces = rest_inverse(total, flat_other, other, dims, None if last else side_other)
+    return pieces[:1] + [shift_perm(pieces[t], "col", -2 * t) for t in range(1, cols // 2)]
 
 
 def on_device(velocity, stress, buoyancy, lame, shear, kernel, history):
@@ -445,30 +667,33 @@
     where = jnp.stack([lax.axis_index("row"), lax.axis_index("col")]).astype(jnp.int32)
 
     halo = exchange(first_borders(stress))
-    mine, other, wide = tables(where, dims)
+    inner = push_inner(velocity, stress, buoyancy)
+    top = push_top(inner, buoyancy, halo)
+    faces = gather_depth(top)
+    tables_ = tables(where, dims)
     past = past_sums(kernel, history)
     recent = kernel[:STEPS]
+    velocity, borders = push_rest(inner, buoyancy, halo, top)
     spectra = []
+    groups = [faces]
+    traction = None
     for step in range(STEPS):
-        velocity, top, borders = push_velocity(velocity, stress, buoyancy, halo)
-        blocks = [top] + [shift_perm(top, "col", 2 * t) for t in range(1, cols // 2)]
-        sent = part_forward(blocks, other, dims, "forward_other")
-        came = partner_perm(sent)
-        kept = part_forward(blocks, mine, dims, "forward_mine")
-        pieces = join(kept, came, dims)
-        pieces = pieces[:1] + [shift_perm(pieces[s], "row", s) for s in range(1, rows)]
-        spec, pieces = convolve(pieces, wide, past[step], recent, spectra, dims)
+        last = step == STEPS - 1
+        pieces, halo = forward(groups, borders, tables_, dims)
+        side = None if last else tables_[3][2]
+        spec, pieces = convolve(pieces, tables_[2], past[step], recent, spectra, dims, side)
         spectra.append(spec)
-        pieces = pieces[:1] + [shift_perm(pieces[s], "row", -s) for s in range(1, rows)]
-        flat = turn(pieces, dims)
-        flat_other = partner_perm(flat)
-        total = part_inverse(flat, mine, dims)
-        pieces = rest_inverse(total, flat_other, other, dims)
-        pieces = pieces[:1] + [shift_perm(pieces[t], "col", -2 * t) for t in range(1, cols // 2)]
-        stress = push_stress(stress, velocity, lame, shear, exchange(borders))
-        stress, borders = add_traction(stress, pieces, step < STEPS - 1)
-        if step < STEPS - 1:
-            halo = exchange(borders)
+        stress, next_borders = push_stress(stress, velocity, lame, shear, halo, traction)
+        token = stress if last else next_borders[1]
+        pieces = inverse(pieces, tables_, dims, recent.shape[1], last, token)
+        if last:
+            break
+        velocity, early = push_velocity(velocity, stress, buoyancy, exchange(next_borders))
+        groups = [gather_depth(early)]
+        traction, face = top_after(pieces, velocity, buoyancy)
+        groups.append(gather_depth(face))
+        velocity, borders = finish_velocity(velocity, buoyancy, traction, face)
+    stress = add_traction(stress, pieces)
     return (velocity, stress, spectra[-1])
 
 

time: 121 us -> 108 us (0.89)
  waiting for transfers between devices: 51.7 us -> 29.2 us
  starting transfers between devices: 46.7 us -> 54.7 us
  Pallas kernels: 18 us -> 19.6 us
    ppermute x40 -> x39, waiting for transfers between devices: 47.7 us -> 27 us  [shift_perm(): lax.ppermute(x, axis, [(i, (i + shift) % count) for i in range(count)])]
    ppermute x40 -> x39, starting transfers between devices: 46.2 us -> 54.3 us  [shift_perm(): lax.ppermute(x, axis, [(i, (i + shift) % count) for i in range(count)])]
    ppermute x4, waiting for transfers between devices: 3.94 us -> 2.15 us  [partner_perm(): return lax.ppermute(x, 'col', [(i, i ^ 1) for i in range(count)])]
    pallas_call x23 -> x26, Pallas kernels: 18 us -> 19.6 us  [call(): pl.pallas_call(run, name=name, out_shape=[jax.ShapeDtypeStruct(s, d) for...]
  transfers between devices with their start and end apart: 44 -> 43, of which waited for: 29 -> 19; matrix products, arithmetic and copies ran while one was open for 0% -> 0% of each run, Pallas kernels for 6% -> 12%
where the time goes in v1:
time: 108 us
  starting transfers between devices  54.7 us (51%)
  waiting for transfers between devices  29.2 us (27%)
  Pallas kernels  19.6 us (18%)
  local copies, waits for them, and re-layouts  3.14 us (3%)
    ppermute x39, starting transfers between devices, shift_perm(): lax.ppermute(x, axis, [(i, (i + shift) % count) for i in range(count)])  54.3 us
    ppermute x39, waiting for transfers between devices, shift_perm(): lax.ppermute(x, axis, [(i, (i + shift) % count) for i in range(count)])  27 us
    pallas_call x26, Pallas kernels, call(): pl.pallas_call(run, name=name, out_shape=[jax.ShapeDtypeStruct(s, d) for...  19.6 us
    unnamed x20, local copies, waits for them, and re-layouts  3.13 us
  transfers between devices with their start and end apart: 43, of which 19 were waited for; matrix products, arithmetic and copies ran while one was open for 0% of the time, Pallas kernels for 12%

profile of v1, /device:TPU:0, one launch (start us, length us, event | category | flops | bytes accessed | tf_op | source)
XLA Modules:
  0.0 107.6 jit_solution(12970857457153797488)
XLA Ops:
  2.7 4.0 %collective-permute-start.3 = (f32[8,768]{1,0:T(8,128)S(1)}, f32[8,768]{1,0:T(8,128)S(1)}, u32[]{:S(2)}, u32[]{:S(2)}) collective-permute-start(f32[8,768]{1,0:T(8,128)S(1)} %get-tuple-element.61), channel_id=1, source_target_pairs={{0,7},{1,0},{2,1},{3,2},{4,3},{5,4},{6,5},{7,6},{8,15},{9,8},{10,9... | collective-permute-start | bytes 73736 | tf_op jit(solution)/shard_map/ppermute | solution.py:74
  6.7 2.0 %collective-permute-start = (f32[24,128]{1,0:T(8,128)S(1)}, f32[24,128]{1,0:T(8,128)S(1)}, u32[]{:S(2)}, u32[]{:S(2)}) collective-permute-start(f32[24,128]{1,0:T(8,128)S(1)} %get-tuple-element.59), channel_id=1, source_target_pairs={{0,8},{8,16},{16,24},{24,0},{1,9},{9,17},{17,25},{25,1},{2,10},{10... | collective-permute-start | bytes 36872 | tf_op jit(solution)/shard_map/ppermute | solution.py:74
  13.2 2.6 %collective-permute-start.5 = (f32[192,128]{1,0:T(8,128)S(1)}, f32[192,128]{1,0:T(8,128)S(1)}, u32[]{:S(2)}, u32[]{:S(2)}) collective-permute-start(f32[192,128]{1,0:T(8,128)S(1)} %push_top.1.refs_6_.refs_0_), channel_id=1, source_target_pairs={{0,4},{1,5},{2,6},{3,7},{4,0},{5,1},{6,2},{7,3},{8,12},{9,13},{10,... | collective-permute-start | bytes 294920 | tf_op jit(solution)/shard_map/ppermute | solution.py:74
  15.8 1.3 %collective-permute-start.6 = (f32[192,128]{1,0:T(8,128)S(1)}, f32[192,128]{1,0:T(8,128)S(1)}, u32[]{:S(2)}, u32[]{:S(2)}) collective-permute-start(f32[192,128]{1,0:T(8,128)S(1)} %push_top.1.refs_6_.refs_0_), channel_id=1, source_target_pairs={{0,6},{1,7},{2,0},{3,1},{4,2},{5,3},{6,4},{7,5},{8,14},{9,15},{10,... | collective-permute-start | bytes 294920 | tf_op jit(solution)/shard_map/ppermute | solution.py:74
  17.2 2.5 %tables.1 = (bf16[256,512]{1,0:T(8,128)(2,1)S(1)}, bf16[256,512]{1,0:T(8,128)(2,1)S(1)}, bf16[256,512]{1,0:T(8,128)(2,1)S(1)}, bf16[256,512]{1,0:T(8,128)(2,1)S(...) custom-call(s32[2]{0:T(128)S(1)} %pad_add_fusion.refs_0_), custom_call_target="tpu_custom_call" | custom-call | bytes 2228232 | tf_op jit(solution)/shard_map/tables/pallas_call | solution.py:30
  19.7 1.8 %push_rest.1 = (f32[3,4,64,128]{3,2,1,0:T(8,128)S(1)}, f32[8,768]{1,0:T(8,128)S(1)}, f32[24,128]{1,0:T(8,128)S(1)}, f32[24,128]{1,0:T(8,128)S(1)}) custom-call(f32[3,4,64,128]{3,2,1,0:T(8,128)S(1)} %push_inner.1.refs_0_, f32[4,64,128]{2,1,0:T(8,128)S(1)} %copy-done.3, f32[24,128]{1,0:T(8,128)S(1)} %collective-permute-done.refs_2_, ...), custom_call_target="tpu_custom_call" | custom-call | bytes 1138688 | tf_op jit(solution)/shard_map/push_rest/pallas_call | solution.py:30
  23.1 3.1 %collective-permute-start.9 = (f32[8,768]{1,0:T(8,128)S(1)}, f32[8,768]{1,0:T(8,128)S(1)}, u32[]{:S(2)}, u32[]{:S(2)}) collective-permute-start(f32[8,768]{1,0:T(8,128)S(1)} %get-tuple-element.69), channel_id=1, source_target_pairs={{0,7},{1,0},{2,1},{3,2},{4,3},{5,4},{6,5},{7,6},{8,15},{9,8},{10,9... | collective-permute-start | bytes 73736 | tf_op jit(solution)/shard_map/ppermute | solution.py:74
  27.8 1.7 %collective-permute-start.10 = (f32[120,128]{1,0:T(8,128)S(1)}, f32[120,128]{1,0:T(8,128)S(1)}, u32[]{:S(2)}, u32[]{:S(2)}) collective-permute-start(f32[120,128]{1,0:T(8,128)S(1)} %get-tuple-element.70), channel_id=1, source_target_pairs={{0,8},{8,16},{16,24},{24,0},{1,9},{9,17},{17,25},{25,1},{2,10},{10... | collective-permute-start | bytes 184328 | tf_op jit(solution)/shard_map/ppermute | solution.py:74
  30.7 1.6 %collective-permute-start.16 = (f32[96,128]{1,0:T(8,128)S(1)}, f32[96,128]{1,0:T(8,128)S(1)}, u32[]{:S(2)}, u32[]{:S(2)}) collective-permute-start(f32[96,128]{1,0:T(8,128)S(1)} %get-tuple-element.79), channel_id=1, source_target_pairs={{0,16},{8,24},{16,0},{24,8},{1,17},{9,25},{17,1},{25,9},{2,18},{10... | collective-permute-start | bytes 147464 | tf_op jit(solution)/shard_map/ppermute | solution.py:74
  33.2 1.6 %collective-permute-done.16.refs_3_ = f32[96,128]{1,0:T(8,128)S(1)} collective-permute-done((f32[96,128]{1,0:T(8,128)S(1)}, f32[96,128]{1,0:T(8,128)S(1)}, u32[]{:S(2)}, u32[]{:S(2)}) %collective-permute-start.16) | collective-permute-done | bytes 49184 | tf_op jit(solution)/shard_map/ppermute | solution.py:74
  35.9 1.7 %collective-permute-start.17 = (f32[104,128]{1,0:T(8,128)S(1)}, f32[104,128]{1,0:T(8,128)S(1)}, u32[]{:S(2)}, u32[]{:S(2)}) collective-permute-start(f32[104,128]{1,0:T(8,128)S(1)} %get-tuple-element.84), channel_id=1, source_target_pairs={{0,24},{8,0},{16,8},{24,16},{1,25},{9,1},{17,9},{25,17},{2,26},{10... | collective-permute-start | bytes 159752 | tf_op jit(solution)/shard_map/ppermute | solution.py:74
  37.5 1.5 %collective-permute-start.18 = (f32[104,128]{1,0:T(8,128)S(1)}, f32[104,128]{1,0:T(8,128)S(1)}, u32[]{:S(2)}, u32[]{:S(2)}) collective-permute-start(f32[104,128]{1,0:T(8,128)S(1)} %get-tuple-element.85), channel_id=1, source_target_pairs={{0,16},{8,24},{16,0},{24,8},{1,17},{9,25},{17,1},{25,9},{2,18},{10... | collective-permute-start | bytes 159752 | tf_op jit(solution)/shard_map/ppermute | solution.py:74
  39.5 2.2 %push_stress.2 = (f32[6,4,64,128]{3,2,1,0:T(8,128)S(1)}, f32[8,768]{1,0:T(8,128)S(1)}, f32[24,128]{1,0:T(8,128)S(1)}, f32[24,128]{1,0:T(8,128)S(1)}) custom-call(f32[6,4,64,128]{3,2,1,0:T(8,128)S(1)} %copy-done.1, f32[3,4,64,128]{3,2,1,0:T(8,128)S(1)} %get-tuple-element.62.refs_1_.refs_0_, f32[4,64,128]{2,1,0:T(8,128)S(1)} %copy-done.6, ...), custom_call_target="tpu_custom_call" | custom-call | bytes 2449408 | tf_op jit(solution)/shard_map/push_stress/pallas_call | solution.py:30
  42.0 2.0 %collective-permute-done.19.refs_3_ = f32[104,128]{1,0:T(8,128)S(1)} collective-permute-done((f32[104,128]{1,0:T(8,128)S(1)}, f32[104,128]{1,0:T(8,128)S(1)}, u32[]{:S(2)}, u32[]{:S(2)}) %collective-permute-start.19) | collective-permute-done | bytes 53280 | tf_op jit(solution)/shard_map/ppermute | solution.py:74
  48.9 2.9 %collective-permute-start.13 = (f32[24,128]{1,0:T(8,128)S(1)}, f32[24,128]{1,0:T(8,128)S(1)}, u32[]{:S(2)}, u32[]{:S(2)}) collective-permute-start(f32[24,128]{1,0:T(8,128)S(1)} %get-tuple-element.74.refs_4_), channel_id=1, source_target_pairs={{0,24},{8,0},{16,8},{24,16},{1,25},{9,1},{17,9},{25,17},{2,26},{10... | collective-permute-start | bytes 36872 | tf_op jit(solution)/shard_map/ppermute | solution.py:74
  51.8 1.7 %collective-permute-done.12.refs_3_ = f32[24,128]{1,0:T(8,128)S(1)} collective-permute-done((f32[24,128]{1,0:T(8,128)S(1)}, f32[24,128]{1,0:T(8,128)S(1)}, u32[]{:S(2)}, u32[]{:S(2)}) %collective-permute-start.12) | collective-permute-done | bytes 12320 | tf_op jit(solution)/shard_map/ppermute | solution.py:74
  53.5 3.5 %collective-permute-start.15 = (f32[8,768]{1,0:T(8,128)S(1)}, f32[8,768]{1,0:T(8,128)S(1)}, u32[]{:S(2)}, u32[]{:S(2)}) collective-permute-start(f32[8,768]{1,0:T(8,128)S(1)} %get-tuple-element.75), channel_id=1, source_target_pairs={{0,7},{1,0},{2,1},{3,2},{4,3},{5,4},{6,5},{7,6},{8,15},{9,8},{10,9... | collective-permute-start | bytes 73736 | tf_op jit(solution)/shard_map/ppermute | solution.py:74
  57.0 1.5 %collective-permute-done.14.refs_5_ = f32[8,768]{1,0:T(8,128)S(1)} collective-permute-done((f32[8,768]{1,0:T(8,128)S(1)}, f32[8,768]{1,0:T(8,128)S(1)}, u32[]{:S(2)}, u32[]{:S(2)}) %collective-permute-start.14) | collective-permute-done | bytes 24608 | tf_op jit(solution)/shard_map/ppermute | solution.py:74
  58.5 1.3 %push_velocity.1 = (f32[3,4,64,128]{3,2,1,0:T(8,128)S(1)}, f32[128,128]{1,0:T(8,128)S(1)}) custom-call(f32[3,4,64,128]{3,2,1,0:T(8,128)S(1)} %get-tuple-element.62.refs_1_.refs_0_, f32[6,4,64,128]{3,2,1,0:T(8,128)S(1)} %get-tuple-element.72.refs_1_.refs_0_, f32[4,64,128]{2,1,0:T(8,128)S(1)} %copy-done.3, f32[24,128]{1,0:T(8,128)S(1)} %collective-permute-done.12.refs_3_, ...), custom_call_target="tpu_custom_call" | custom-call | bytes 1843200 | tf_op jit(solution)/shard_map/push_velocity/pallas_call | solution.py:30
  60.0 1.6 %collective-permute-start.25 = (f32[128,128]{1,0:T(8,128)S(1)}, f32[128,128]{1,0:T(8,128)S(1)}, u32[]{:S(2)}, u32[]{:S(2)}) collective-permute-start(f32[128,128]{1,0:T(8,128)S(1)} %get-tuple-element.96.refs_0_), channel_id=1, source_target_pairs={{0,4},{1,5},{2,6},{3,7},{4,0},{5,1},{6,2},{7,3},{8,12},{9,13},{10,... | collective-permute-start | bytes 196616 | tf_op jit(solution)/shard_map/ppermute | solution.py:74
  61.6 2.8 %collective-permute-start.26 = (f32[128,128]{1,0:T(8,128)S(1)}, f32[128,128]{1,0:T(8,128)S(1)}, u32[]{:S(2)}, u32[]{:S(2)}) collective-permute-start(f32[128,128]{1,0:T(8,128)S(1)} %get-tuple-element.96.refs_0_), channel_id=1, source_target_pairs={{0,6},{1,7},{2,0},{3,1},{4,2},{5,3},{6,4},{7,5},{8,14},{9,15},{10,... | collective-permute-start | bytes 196616 | tf_op jit(solution)/shard_map/ppermute | solution.py:74
  64.8 1.4 %collective-permute-start.28 = (f32[64,128]{1,0:T(8,128)S(1)}, f32[64,128]{1,0:T(8,128)S(1)}, u32[]{:S(2)}, u32[]{:S(2)}) collective-permute-start(f32[64,128]{1,0:T(8,128)S(1)} %get-tuple-element.94.refs_3_.refs_4_), channel_id=1, source_target_pairs={{0,4},{1,5},{2,6},{3,7},{4,0},{5,1},{6,2},{7,3},{8,12},{9,13},{10,... | collective-permute-start | bytes 98312 | tf_op jit(solution)/shard_map/ppermute | solution.py:74
  66.8 2.3 %collective-permute-start.29 = (f32[64,128]{1,0:T(8,128)S(1)}, f32[64,128]{1,0:T(8,128)S(1)}, u32[]{:S(2)}, u32[]{:S(2)}) collective-permute-start(f32[64,128]{1,0:T(8,128)S(1)} %get-tuple-element.94.refs_3_.refs_4_), channel_id=1, source_target_pairs={{0,6},{1,7},{2,0},{3,1},{4,2},{5,3},{6,4},{7,5},{8,14},{9,15},{10,... | collective-permute-start | bytes 98312 | tf_op jit(solution)/shard_map/ppermute | solution.py:74
  72.9 3.2 %collective-permute-start.32 = (f32[8,768]{1,0:T(8,128)S(1)}, f32[8,768]{1,0:T(8,128)S(1)}, u32[]{:S(2)}, u32[]{:S(2)}) collective-permute-start(f32[8,768]{1,0:T(8,128)S(1)} %get-tuple-element.99), channel_id=1, source_target_pairs={{0,7},{1,0},{2,1},{3,2},{4,3},{5,4},{6,5},{7,6},{8,15},{9,8},{10,9... | collective-permute-start | bytes 73736 | tf_op jit(solution)/shard_map/ppermute | solution.py:74
  78.1 2.6 %collective-permute-start.34 = (f32[120,128]{1,0:T(8,128)S(1)}, f32[120,128]{1,0:T(8,128)S(1)}, u32[]{:S(2)}, u32[]{:S(2)}) collective-permute-start(f32[120,128]{1,0:T(8,128)S(1)} %get-tuple-element.101), channel_id=1, source_target_pairs={{0,24},{8,0},{16,8},{24,16},{1,25},{9,1},{17,9},{25,17},{2,26},{10... | collective-permute-start | bytes 184328 | tf_op jit(solution)/shard_map/ppermute | solution.py:74
  81.9 2.9 %collective-permute-done.35.refs_2_ = f32[96,128]{1,0:T(8,128)S(1)} collective-permute-done((f32[96,128]{1,0:T(8,128)S(1)}, f32[96,128]{1,0:T(8,128)S(1)}, u32[]{:S(2)}, u32[]{:S(2)}) %collective-permute-start.35) | collective-permute-done | bytes 49184 | tf_op jit(solution)/shard_map/ppermute | solution.py:74
  84.8 1.5 %convolve.3 = (f32[2,3,2,32,256]{4,3,2,1,0:T(8,128)}, f32[96,128]{1,0:T(8,128)S(1)}, f32[96,128]{1,0:T(8,128)S(1)}, f32[96,128]{1,0:T(8,128)S(1)}, f32[96,128]{1,0:T(8,128)S(1)}) custom-call(f32[96,128]{1,0:T(8,128)S(1)} %get-tuple-element.102.refs_0_, f32[120,128]{1,0:T(8,128)S(1)} %collective-permute-done.33.refs_4_.refs_1_, ...), custom_call_target="tpu_custom_call" | custom-call | bytes 2449408 | tf_op jit(solution)/shard_map/convolve/pallas_call | solution.py:30
  89.5 1.4 %push_stress.3.refs_4_.refs_0_ = f32[6,4,64,128]{3,2,1,0:T(8,128)S(1)} custom-call(f32[6,4,64,128]{3,2,1,0:T(8,128)S(1)} %get-tuple-element.72.refs_1_.refs_0_, f32[3,4,64,128]{3,2,1,0:T(8,128)S(1)} %copy-done.8, f32[4,64,128]{2,1,0:T(8,128)S(1)} %copy-done.6, f32[4,64,128]{2,1,0:T(8,128)S(1)} %copy-done.7, ...), custom_call_target="tpu_custom_call" | custom-call | bytes 2506752 | tf_op jit(solution)/shard_map/push_stress/pallas_call | solution.py:30
  91.4 2.1 %collective-permute-done.38.refs_3_ = f32[96,128]{1,0:T(8,128)S(1)} collective-permute-done((f32[96,128]{1,0:T(8,128)S(1)}, f32[96,128]{1,0:T(8,128)S(1)}, u32[]{:S(2)}, u32[]{:S(2)}) %collective-permute-start.38) | collective-permute-done | bytes 49184 | tf_op jit(solution)/shard_map/ppermute | solution.py:74
  95.5 1.5 %collective-permute-start.40 = (f32[192,128]{1,0:T(8,128)S(1)}, f32[192,128]{1,0:T(8,128)S(1)}, u32[]{:S(2)}, u32[]{:S(2)}) collective-permute-start(f32[192,128]{1,0:T(8,128)S(1)} %get-tuple-element.111), channel_id=1, source_target_pairs={{0,6},{1,7},{2,0},{3,1},{4,2},{5,3},{6,4},{7,5},{8,14},{9,15},{10,... | collective-permute-start | bytes 294920 | tf_op jit(solution)/shard_map/ppermute | solution.py:74
  97.7 2.7 %collective-permute-done.40.refs_2_ = f32[192,128]{1,0:T(8,128)S(1)} collective-permute-done((f32[192,128]{1,0:T(8,128)S(1)}, f32[192,128]{1,0:T(8,128)S(1)}, u32[]{:S(2)}, u32[]{:S(2)}) %collective-permute-start.40) | collective-permute-done | bytes 98336 | tf_op jit(solution)/shard_map/ppermute | solution.py:74
  100.4 6.3 %collective-permute-done.41.refs_3_ = f32[192,128]{1,0:T(8,128)S(1)} collective-permute-done((f32[192,128]{1,0:T(8,128)S(1)}, f32[192,128]{1,0:T(8,128)S(1)}, u32[]{:S(2)}, u32[]{:S(2)}) %collective-permute-start.41) | collective-permute-done | bytes 98336 | tf_op jit(solution)/shard_map/ppermute | solution.py:74
  (102 shorter events, 33.8 us)
Async XLA Ops:
  2.2 10.2 %collective-permute-start.2 = (f32[8,768]{1,0:T(8,128)S(1)}, f32[8,768]{1,0:T(8,128)S(1)}, u32[]{:S(2)}, u32[]{:S(2)}) collective-permute-start(f32[8,768]{1,0:T(8,128)S(1)} %get-tuple-element.61), channel_id=1, source_target_pairs={{0,1},{1,2},{2,3},{3,4},{4,5},{5,6},{6,7},{7,0},{8,9},{9,10},{10,1... | collective-permute-start | bytes 73736 | tf_op jit(solution)/shard_map/ppermute | solution.py:74
  2.7 9.7 %collective-permute-start.3 = (f32[8,768]{1,0:T(8,128)S(1)}, f32[8,768]{1,0:T(8,128)S(1)}, u32[]{:S(2)}, u32[]{:S(2)}) collective-permute-start(f32[8,768]{1,0:T(8,128)S(1)} %get-tuple-element.61), channel_id=1, source_target_pairs={{0,7},{1,0},{2,1},{3,2},{4,3},{5,4},{6,5},{7,6},{8,15},{9,8},{10,9... | collective-permute-start | bytes 73736 | tf_op jit(solution)/shard_map/ppermute | solution.py:74
  6.7 5.4 %collective-permute-start = (f32[24,128]{1,0:T(8,128)S(1)}, f32[24,128]{1,0:T(8,128)S(1)}, u32[]{:S(2)}, u32[]{:S(2)}) collective-permute-start(f32[24,128]{1,0:T(8,128)S(1)} %get-tuple-element.59), channel_id=1, source_target_pairs={{0,8},{8,16},{16,24},{24,0},{1,9},{9,17},{17,25},{25,1},{2,10},{10... | collective-permute-start | bytes 36872 | tf_op jit(solution)/shard_map/ppermute | solution.py:74
  12.9 8.6 %collective-permute-start.4 = (f32[192,128]{1,0:T(8,128)S(1)}, f32[192,128]{1,0:T(8,128)S(1)}, u32[]{:S(2)}, u32[]{:S(2)}) collective-permute-start(f32[192,128]{1,0:T(8,128)S(1)} %push_top.1.refs_6_.refs_0_), channel_id=1, source_target_pairs={{0,2},{1,3},{2,4},{3,5},{4,6},{5,7},{6,0},{7,1},{8,10},{9,11},{10,... | collective-permute-start | bytes 294920 | tf_op jit(solution)/shard_map/ppermute | solution.py:74
  13.2 8.9 %collective-permute-start.5 = (f32[192,128]{1,0:T(8,128)S(1)}, f32[192,128]{1,0:T(8,128)S(1)}, u32[]{:S(2)}, u32[]{:S(2)}) collective-permute-start(f32[192,128]{1,0:T(8,128)S(1)} %push_top.1.refs_6_.refs_0_), channel_id=1, source_target_pairs={{0,4},{1,5},{2,6},{3,7},{4,0},{5,1},{6,2},{7,3},{8,12},{9,13},{10,... | collective-permute-start | bytes 294920 | tf_op jit(solution)/shard_map/ppermute | solution.py:74
  15.8 6.3 %collective-permute-start.6 = (f32[192,128]{1,0:T(8,128)S(1)}, f32[192,128]{1,0:T(8,128)S(1)}, u32[]{:S(2)}, u32[]{:S(2)}) collective-permute-start(f32[192,128]{1,0:T(8,128)S(1)} %push_top.1.refs_6_.refs_0_), channel_id=1, source_target_pairs={{0,6},{1,7},{2,0},{3,1},{4,2},{5,3},{6,4},{7,5},{8,14},{9,15},{10,... | collective-permute-start | bytes 294920 | tf_op jit(solution)/shard_map/ppermute | solution.py:74
  22.5 5.2 %collective-permute-start.7 = (f32[384,128]{1,0:T(8,128)S(1)}, f32[384,128]{1,0:T(8,128)S(1)}, u32[]{:S(2)}, u32[]{:S(2)}) collective-permute-start(f32[384,128]{1,0:T(8,128)S(1)} %forward_other.2), channel_id=1, source_target_pairs={{0,1},{1,0},{2,3},{3,2},{4,5},{5,4},{6,7},{7,6},{8,9},{9,8},{10,11... | collective-permute-start | bytes 589832 | tf_op jit(solution)/shard_map/ppermute | solution.py:79
  22.6 5.1 %collective-permute-start.8 = (f32[8,768]{1,0:T(8,128)S(1)}, f32[8,768]{1,0:T(8,128)S(1)}, u32[]{:S(2)}, u32[]{:S(2)}) collective-permute-start(f32[8,768]{1,0:T(8,128)S(1)} %get-tuple-element.69), channel_id=1, source_target_pairs={{0,1},{1,2},{2,3},{3,4},{4,5},{5,6},{6,7},{7,0},{8,9},{9,10},{10,1... | collective-permute-start | bytes 73736 | tf_op jit(solution)/shard_map/ppermute | solution.py:74
  27.8 7.1 %collective-permute-start.10 = (f32[120,128]{1,0:T(8,128)S(1)}, f32[120,128]{1,0:T(8,128)S(1)}, u32[]{:S(2)}, u32[]{:S(2)}) collective-permute-start(f32[120,128]{1,0:T(8,128)S(1)} %get-tuple-element.70), channel_id=1, source_target_pairs={{0,8},{8,16},{16,24},{24,0},{1,9},{9,17},{17,25},{25,1},{2,10},{10... | collective-permute-start | bytes 184328 | tf_op jit(solution)/shard_map/ppermute | solution.py:74
  29.5 5.3 %collective-permute-start.11 = (f32[120,128]{1,0:T(8,128)S(1)}, f32[120,128]{1,0:T(8,128)S(1)}, u32[]{:S(2)}, u32[]{:S(2)}) collective-permute-start(f32[120,128]{1,0:T(8,128)S(1)} %get-tuple-element.71), channel_id=1, source_target_pairs={{0,24},{8,0},{16,8},{24,16},{1,25},{9,1},{17,9},{25,17},{2,26},{10... | collective-permute-start | bytes 184328 | tf_op jit(solution)/shard_map/ppermute | solution.py:74
  35.9 5.9 %collective-permute-start.17 = (f32[104,128]{1,0:T(8,128)S(1)}, f32[104,128]{1,0:T(8,128)S(1)}, u32[]{:S(2)}, u32[]{:S(2)}) collective-permute-start(f32[104,128]{1,0:T(8,128)S(1)} %get-tuple-element.84), channel_id=1, source_target_pairs={{0,24},{8,0},{16,8},{24,16},{1,25},{9,1},{17,9},{25,17},{2,26},{10... | collective-permute-start | bytes 159752 | tf_op jit(solution)/shard_map/ppermute | solution.py:74
  39.0 5.0 %collective-permute-start.19 = (f32[104,128]{1,0:T(8,128)S(1)}, f32[104,128]{1,0:T(8,128)S(1)}, u32[]{:S(2)}, u32[]{:S(2)}) collective-permute-start(f32[104,128]{1,0:T(8,128)S(1)} %get-tuple-element.86), channel_id=1, source_target_pairs={{0,8},{8,16},{16,24},{24,0},{1,9},{9,17},{17,25},{25,1},{2,10},{10... | collective-permute-start | bytes 159752 | tf_op jit(solution)/shard_map/ppermute | solution.py:74
  46.1 15.5 %collective-permute-start.21 = (f32[208,128]{1,0:T(8,128)S(1)}, f32[208,128]{1,0:T(8,128)S(1)}, u32[]{:S(2)}, u32[]{:S(2)}) collective-permute-start(f32[208,128]{1,0:T(8,128)S(1)} %get-tuple-element.90), channel_id=1, source_target_pairs={{0,6},{1,7},{2,0},{3,1},{4,2},{5,3},{6,4},{7,5},{8,14},{9,15},{10,... | collective-permute-start | bytes 319496 | tf_op jit(solution)/shard_map/ppermute | solution.py:74
  47.3 17.1 %collective-permute-start.22 = (f32[208,128]{1,0:T(8,128)S(1)}, f32[208,128]{1,0:T(8,128)S(1)}, u32[]{:S(2)}, u32[]{:S(2)}) collective-permute-start(f32[208,128]{1,0:T(8,128)S(1)} %get-tuple-element.91), channel_id=1, source_target_pairs={{0,4},{1,5},{2,6},{3,7},{4,0},{5,1},{6,2},{7,3},{8,12},{9,13},{10,... | collective-permute-start | bytes 319496 | tf_op jit(solution)/shard_map/ppermute | solution.py:74
  47.9 16.5 %collective-permute-start.23 = (f32[208,128]{1,0:T(8,128)S(1)}, f32[208,128]{1,0:T(8,128)S(1)}, u32[]{:S(2)}, u32[]{:S(2)}) collective-permute-start(f32[208,128]{1,0:T(8,128)S(1)} %get-tuple-element.92), channel_id=1, source_target_pairs={{0,2},{1,3},{2,4},{3,5},{4,6},{5,7},{6,0},{7,1},{8,10},{9,11},{10,... | collective-permute-start | bytes 319496 | tf_op jit(solution)/shard_map/ppermute | solution.py:74
  53.5 5.0 %collective-permute-start.14 = (f32[8,768]{1,0:T(8,128)S(1)}, f32[8,768]{1,0:T(8,128)S(1)}, u32[]{:S(2)}, u32[]{:S(2)}) collective-permute-start(f32[8,768]{1,0:T(8,128)S(1)} %get-tuple-element.75), channel_id=1, source_target_pairs={{0,1},{1,2},{2,3},{3,4},{4,5},{5,6},{6,7},{7,0},{8,9},{9,10},{10,1... | collective-permute-start | bytes 73736 | tf_op jit(solution)/shard_map/ppermute | solution.py:74
  53.5 5.1 %collective-permute-start.15 = (f32[8,768]{1,0:T(8,128)S(1)}, f32[8,768]{1,0:T(8,128)S(1)}, u32[]{:S(2)}, u32[]{:S(2)}) collective-permute-start(f32[8,768]{1,0:T(8,128)S(1)} %get-tuple-element.75), channel_id=1, source_target_pairs={{0,7},{1,0},{2,1},{3,2},{4,3},{5,4},{6,5},{7,6},{8,15},{9,8},{10,9... | collective-permute-start | bytes 73736 | tf_op jit(solution)/shard_map/ppermute | solution.py:74
  59.8 6.9 %collective-permute-start.24 = (f32[128,128]{1,0:T(8,128)S(1)}, f32[128,128]{1,0:T(8,128)S(1)}, u32[]{:S(2)}, u32[]{:S(2)}) collective-permute-start(f32[128,128]{1,0:T(8,128)S(1)} %get-tuple-element.96.refs_0_), channel_id=1, source_target_pairs={{0,2},{1,3},{2,4},{3,5},{4,6},{5,7},{6,0},{7,1},{8,10},{9,11},{10,... | collective-permute-start | bytes 196616 | tf_op jit(solution)/shard_map/ppermute | solution.py:74
  60.0 9.9 %collective-permute-start.25 = (f32[128,128]{1,0:T(8,128)S(1)}, f32[128,128]{1,0:T(8,128)S(1)}, u32[]{:S(2)}, u32[]{:S(2)}) collective-permute-start(f32[128,128]{1,0:T(8,128)S(1)} %get-tuple-element.96.refs_0_), channel_id=1, source_target_pairs={{0,4},{1,5},{2,6},{3,7},{4,0},{5,1},{6,2},{7,3},{8,12},{9,13},{10,... | collective-permute-start | bytes 196616 | tf_op jit(solution)/shard_map/ppermute | solution.py:74
  61.6 8.3 %collective-permute-start.26 = (f32[128,128]{1,0:T(8,128)S(1)}, f32[128,128]{1,0:T(8,128)S(1)}, u32[]{:S(2)}, u32[]{:S(2)}) collective-permute-start(f32[128,128]{1,0:T(8,128)S(1)} %get-tuple-element.96.refs_0_), channel_id=1, source_target_pairs={{0,6},{1,7},{2,0},{3,1},{4,2},{5,3},{6,4},{7,5},{8,14},{9,15},{10,... | collective-permute-start | bytes 196616 | tf_op jit(solution)/shard_map/ppermute | solution.py:74
  64.7 5.9 %collective-permute-start.27 = (f32[64,128]{1,0:T(8,128)S(1)}, f32[64,128]{1,0:T(8,128)S(1)}, u32[]{:S(2)}, u32[]{:S(2)}) collective-permute-start(f32[64,128]{1,0:T(8,128)S(1)} %get-tuple-element.94.refs_3_.refs_4_), channel_id=1, source_target_pairs={{0,2},{1,3},{2,4},{3,5},{4,6},{5,7},{6,0},{7,1},{8,10},{9,11},{10,... | collective-permute-start | bytes 98312 | tf_op jit(solution)/shard_map/ppermute | solution.py:74
  64.8 7.1 %collective-permute-start.28 = (f32[64,128]{1,0:T(8,128)S(1)}, f32[64,128]{1,0:T(8,128)S(1)}, u32[]{:S(2)}, u32[]{:S(2)}) collective-permute-start(f32[64,128]{1,0:T(8,128)S(1)} %get-tuple-element.94.refs_3_.refs_4_), channel_id=1, source_target_pairs={{0,4},{1,5},{2,6},{3,7},{4,0},{5,1},{6,2},{7,3},{8,12},{9,13},{10,... | collective-permute-start | bytes 98312 | tf_op jit(solution)/shard_map/ppermute | solution.py:74
  66.8 5.1 %collective-permute-start.29 = (f32[64,128]{1,0:T(8,128)S(1)}, f32[64,128]{1,0:T(8,128)S(1)}, u32[]{:S(2)}, u32[]{:S(2)}) collective-permute-start(f32[64,128]{1,0:T(8,128)S(1)} %get-tuple-element.94.refs_3_.refs_4_), channel_id=1, source_target_pairs={{0,6},{1,7},{2,0},{3,1},{4,2},{5,3},{6,4},{7,5},{8,14},{9,15},{10,... | collective-permute-start | bytes 98312 | tf_op jit(solution)/shard_map/ppermute | solution.py:74
  72.4 5.3 %collective-permute-start.30 = (f32[384,128]{1,0:T(8,128)S(1)}, f32[384,128]{1,0:T(8,128)S(1)}, u32[]{:S(2)}, u32[]{:S(2)}) collective-permute-start(f32[384,128]{1,0:T(8,128)S(1)} %forward_other.3), channel_id=1, source_target_pairs={{0,1},{1,0},{2,3},{3,2},{4,5},{5,4},{6,7},{7,6},{8,9},{9,8},{10,11... | collective-permute-start | bytes 589832 | tf_op jit(solution)/shard_map/ppermute | solution.py:79
  72.6 5.1 %collective-permute-start.31 = (f32[8,768]{1,0:T(8,128)S(1)}, f32[8,768]{1,0:T(8,128)S(1)}, u32[]{:S(2)}, u32[]{:S(2)}) collective-permute-start(f32[8,768]{1,0:T(8,128)S(1)} %get-tuple-element.99), channel_id=1, source_target_pairs={{0,1},{1,2},{2,3},{3,4},{4,5},{5,6},{6,7},{7,0},{8,9},{9,10},{10,1... | collective-permute-start | bytes 73736 | tf_op jit(solution)/shard_map/ppermute | solution.py:74
  72.9 4.7 %collective-permute-start.32 = (f32[8,768]{1,0:T(8,128)S(1)}, f32[8,768]{1,0:T(8,128)S(1)}, u32[]{:S(2)}, u32[]{:S(2)}) collective-permute-start(f32[8,768]{1,0:T(8,128)S(1)} %get-tuple-element.99), channel_id=1, source_target_pairs={{0,7},{1,0},{2,1},{3,2},{4,3},{5,4},{6,5},{7,6},{8,15},{9,8},{10,9... | collective-permute-start | bytes 73736 | tf_op jit(solution)/shard_map/ppermute | solution.py:74
  77.7 7.1 %collective-permute-start.33 = (f32[120,128]{1,0:T(8,128)S(1)}, f32[120,128]{1,0:T(8,128)S(1)}, u32[]{:S(2)}, u32[]{:S(2)}) collective-permute-start(f32[120,128]{1,0:T(8,128)S(1)} %get-tuple-element.100), channel_id=1, source_target_pairs={{0,8},{8,16},{16,24},{24,0},{1,9},{9,17},{17,25},{25,1},{2,10},{10... | collective-permute-start | bytes 184328 | tf_op jit(solution)/shard_map/ppermute | solution.py:74
  78.1 6.7 %collective-permute-start.34 = (f32[120,128]{1,0:T(8,128)S(1)}, f32[120,128]{1,0:T(8,128)S(1)}, u32[]{:S(2)}, u32[]{:S(2)}) collective-permute-start(f32[120,128]{1,0:T(8,128)S(1)} %get-tuple-element.101), channel_id=1, source_target_pairs={{0,24},{8,0},{16,8},{24,16},{1,25},{9,1},{17,9},{25,17},{2,26},{10... | collective-permute-start | bytes 184328 | tf_op jit(solution)/shard_map/ppermute | solution.py:74
  88.5 5.0 %collective-permute-start.38 = (f32[96,128]{1,0:T(8,128)S(1)}, f32[96,128]{1,0:T(8,128)S(1)}, u32[]{:S(2)}, u32[]{:S(2)}) collective-permute-start(f32[96,128]{1,0:T(8,128)S(1)} %get-tuple-element.109), channel_id=1, source_target_pairs={{0,8},{8,16},{16,24},{24,0},{1,9},{9,17},{17,25},{25,1},{2,10},{10... | collective-permute-start | bytes 147464 | tf_op jit(solution)/shard_map/ppermute | solution.py:74
  95.5 4.9 %collective-permute-start.40 = (f32[192,128]{1,0:T(8,128)S(1)}, f32[192,128]{1,0:T(8,128)S(1)}, u32[]{:S(2)}, u32[]{:S(2)}) collective-permute-start(f32[192,128]{1,0:T(8,128)S(1)} %get-tuple-element.111), channel_id=1, source_target_pairs={{0,6},{1,7},{2,0},{3,1},{4,2},{5,3},{6,4},{7,5},{8,14},{9,15},{10,... | collective-permute-start | bytes 294920 | tf_op jit(solution)/shard_map/ppermute | solution.py:74
  97.0 9.6 %collective-permute-start.41 = (f32[192,128]{1,0:T(8,128)S(1)}, f32[192,128]{1,0:T(8,128)S(1)}, u32[]{:S(2)}, u32[]{:S(2)}) collective-permute-start(f32[192,128]{1,0:T(8,128)S(1)} %get-tuple-element.112), channel_id=1, source_target_pairs={{0,4},{1,5},{2,6},{3,7},{4,0},{5,1},{6,2},{7,3},{8,12},{9,13},{10,... | collective-permute-start | bytes 294920 | tf_op jit(solution)/shard_map/ppermute | solution.py:74
  97.0 9.6 %collective-permute-start.42 = (f32[192,128]{1,0:T(8,128)S(1)}, f32[192,128]{1,0:T(8,128)S(1)}, u32[]{:S(2)}, u32[]{:S(2)}) collective-permute-start(f32[192,128]{1,0:T(8,128)S(1)} %get-tuple-element.113), channel_id=1, source_target_pairs={{0,2},{1,3},{2,4},{3,5},{4,6},{5,7},{6,0},{7,1},{8,10},{9,11},{10,... | collective-permute-start | bytes 294920 | tf_op jit(solution)/shard_map/ppermute | solution.py:74
  (21 other events, 99.6 us)

commit v2 on v1

--- a/solution.py
+++ b/solution.py
@@ -1,4 +1,3 @@
-import functools
 import math
 
 import jax
@@ -7,6 +6,7 @@
 from jax.experimental import pallas as pl
 from jax.experimental.pallas import tpu as pltpu
 from jax.sharding import PartitionSpec as P
+
 
 STEPS = 2
 VMEM_LIMIT = 16 * 1024 * 1024
@@ -18,7 +18,7 @@
 NT = (((1,), (1,)), ((), ()))
 
 
-def call(body, name, outs, *args, scratch=(), after=()):
+def call(body, outs, *args, scratch=(), after=()):
     nbytes = sum(a.size * a.dtype.itemsize for a in args) + sum(
         math.prod(s) * jnp.dtype(d).itemsize for s, d in outs
     )
@@ -29,7 +29,6 @@
 
     results = pl.pallas_call(
         run,
-        name=name,
         out_shape=[jax.ShapeDtypeStruct(s, d) for s, d in outs],
         in_specs=[
             pl.BlockSpec(memory_space=pltpu.SMEM if a.dtype == jnp.int32 else pltpu.VMEM)
@@ -74,6 +73,17 @@
     return lax.ppermute(x, axis, [(i, (i + shift) % count) for i in range(count)])
 
 
+def depth_mask(t, odd, depth):
+    return (depth - t) & (depth - 1) if odd else t
+
+
+def depth_perm(x, t):
+    count = lax.axis_size("col")
+    return lax.ppermute(
+        x, "col", [(i, i ^ (2 * depth_mask(t, i & 1, count // 2))) for i in range(count)]
+    )
+
+
 def partner_perm(x):
     count = lax.axis_size("col")
     return lax.ppermute(x, "col", [(i, i ^ 1) for i in range(count)])
@@ -96,19 +106,33 @@
     def body(where_ref, oh, ol, ph, pl_, wh, wl, eo, ep, we):
         r, c = where_ref[0], where_ref[1]
 
+        def met(t):
+            turned = jnp.where((c & 1) == 1, (depth - t) & (depth - 1), t & (depth - 1))
+            return c ^ (2 * turned)
+
         def put(hi_ref, lo_ref, index, value):
             hi, lo = split(value)
             hi_ref[index] = hi
             lo_ref[index] = lo
 
+        line = iota((nk, yb), 0)
+        lane = iota((nk, yb), 1)
+        first_wave = ((line // kyb + r) & (rows - 1)) * (cols * kyb) + c * kyb + line % kyb
+        own_cos, own_sin = unit(first_wave * lane, ny)
+        hop = ((c ^ 1) - c) * kyb
+        hop_cos, hop_sin = unit(hop * iota((8, yb), 1), ny)
+        hop_cos, hop_sin = hop_cos[0:1], hop_sin[0:1]
         for flip, hi_ref, lo_ref, side_ref in ((0, oh, ol, eo), (1, ph, pl_, ep)):
             col = c ^ 1 if flip else c
-            line = iota((nk, yb), 0)
-            lane = iota((nk, yb), 1)
-            wave = ((line // kyb + r) & (rows - 1)) * (cols * kyb) + col * kyb + line % kyb
-            base_cos, base_sin = unit(wave * lane, ny)
-            start = ((c - 2 * lane) & (cols - 1)) * yb
-            turn_cos, turn_sin = unit(wave * start, ny)
+            base_cos, base_sin = own_cos, own_sin
+            if flip:
+                base_cos = own_cos * hop_cos - own_sin * hop_sin
+                base_sin = own_sin * hop_cos + own_cos * hop_sin
+            turn = iota((max(8, depth), nk), 0)
+            across = iota((max(8, depth), nk), 1)
+            wave = ((across // kyb + r) & (rows - 1)) * (cols * kyb) + col * kyb + across % kyb
+            turn_cos, turn_sin = unit(wave * ((met(turn)) * yb), ny)
+            turn_cos, turn_sin = turn_cos.T, turn_sin.T
             scale = 1.0 / math.sqrt(ny)
             for t in range(depth):
                 tc, ts = turn_cos[:, t : t + 1] * scale, turn_sin[:, t : t + 1] * scale
@@ -117,7 +141,7 @@
                 put(hi_ref, lo_ref, (pl.ds(nk, nk), span), -(base_sin * tc + base_cos * ts))
             line, lane = iota((depth * 8, nk), 0), iota((depth * 8, nk), 1)
             wave = ((lane // kyb + r) & (rows - 1)) * (cols * kyb) + col * kyb + lane % kyb
-            spot = ((c - 2 * (line // 8)) & (cols - 1)) * yb + beyond(line % 8, yb)
+            spot = (met(line // 8)) * yb + beyond(line % 8, yb)
             side_cos, side_sin = unit(wave * spot, ny)
             side_ref[:, :nk] = side_cos * scale
             side_ref[:, nk:] = -side_sin * scale
@@ -145,7 +169,7 @@
     y_shape, x_shape = (2 * nk, depth * yb), (2 * nx, 2 * nx)
     outs = [(y_shape, BF16)] * 4 + [(x_shape, BF16)] * 2
     outs += [((depth * 8, 2 * nk), F32)] * 2 + [((rows * 8, 2 * nx), F32)]
-    oh, ol, ph, pl_, wh, wl, eo, ep, we = call(body, "tables", outs, where)
+    oh, ol, ph, pl_, wh, wl, eo, ep, we = call(body, outs, where)
     return (oh, ol), (ph, pl_), (wh, wl), (eo, ep, we)
 
 
@@ -171,7 +195,7 @@
                 for part in range(2):
                     out_refs[step][line, pl.ds(part * nx, nx)] = totals[step][part]
 
-    return call(body, "past", [((comps * kyb, 2 * nx), F32)] * STEPS, kernel, history)
+    return call(body, [((comps * kyb, 2 * nx), F32)] * STEPS, kernel, history)
 
 
 ROW_PARTS = (0, 3, 4)
@@ -263,7 +287,7 @@
         rows, cols = plane_list(ROW_PARTS, layers), plane_list(COL_PARTS, layers)
         put_borders(lambda w: s_ref[w[0], w[1]], rows, cols, *outs)
 
-    return call(body, "borders", borders_shapes(layers, xb, yb), stress)
+    return call(body, borders_shapes(layers, xb, yb), stress)
 
 
 def exchange_edges(edge):
@@ -280,10 +304,10 @@
 DEPTH_PARTS = (4, 5, 2)
 
 
-def push_inner(velocity, stress, buoyancy):
-    comps, layers, xb, yb = velocity.shape
-
-    def body(v_ref, s_ref, b_ref, nv_ref, pad):
+def inner_force(stress, comps):
+    _, layers, xb, yb = stress.shape
+
+    def body(s_ref, f_ref, pad):
         none = jnp.zeros((2, yb), F32)
         stacked = jnp.concatenate(
             [s_ref[p, l] for p, l in plane_list(COL_PARTS, layers)], axis=0
@@ -295,33 +319,34 @@
                 force = row_deriv(pad.at[j], s_ref[ROW_PARTS[comp], layer], none, none)
                 force = force + along_y[j * xb : (j + 1) * xb]
                 force = force + depth_deriv(lambda l: s_ref[DEPTH_PARTS[comp], l], layer, layers)
-                nv_ref[comp, layer] = v_ref[comp, layer] + b_ref[layer] * force
+                f_ref[comp, layer] = force
 
     return call(
-        body, "push_inner", [(velocity.shape, F32)], velocity, stress, buoyancy,
+        body, [((comps, layers, xb, yb), F32)], stress,
         scratch=[pltpu.VMEM((comps * layers, xb + 16, yb), F32)],
     )[0]
 
 
-def push_top(inner, buoyancy, halo):
+def push_top(velocity, inner, buoyancy, halo):
     comps, layers, xb, yb = inner.shape
 
-    def body(v_ref, b_ref, up, dn, lf, rt, top_ref):
+    def body(v_ref, f_ref, b_ref, up, dn, lf, rt, top_ref):
         left_w, right_w = outer_weights(yb)
         for comp in range(comps):
             j = comp * layers
             pair, lane = slice(2 * j, 2 * j + 2), slice(j * xb, (j + 1) * xb)
             patch = row_patch(up[pair, :], dn[pair, :], xb)
             patch = patch + dot6(lf[:, lane].T, left_w, NN) + dot6(rt[:, lane].T, right_w, NN)
-            top_ref[comp * xb : (comp + 1) * xb, :] = v_ref[comp, 0] + b_ref[0] * patch
-
-    return call(body, "push_top", [((comps * xb, yb), F32)], inner, buoyancy, *halo)[0]
-
-
-def push_rest(inner, buoyancy, halo, top):
+            push = b_ref[0] * (f_ref[comp, 0] + patch)
+            top_ref[comp * xb : (comp + 1) * xb, :] = v_ref[comp, 0] + push
+
+    return call(body, [((comps * xb, yb), F32)], velocity, inner, buoyancy, *halo)[0]
+
+
+def push_rest(velocity, inner, buoyancy, halo, top):
     comps, layers, xb, yb = inner.shape
 
-    def body(v_ref, b_ref, up, dn, lf, rt, top_ref, nv_ref, edge, first, last):
+    def body(v_ref, f_ref, b_ref, up, dn, lf, rt, top_ref, nv_ref, edge, first, last):
         left_w, right_w = outer_weights(yb)
         along_y = dot6(lf[...].T, left_w, NN) + dot6(rt[...].T, right_w, NN)
         for comp in range(comps):
@@ -330,19 +355,20 @@
                 j = comp * layers + layer
                 pair = slice(2 * j, 2 * j + 2)
                 patch = row_patch(up[pair, :], dn[pair, :], xb) + along_y[j * xb : (j + 1) * xb]
-                nv_ref[comp, layer] = v_ref[comp, layer] + b_ref[layer] * patch
+                push = b_ref[layer] * (f_ref[comp, layer] + patch)
+                nv_ref[comp, layer] = v_ref[comp, layer] + push
         planes = plane_list(range(comps), layers)
         put_borders(lambda w: nv_ref[w[0], w[1]], planes, planes, edge, first, last)
 
     outs = [(inner.shape, F32)] + borders_shapes(layers, xb, yb)
-    new, *borders = call(body, "push_rest", outs, inner, buoyancy, *halo, top)
+    new, *borders = call(body, outs, velocity, inner, buoyancy, *halo, top)
     return new, borders
 
 
 def push_velocity(velocity, stress, buoyancy, halo):
     comps, layers, xb, yb = velocity.shape
 
-    def body(v_ref, s_ref, b_ref, up, dn, lf, rt, nv_ref, top_ref, pad):
+    def body(v_ref, s_ref, b_ref, up, dn, lf, rt, nv_ref, pad):
         stacked = jnp.concatenate(
             [s_ref[p, l] for p, l in plane_list(COL_PARTS, layers)], axis=0
         )
@@ -354,16 +380,12 @@
                 force = row_deriv(pad.at[j], s_ref[ROW_PARTS[comp], layer], up[pair, :], dn[pair, :])
                 force = force + along_y[j * xb : (j + 1) * xb]
                 force = force + depth_deriv(lambda l: s_ref[DEPTH_PARTS[comp], l], layer, layers)
-                new = v_ref[comp, layer] + b_ref[layer] * force
-                nv_ref[comp, layer] = new
-                if layer == 0 and comp < comps - 1:
-                    top_ref[comp * xb : (comp + 1) * xb, :] = new
-
-    outs = [(velocity.shape, F32), (((comps - 1) * xb, yb), F32)]
+                nv_ref[comp, layer] = v_ref[comp, layer] + b_ref[layer] * force
+
     return call(
-        body, "push_velocity", outs, velocity, stress, buoyancy, *halo,
+        body, [(velocity.shape, F32)], velocity, stress, buoyancy, *halo,
         scratch=[pltpu.VMEM((comps * layers, xb + 16, yb), F32)],
-    )
+    )[0]
 
 
 def push_stress(stress, velocity, lame, shear, halo, traction=None):
@@ -407,7 +429,7 @@
     args = [stress, velocity, lame, shear, *halo] + ([] if traction is None else [traction])
     outs = [(stress.shape, F32)] + (borders_shapes(layers, xb, yb) if traction is None else [])
     new, *borders = call(
-        body, "push_stress", outs, *args,
+        body, outs, *args,
         scratch=[pltpu.VMEM((comps * layers, xb + 16, yb), F32)],
     )
     return new, borders
@@ -421,7 +443,7 @@
 
 
 def top_after(pieces, velocity, buoyancy):
-    comps, layers, xb, yb = velocity.shape
+    comps, _, xb, yb = velocity.shape
     height = pieces[0].shape[0]
 
     def body(v_ref, b_ref, *refs):
@@ -436,10 +458,12 @@
         near = jnp.where(gap == 1, NEAR, 0.0) - jnp.where(gap == -1, NEAR, 0.0)
         outer = near + jnp.where(gap == 2, FAR, 0.0) - jnp.where(gap == -2, FAR, 0.0)
         force = force + (dot6(total[xb : 2 * xb], inner_weights(yb), NN) + dot6(side, outer, NN))
-        face_ref[...] = v_ref[comps - 1, 0] + b_ref[0] * force
+        for comp in range(comps - 1):
+            face_ref[comp * xb : (comp + 1) * xb, :] = v_ref[comp, 0]
+        face_ref[(comps - 1) * xb :, :] = v_ref[comps - 1, 0] + b_ref[0] * force
 
     return call(
-        body, "top_after", [((height, yb), F32), ((xb, yb), F32)], velocity, buoyancy, *pieces,
+        body, [((height, yb), F32), ((comps * xb, yb), F32)], velocity, buoyancy, *pieces,
         scratch=[pltpu.VMEM((xb + 16, yb), F32)],
     )
 
@@ -453,7 +477,7 @@
             for layer in range(layers):
                 new = v_ref[comp, layer]
                 if layer == 0 and comp == comps - 1:
-                    new = f_ref[...]
+                    new = f_ref[comp * xb :, :]
                 if layer in (1, 2):
                     weight = -NEAR if layer == 1 else -FAR
                     new = new + b_ref[layer] * (weight * push)
@@ -462,7 +486,7 @@
         put_borders(lambda w: nv_ref[w[0], w[1]], planes, planes, edge, first, last)
 
     outs = [(velocity.shape, F32)] + borders_shapes(layers, xb, yb)
-    new, *borders = call(body, "finish_velocity", outs, velocity, buoyancy, traction, face)
+    new, *borders = call(body, outs, velocity, buoyancy, traction, face)
     return new, borders
 
 
@@ -476,24 +500,17 @@
         for comp, part in enumerate(DEPTH_PARTS):
             ns_ref[part, 0] = s_ref[part, 0] + total[comp * xb : (comp + 1) * xb]
 
-    return call(body, "traction", [(stress.shape, F32)], stress, *pieces)[0]
-
-
-def part_forward(groups, table, dims, name, after=()):
-    rows, cols, xb, yb, kyb = dims
+    return call(body, [(stress.shape, F32)], stress, *pieces)[0]
+
+
+def part_forward(blocks, table, dims, after=()):
+    rows, _, xb, _, kyb = dims
     nk = rows * kyb
-    comps = sum(blocks[0].shape[0] for blocks in groups) // xb
-    depth = cols // 2
+    comps = blocks[0].shape[0] // xb
 
     def body(*refs):
         hi, lo, out = refs[-3:]
-        data = jnp.concatenate(
-            [
-                jnp.concatenate([ref[...] for ref in refs[g * depth : (g + 1) * depth]], axis=1)
-                for g in range(len(groups))
-            ],
-            axis=0,
-        )
+        data = jnp.concatenate([ref[...] for ref in refs[:-3]], axis=1)
         total = dot3((hi[...], lo[...]), split(data), NT)
         for s in range(rows):
             for comp in range(comps):
@@ -503,11 +520,10 @@
                 at = (s * comps + comp) * kyb
                 out[at : at + kyb, :] = jnp.concatenate([real, imag], axis=1)
 
-    blocks = [block for group in groups for block in group]
-    return call(body, name, [((rows * comps * kyb, 2 * xb), F32)], *blocks, *table, after=after)[0]
-
-
-def join(mine, other, first, last, dims, after):
+    return call(body, [((rows * comps * kyb, 2 * xb), F32)], *blocks, *table, after=after)[0]
+
+
+def join(mine, other, first, last, dims):
     rows = dims[0]
     height, extra = mine.shape[0] // rows, first.shape[0]
     riders = {1: 1, rows - 1: 0}
@@ -521,11 +537,11 @@
                 out[height:, :] = borders[riders[s]][...]
 
     outs = [((height + (extra if s in riders else 0), mine.shape[1]), F32) for s in range(rows)]
-    return call(body, "join", outs, mine, other, first, last, after=after)
+    return call(body, outs, mine, other, first, last)
 
 
 def convolve(blocks, table, past, kernel, before, dims, side=None):
-    rows, cols, xb, yb, kyb = dims
+    rows, _, xb, _, kyb = dims
     nx = rows * xb
     comps = blocks[0].shape[0] // kyb
     step = len(before)
@@ -572,12 +588,12 @@
     height = comps * kyb + (0 if side is None else 8)
     outs = [(spec_shape, F32)] + [((height, 2 * xb), F32)] * rows
     args = ([] if side is None else [side]) + [*blocks, *table, past, kernel, *before]
-    spec, *pieces = call(body, "convolve", outs, *args)
+    spec, *pieces = call(body, outs, *args)
     return spec, pieces
 
 
 def turn(blocks, dims, comps, after):
-    rows, cols, xb, yb, kyb = dims
+    rows, _, xb, _, kyb = dims
     main, wide = comps * xb, 2 * rows * kyb
     sides = blocks[0].shape[0] > comps * kyb
 
@@ -593,7 +609,7 @@
             out[main : main + 8, :] = jnp.zeros((8, wide), F32)
             out[main : main + 4, :] = jnp.concatenate(parts, axis=1)
 
-    return call(body, "turn", [((main + (8 if sides else 0), wide), F32)], *blocks, after=after)[0]
+    return call(body, [((main + (8 if sides else 0), wide), F32)], *blocks, after=after)[0]
 
 
 def y_inverse(d_ref, hi, lo, dims, side_ref):
@@ -614,7 +630,7 @@
 
     shape = (data.shape[0] + (0 if side is None else 8), dims[1] // 2 * dims[3])
     extra = [] if side is None else [side]
-    return call(body, "inverse_mine", [(shape, F32)], data, *table, *extra)[0]
+    return call(body, [(shape, F32)], data, *table, *extra)[0]
 
 
 def rest_inverse(mine, data, table, dims, side=None):
@@ -628,35 +644,41 @@
 
     outs = [((mine.shape[0], yb), F32)] * (cols // 2)
     extra = [] if side is None else [side]
-    return call(body, "inverse_other", outs, mine, data, *table, *extra)
+    return call(body, outs, mine, data, *table, *extra)
+
+
+def in_turn(blocks):
+    moved = []
+    for t, block in enumerate(blocks, 1):
+        moved.append(depth_perm(block, t))
+    return moved
 
 
 def gather_depth(block):
-    count = lax.axis_size("col") // 2
-    return [block] + [shift_perm(block, "col", 2 * t) for t in range(1, count)]
-
-
-def forward(groups, borders, tables_, dims):
+    return [block] + in_turn([block] * (lax.axis_size("col") // 2 - 1))
+
+
+def forward(faces, borders, tables_, dims, after):
     mine, other = tables_[:2]
     edge, first, last = borders
-    sent = part_forward(groups, other, dims, "forward_other", after=(first,))
+    sent = part_forward(faces, other, dims, after=(first, *after))
     came = partner_perm(sent)
-    kept = part_forward(groups, mine, dims, "forward_mine")
+    kept = part_forward(faces, mine, dims)
+    pieces = join(kept, came, first, last, dims)
+    pieces = pieces[:1] + [shift_perm(pieces[s], "row", s) for s in range(1, dims[0])]
     beside = exchange_edges(edge)
-    pieces = join(kept, came, first, last, dims, beside)
-    pieces = pieces[:1] + [shift_perm(pieces[s], "row", s) for s in range(1, dims[0])]
     return pieces, (pieces[1], pieces[-1], *beside)
 
 
-def inverse(pieces, tables_, dims, comps, last, token):
+def inverse(pieces, tables_, dims, comps, last, after):
     mine, other, _, (side_mine, side_other, _) = tables_
-    rows, cols = dims[:2]
+    rows, _ = dims[:2]
     pieces = pieces[:1] + [shift_perm(pieces[s], "row", -s) for s in range(1, rows)]
-    flat = turn(pieces, dims, comps, (token,))
+    flat = turn(pieces, dims, comps, after)
     flat_other = partner_perm(flat)
     total = part_inverse(flat, mine, dims, None if last else side_mine)
     pieces = rest_inverse(total, flat_other, other, dims, None if last else side_other)
-    return pieces[:1] + [shift_perm(pieces[t], "col", -2 * t) for t in range(1, cols // 2)]
+    return pieces[:1] + in_turn(pieces[1:])
 
 
 def on_device(velocity, stress, buoyancy, lame, shear, kernel, history):
@@ -667,32 +689,34 @@
     where = jnp.stack([lax.axis_index("row"), lax.axis_index("col")]).astype(jnp.int32)
 
     halo = exchange(first_borders(stress))
-    inner = push_inner(velocity, stress, buoyancy)
-    top = push_top(inner, buoyancy, halo)
+    inner = inner_force(stress, velocity.shape[0])
+    top = push_top(velocity, inner, buoyancy, halo)
     faces = gather_depth(top)
     tables_ = tables(where, dims)
     past = past_sums(kernel, history)
     recent = kernel[:STEPS]
-    velocity, borders = push_rest(inner, buoyancy, halo, top)
+    velocity, borders = push_rest(velocity, inner, buoyancy, halo, top)
     spectra = []
-    groups = [faces]
     traction = None
     for step in range(STEPS):
         last = step == STEPS - 1
-        pieces, halo = forward(groups, borders, tables_, dims)
+        pieces, halo = forward(faces, borders, tables_, dims, () if last else past)
         side = None if last else tables_[3][2]
-        spec, pieces = convolve(pieces, tables_[2], past[step], recent, spectra, dims, side)
+        spec, pieces = convolve(
+            pieces, tables_[2], past[step], recent, spectra, dims, side
+        )
         spectra.append(spec)
         stress, next_borders = push_stress(stress, velocity, lame, shear, halo, traction)
-        token = stress if last else next_borders[1]
-        pieces = inverse(pieces, tables_, dims, recent.shape[1], last, token)
+        after = () if last else (next_borders[1],)
+        if not last:
+            halo = exchange(next_borders)
+        pieces = inverse(pieces, tables_, dims, recent.shape[1], last, after)
         if last:
             break
-        velocity, early = push_velocity(velocity, stress, buoyancy, exchange(next_borders))
-        groups = [gather_depth(early)]
-        traction, face = top_after(pieces, velocity, buoyancy)
-        groups.append(gather_depth(face))
-        velocity, borders = finish_velocity(velocity, buoyancy, traction, face)
+        velocity = push_velocity(velocity, stress, buoyancy, halo)
+        traction, top = top_after(pieces, velocity, buoyancy)
+        faces = gather_depth(top)
+        velocity, borders = finish_velocity(velocity, buoyancy, traction, top)
     stress = add_traction(stress, pieces)
     return (velocity, stress, spectra[-1])
 

time: 108 us -> 106 us (0.981)
  waiting for transfers between devices: 29.2 us -> 39.4 us
  starting transfers between devices: 54.7 us -> 44.9 us
  local copies, waits for them, and re-layouts: 3.14 us -> 1.17 us
    ppermute x39 -> x24, starting transfers between devices: 54.3 us -> 26.8 us  [shift_perm(): lax.ppermute(x, axis, [(i, (i + shift) % count) for i in range(count)])]
    ppermute x0 -> x12, starting transfers between devices: none -> 17.8 us  [depth_perm(): lax.ppermute(x, 'col', [(i, i ^ 2 * depth_mask(t, i & 1, count // 2)) for...]
    ppermute x0 -> x12, waiting for transfers between devices: none -> 6.16 us  [depth_perm(): lax.ppermute(x, 'col', [(i, i ^ 2 * depth_mask(t, i & 1, count // 2)) for...]
    ppermute x39 -> x24, waiting for transfers between devices: 27 us -> 29.2 us  [shift_perm(): lax.ppermute(x, axis, [(i, (i + shift) % count) for i in range(count)])]
    unnamed x20 -> x18, local copies, waits for them, and re-layouts: 3.13 us -> 1.16 us
    ppermute x4, waiting for transfers between devices: 2.15 us -> 4.07 us  [partner_perm(): return lax.ppermute(x, 'col', [(i, i ^ 1) for i in range(count)])]
  transfers between devices with their start and end apart: 43 -> 40, of which waited for: 19 -> 22; matrix products, arithmetic and copies ran while one was open for 0% -> 0% of each run, Pallas kernels for 12% -> 12%
where the time goes in v2:
time: 106 us
  starting transfers between devices  44.9 us (42%)
  waiting for transfers between devices  39.4 us (37%)
  Pallas kernels  19.2 us (18%)
  local copies, waits for them, and re-layouts  1.17 us (1%)
    ppermute x24, waiting for transfers between devices, shift_perm(): lax.ppermute(x, axis, [(i, (i + shift) % count) for i in range(count)])  29.2 us
    ppermute x24, starting transfers between devices, shift_perm(): lax.ppermute(x, axis, [(i, (i + shift) % count) for i in range(count)])  26.8 us
    pallas_call x26, Pallas kernels, call(): pl.pallas_call(run, out_shape=[jax.ShapeDtypeStruct(s, d) for s, d in out...  19.2 us
    ppermute x12, starting transfers between devices, depth_perm(): lax.ppermute(x, 'col', [(i, i ^ 2 * depth_mask(t, i & 1, count // 2)) for...  17.8 us
    ppermute x12, waiting for transfers between devices, depth_perm(): lax.ppermute(x, 'col', [(i, i ^ 2 * depth_mask(t, i & 1, count // 2)) for...  6.16 us
    ppermute x4, waiting for transfers between devices, partner_perm(): return lax.ppermute(x, 'col', [(i, i ^ 1) for i in range(count)])  4.07 us
  transfers between devices with their start and end apart: 40, of which 22 were waited for; matrix products, arithmetic and copies ran while one was open for 0% of the time, Pallas kernels for 12%

profile of v2, /device:TPU:0, one launch (start us, length us, event | category | flops | bytes accessed | tf_op | source)
XLA Modules:
  0.0 105.7 jit_solution(4055799004697342197)
XLA Ops:
  2.2 4.5 %collective-permute-start.3 = (f32[8,768]{1,0:T(8,128)S(1)}, f32[8,768]{1,0:T(8,128)S(1)}, u32[]{:S(2)}, u32[]{:S(2)}) collective-permute-start(f32[8,768]{1,0:T(8,128)S(1)} %get-tuple-element.59), channel_id=1, source_target_pairs={{0,7},{1,0},{2,1},{3,2},{4,3},{5,4},{6,5},{7,6},{8,15},{9,8},{10,9... | collective-permute-start | bytes 73736 | tf_op jit(solution)/shard_map/ppermute | solution.py:73
  6.7 1.5 %collective-permute-start = (f32[24,128]{1,0:T(8,128)S(1)}, f32[24,128]{1,0:T(8,128)S(1)}, u32[]{:S(2)}, u32[]{:S(2)}) collective-permute-start(f32[24,128]{1,0:T(8,128)S(1)} %get-tuple-element.57), channel_id=1, source_target_pairs={{0,8},{8,16},{16,24},{24,0},{1,9},{9,17},{17,25},{25,1},{2,10},{10... | collective-permute-start | bytes 36872 | tf_op jit(solution)/shard_map/ppermute | solution.py:73
  8.2 1.4 %collective-permute-start.1 = (f32[24,128]{1,0:T(8,128)S(1)}, f32[24,128]{1,0:T(8,128)S(1)}, u32[]{:S(2)}, u32[]{:S(2)}) collective-permute-start(f32[24,128]{1,0:T(8,128)S(1)} %get-tuple-element.58), channel_id=1, source_target_pairs={{0,24},{8,0},{16,8},{24,16},{1,25},{9,1},{17,9},{25,17},{2,26},{10... | collective-permute-start | bytes 36872 | tf_op jit(solution)/shard_map/ppermute | solution.py:73
  13.5 3.3 %collective-permute-start.4 = (f32[192,128]{1,0:T(8,128)S(1)}, f32[192,128]{1,0:T(8,128)S(1)}, u32[]{:S(2)}, u32[]{:S(2)}) collective-permute-start(f32[192,128]{1,0:T(8,128)S(1)} %shard_map.96.refs_7_.refs_0_), channel_id=1, source_target_pairs={{0,2},{1,7},{2,0},{3,5},{4,6},{5,3},{6,4},{7,1},{8,10},{9,15},{10,... | collective-permute-start | bytes 294920 | tf_op jit(solution)/shard_map/ppermute | solution.py:82
  16.9 1.9 %shard_map.98 = (bf16[256,512]{1,0:T(8,128)(2,1)S(1)}, bf16[256,512]{1,0:T(8,128)(2,1)S(1)}, bf16[256,512]{1,0:T(8,128)(2,1)S(1)}, bf16[256,512]{1,0:T(8,128)(2,...) custom-call(s32[2]{0:T(128)S(1)} %pad_add_fusion.refs_0_), custom_call_target="tpu_custom_call" | custom-call | bytes 2228232 | tf_op jit(solution)/shard_map/pallas_call | solution.py:30
  19.6 1.8 %shard_map.97 = (f32[3,4,64,128]{3,2,1,0:T(8,128)S(1)}, f32[8,768]{1,0:T(8,128)S(1)}, f32[24,128]{1,0:T(8,128)S(1)}, f32[24,128]{1,0:T(8,128)S(1)}) custom-call(f32[3,4,64,128]{3,2,1,0:T(8,128)S(1)} %copy-done.4, f32[3,4,64,128]{3,2,1,0:T(8,128)S(1)} %shard_map.94.refs_1_, f32[4,64,128]{2,1,0:T(8,128)S(1)} %copy-done.2, ...), custom_call_target="tpu_custom_call" | custom-call | bytes 1531904 | tf_op jit(solution)/shard_map/pallas_call | solution.py:30
  21.4 1.8 %collective-permute-done.5.refs_2_ = f32[192,128]{1,0:T(8,128)S(1)} collective-permute-done((f32[192,128]{1,0:T(8,128)S(1)}, f32[192,128]{1,0:T(8,128)S(1)}, u32[]{:S(2)}, u32[]{:S(2)}) %collective-permute-start.5) | collective-permute-done | bytes 98336 | tf_op jit(solution)/shard_map/ppermute | solution.py:82
  25.2 2.4 %collective-permute-start.8 = (f32[120,128]{1,0:T(8,128)S(1)}, f32[120,128]{1,0:T(8,128)S(1)}, u32[]{:S(2)}, u32[]{:S(2)}) collective-permute-start(f32[120,128]{1,0:T(8,128)S(1)} %get-tuple-element.69), channel_id=1, source_target_pairs={{0,8},{8,16},{16,24},{24,0},{1,9},{9,17},{17,25},{25,1},{2,10},{10... | collective-permute-start | bytes 184328 | tf_op jit(solution)/shard_map/ppermute | solution.py:73
  28.2 1.5 %collective-permute-start.16 = (f32[96,128]{1,0:T(8,128)S(1)}, f32[96,128]{1,0:T(8,128)S(1)}, u32[]{:S(2)}, u32[]{:S(2)}) collective-permute-start(f32[96,128]{1,0:T(8,128)S(1)} %get-tuple-element.78), channel_id=1, source_target_pairs={{0,16},{8,24},{16,0},{24,8},{1,17},{9,25},{17,1},{25,9},{2,18},{10... | collective-permute-start | bytes 147464 | tf_op jit(solution)/shard_map/ppermute | solution.py:73
  29.7 2.5 %collective-permute-done.16.refs_3_ = f32[96,128]{1,0:T(8,128)S(1)} collective-permute-done((f32[96,128]{1,0:T(8,128)S(1)}, f32[96,128]{1,0:T(8,128)S(1)}, u32[]{:S(2)}, u32[]{:S(2)}) %collective-permute-start.16) | collective-permute-done | bytes 49184 | tf_op jit(solution)/shard_map/ppermute | solution.py:73
  33.3 2.1 %collective-permute-start.17 = (f32[104,128]{1,0:T(8,128)S(1)}, f32[104,128]{1,0:T(8,128)S(1)}, u32[]{:S(2)}, u32[]{:S(2)}) collective-permute-start(f32[104,128]{1,0:T(8,128)S(1)} %get-tuple-element.82), channel_id=1, source_target_pairs={{0,24},{8,0},{16,8},{24,16},{1,25},{9,1},{17,9},{25,17},{2,26},{10... | collective-permute-start | bytes 159752 | tf_op jit(solution)/shard_map/ppermute | solution.py:73
  37.5 1.5 %collective-permute-done.11.refs_7_ = f32[8,768]{1,0:T(8,128)S(1)} collective-permute-done((f32[8,768]{1,0:T(8,128)S(1)}, f32[8,768]{1,0:T(8,128)S(1)}, u32[]{:S(2)}, u32[]{:S(2)}) %collective-permute-start.11) | collective-permute-done | bytes 24608 | tf_op jit(solution)/shard_map/ppermute | solution.py:73
  39.0 3.5 %collective-permute-done.10.refs_6_ = f32[8,768]{1,0:T(8,128)S(1)} collective-permute-done((f32[8,768]{1,0:T(8,128)S(1)}, f32[8,768]{1,0:T(8,128)S(1)}, u32[]{:S(2)}, u32[]{:S(2)}) %collective-permute-start.10) | collective-permute-done | bytes 24608 | tf_op jit(solution)/shard_map/ppermute | solution.py:73
  42.6 2.3 %shard_map.103 = (f32[6,4,64,128]{3,2,1,0:T(8,128)S(1)}, f32[8,768]{1,0:T(8,128)S(1)}, f32[24,128]{1,0:T(8,128)S(1)}, f32[24,128]{1,0:T(8,128)S(1)}) custom-call(f32[6,4,64,128]{3,2,1,0:T(8,128)S(1)} %copy-done.1, f32[3,4,64,128]{3,2,1,0:T(8,128)S(1)} %get-tuple-element.60.refs_1_.refs_0_, f32[4,64,128]{2,1,0:T(8,128)S(1)} %copy-done.6, ...), custom_call_target="tpu_custom_call" | custom-call | bytes 2449408 | tf_op jit(solution)/shard_map/pallas_call | solution.py:30
  47.7 3.8 %collective-permute-start.23 = (f32[208,128]{1,0:T(8,128)S(1)}, f32[208,128]{1,0:T(8,128)S(1)}, u32[]{:S(2)}, u32[]{:S(2)}) collective-permute-start(f32[208,128]{1,0:T(8,128)S(1)} %get-tuple-element.90), channel_id=1, source_target_pairs={{0,6},{1,3},{2,4},{3,1},{4,2},{5,7},{6,0},{7,5},{8,14},{9,11},{10,... | collective-permute-start | bytes 319496 | tf_op jit(solution)/shard_map/ppermute | solution.py:82
  51.5 1.5 %collective-permute-start.12 = (f32[24,128]{1,0:T(8,128)S(1)}, f32[24,128]{1,0:T(8,128)S(1)}, u32[]{:S(2)}, u32[]{:S(2)}) collective-permute-start(f32[24,128]{1,0:T(8,128)S(1)} %get-tuple-element.73), channel_id=1, source_target_pairs={{0,8},{8,16},{16,24},{24,0},{1,9},{9,17},{17,25},{25,1},{2,10},{10... | collective-permute-start | bytes 36872 | tf_op jit(solution)/shard_map/ppermute | solution.py:73
  52.9 1.5 %collective-permute-start.13 = (f32[24,128]{1,0:T(8,128)S(1)}, f32[24,128]{1,0:T(8,128)S(1)}, u32[]{:S(2)}, u32[]{:S(2)}) collective-permute-start(f32[24,128]{1,0:T(8,128)S(1)} %get-tuple-element.74.refs_4_), channel_id=1, source_target_pairs={{0,24},{8,0},{16,8},{24,16},{1,25},{9,1},{17,9},{25,17},{2,26},{10... | collective-permute-start | bytes 36872 | tf_op jit(solution)/shard_map/ppermute | solution.py:73
  54.4 1.7 %collective-permute-done.12.refs_3_ = f32[24,128]{1,0:T(8,128)S(1)} collective-permute-done((f32[24,128]{1,0:T(8,128)S(1)}, f32[24,128]{1,0:T(8,128)S(1)}, u32[]{:S(2)}, u32[]{:S(2)}) %collective-permute-start.12) | collective-permute-done | bytes 12320 | tf_op jit(solution)/shard_map/ppermute | solution.py:73
  57.6 4.1 %collective-permute-done.14.refs_5_ = f32[8,768]{1,0:T(8,128)S(1)} collective-permute-done((f32[8,768]{1,0:T(8,128)S(1)}, f32[8,768]{1,0:T(8,128)S(1)}, u32[]{:S(2)}, u32[]{:S(2)}) %collective-permute-start.14) | collective-permute-done | bytes 24608 | tf_op jit(solution)/shard_map/ppermute | solution.py:73
  63.5 4.3 %collective-permute-start.24 = (f32[192,128]{1,0:T(8,128)S(1)}, f32[192,128]{1,0:T(8,128)S(1)}, u32[]{:S(2)}, u32[]{:S(2)}) collective-permute-start(f32[192,128]{1,0:T(8,128)S(1)} %get-tuple-element.92.refs_3_.refs_0_), channel_id=1, source_target_pairs={{0,2},{1,7},{2,0},{3,5},{4,6},{5,3},{6,4},{7,1},{8,10},{9,15},{10,... | collective-permute-start | bytes 294920 | tf_op jit(solution)/shard_map/ppermute | solution.py:82
  70.0 3.0 %collective-permute-done.25.refs_2_ = f32[192,128]{1,0:T(8,128)S(1)} collective-permute-done((f32[192,128]{1,0:T(8,128)S(1)}, f32[192,128]{1,0:T(8,128)S(1)}, u32[]{:S(2)}, u32[]{:S(2)}) %collective-permute-start.25) | collective-permute-done | bytes 98336 | tf_op jit(solution)/shard_map/ppermute | solution.py:82
  76.0 2.0 %collective-permute-start.29 = (f32[120,128]{1,0:T(8,128)S(1)}, f32[120,128]{1,0:T(8,128)S(1)}, u32[]{:S(2)}, u32[]{:S(2)}) collective-permute-start(f32[120,128]{1,0:T(8,128)S(1)} %get-tuple-element.97), channel_id=1, source_target_pairs={{0,24},{8,0},{16,8},{24,16},{1,25},{9,1},{17,9},{25,17},{2,26},{10... | collective-permute-start | bytes 184328 | tf_op jit(solution)/shard_map/ppermute | solution.py:73
  79.0 3.1 %collective-permute-done.32.refs_2_ = f32[96,128]{1,0:T(8,128)S(1)} collective-permute-done((f32[96,128]{1,0:T(8,128)S(1)}, f32[96,128]{1,0:T(8,128)S(1)}, u32[]{:S(2)}, u32[]{:S(2)}) %collective-permute-start.32) | collective-permute-done | bytes 49184 | tf_op jit(solution)/shard_map/ppermute | solution.py:73
  82.1 1.5 %shard_map.115 = (f32[2,3,2,32,256]{4,3,2,1,0:T(8,128)}, f32[96,128]{1,0:T(8,128)S(1)}, f32[96,128]{1,0:T(8,128)S(1)}, f32[96,128]{1,0:T(8,128)S(1)}, f32[96,128]{1,0:T(8,128)S(1)}) custom-call(f32[96,128]{1,0:T(8,128)S(1)} %get-tuple-element.99.refs_0_, f32[120,128]{1,0:T(8,128)S(1)} %collective-permute-done.28.refs_4_.refs_1_, ...), custom_call_target="tpu_custom_call" | custom-call | bytes 2449408 | tf_op jit(solution)/shard_map/pallas_call | solution.py:30
  83.6 1.5 %collective-permute-start.33 = (f32[96,128]{1,0:T(8,128)S(1)}, f32[96,128]{1,0:T(8,128)S(1)}, u32[]{:S(2)}, u32[]{:S(2)}) collective-permute-start(f32[96,128]{1,0:T(8,128)S(1)} %get-tuple-element.103), channel_id=1, source_target_pairs={{0,24},{8,0},{16,8},{24,16},{1,25},{9,1},{17,9},{25,17},{2,26},{10... | collective-permute-start | bytes 147464 | tf_op jit(solution)/shard_map/ppermute | solution.py:73
  86.6 1.5 %collective-permute-done.33.refs_1_ = f32[96,128]{1,0:T(8,128)S(1)} collective-permute-done((f32[96,128]{1,0:T(8,128)S(1)}, f32[96,128]{1,0:T(8,128)S(1)}, u32[]{:S(2)}, u32[]{:S(2)}) %collective-permute-start.33) | collective-permute-done | bytes 49184 | tf_op jit(solution)/shard_map/ppermute | solution.py:73
  89.2 1.7 %collective-permute-done.35.refs_3_ = f32[96,128]{1,0:T(8,128)S(1)} collective-permute-done((f32[96,128]{1,0:T(8,128)S(1)}, f32[96,128]{1,0:T(8,128)S(1)}, u32[]{:S(2)}, u32[]{:S(2)}) %collective-permute-start.35) | collective-permute-done | bytes 49184 | tf_op jit(solution)/shard_map/ppermute | solution.py:73
  93.0 2.4 %collective-permute-start.38 = (f32[192,128]{1,0:T(8,128)S(1)}, f32[192,128]{1,0:T(8,128)S(1)}, u32[]{:S(2)}, u32[]{:S(2)}) collective-permute-start(f32[192,128]{1,0:T(8,128)S(1)} %get-tuple-element.108), channel_id=1, source_target_pairs={{0,4},{1,5},{2,6},{3,7},{4,0},{5,1},{6,2},{7,3},{8,12},{9,13},{10,... | collective-permute-start | bytes 294920 | tf_op jit(solution)/shard_map/ppermute | solution.py:82
  95.3 2.0 %collective-permute-start.39 = (f32[192,128]{1,0:T(8,128)S(1)}, f32[192,128]{1,0:T(8,128)S(1)}, u32[]{:S(2)}, u32[]{:S(2)}) collective-permute-start(f32[192,128]{1,0:T(8,128)S(1)} %get-tuple-element.109), channel_id=1, source_target_pairs={{0,6},{1,3},{2,4},{3,1},{4,2},{5,7},{6,0},{7,5},{8,14},{9,11},{10,... | collective-permute-start | bytes 294920 | tf_op jit(solution)/shard_map/ppermute | solution.py:82
  98.1 2.9 %collective-permute-done.31.refs_7_ = f32[8,768]{1,0:T(8,128)S(1)} collective-permute-done((f32[8,768]{1,0:T(8,128)S(1)}, f32[8,768]{1,0:T(8,128)S(1)}, u32[]{:S(2)}, u32[]{:S(2)}) %collective-permute-start.31) | collective-permute-done | bytes 24608 | tf_op jit(solution)/shard_map/ppermute | solution.py:73
  101.0 2.3 %collective-permute-done.30.refs_6_ = f32[8,768]{1,0:T(8,128)S(1)} collective-permute-done((f32[8,768]{1,0:T(8,128)S(1)}, f32[8,768]{1,0:T(8,128)S(1)}, u32[]{:S(2)}, u32[]{:S(2)}) %collective-permute-start.30) | collective-permute-done | bytes 24608 | tf_op jit(solution)/shard_map/ppermute | solution.py:73
  103.3 1.4 %shard_map.114.refs_0_ = f32[6,4,64,128]{3,2,1,0:T(8,128)S(1)} custom-call(f32[6,4,64,128]{3,2,1,0:T(8,128)S(1)} %get-tuple-element.72.refs_1_.refs_0_, f32[3,4,64,128]{3,2,1,0:T(8,128)S(1)} %copy-done.8, f32[4,64,128]{2,1,0:T(8,128)S(1)} %copy-done.6, f32[4,64,128]{2,1,0:T(8,128)S(1)} %copy-done.7, f32[120,128]{1,0:T(8,128)S(1)} %collective-permute-done.28.refs_4_.refs_1_, ...), custom_call_target="tpu_custom_call" | custom-call | bytes 2506752 | tf_op jit(solution)/shard_map/pallas_call | solution.py:30
  (94 shorter events, 30.5 us)
Async XLA Ops:
  2.2 9.7 %collective-permute-start.3 = (f32[8,768]{1,0:T(8,128)S(1)}, f32[8,768]{1,0:T(8,128)S(1)}, u32[]{:S(2)}, u32[]{:S(2)}) collective-permute-start(f32[8,768]{1,0:T(8,128)S(1)} %get-tuple-element.59), channel_id=1, source_target_pairs={{0,7},{1,0},{2,1},{3,2},{4,3},{5,4},{6,5},{7,6},{8,15},{9,8},{10,9... | collective-permute-start | bytes 73736 | tf_op jit(solution)/shard_map/ppermute | solution.py:73
  6.7 5.2 %collective-permute-start.2 = (f32[8,768]{1,0:T(8,128)S(1)}, f32[8,768]{1,0:T(8,128)S(1)}, u32[]{:S(2)}, u32[]{:S(2)}) collective-permute-start(f32[8,768]{1,0:T(8,128)S(1)} %get-tuple-element.59), channel_id=1, source_target_pairs={{0,1},{1,2},{2,3},{3,4},{4,5},{5,6},{6,7},{7,0},{8,9},{9,10},{10,1... | collective-permute-start | bytes 73736 | tf_op jit(solution)/shard_map/ppermute | solution.py:73
  6.7 4.6 %collective-permute-start = (f32[24,128]{1,0:T(8,128)S(1)}, f32[24,128]{1,0:T(8,128)S(1)}, u32[]{:S(2)}, u32[]{:S(2)}) collective-permute-start(f32[24,128]{1,0:T(8,128)S(1)} %get-tuple-element.57), channel_id=1, source_target_pairs={{0,8},{8,16},{16,24},{24,0},{1,9},{9,17},{17,25},{25,1},{2,10},{10... | collective-permute-start | bytes 36872 | tf_op jit(solution)/shard_map/ppermute | solution.py:73
  8.2 3.7 %collective-permute-start.1 = (f32[24,128]{1,0:T(8,128)S(1)}, f32[24,128]{1,0:T(8,128)S(1)}, u32[]{:S(2)}, u32[]{:S(2)}) collective-permute-start(f32[24,128]{1,0:T(8,128)S(1)} %get-tuple-element.58), channel_id=1, source_target_pairs={{0,24},{8,0},{16,8},{24,16},{1,25},{9,1},{17,9},{25,17},{2,26},{10... | collective-permute-start | bytes 36872 | tf_op jit(solution)/shard_map/ppermute | solution.py:73
  12.3 9.1 %collective-permute-start.6 = (f32[192,128]{1,0:T(8,128)S(1)}, f32[192,128]{1,0:T(8,128)S(1)}, u32[]{:S(2)}, u32[]{:S(2)}) collective-permute-start(f32[192,128]{1,0:T(8,128)S(1)} %shard_map.96.refs_7_.refs_0_), channel_id=1, source_target_pairs={{0,6},{1,3},{2,4},{3,1},{4,2},{5,7},{6,0},{7,5},{8,14},{9,11},{10,... | collective-permute-start | bytes 294920 | tf_op jit(solution)/shard_map/ppermute | solution.py:82
  13.5 9.8 %collective-permute-start.5 = (f32[192,128]{1,0:T(8,128)S(1)}, f32[192,128]{1,0:T(8,128)S(1)}, u32[]{:S(2)}, u32[]{:S(2)}) collective-permute-start(f32[192,128]{1,0:T(8,128)S(1)} %shard_map.96.refs_7_.refs_0_), channel_id=1, source_target_pairs={{0,4},{1,5},{2,6},{3,7},{4,0},{5,1},{6,2},{7,3},{8,12},{9,13},{10,... | collective-permute-start | bytes 294920 | tf_op jit(solution)/shard_map/ppermute | solution.py:82
  13.5 9.8 %collective-permute-start.4 = (f32[192,128]{1,0:T(8,128)S(1)}, f32[192,128]{1,0:T(8,128)S(1)}, u32[]{:S(2)}, u32[]{:S(2)}) collective-permute-start(f32[192,128]{1,0:T(8,128)S(1)} %shard_map.96.refs_7_.refs_0_), channel_id=1, source_target_pairs={{0,2},{1,7},{2,0},{3,5},{4,6},{5,3},{6,4},{7,1},{8,10},{9,15},{10,... | collective-permute-start | bytes 294920 | tf_op jit(solution)/shard_map/ppermute | solution.py:82
  25.2 7.1 %collective-permute-start.8 = (f32[120,128]{1,0:T(8,128)S(1)}, f32[120,128]{1,0:T(8,128)S(1)}, u32[]{:S(2)}, u32[]{:S(2)}) collective-permute-start(f32[120,128]{1,0:T(8,128)S(1)} %get-tuple-element.69), channel_id=1, source_target_pairs={{0,8},{8,16},{16,24},{24,0},{1,9},{9,17},{17,25},{25,1},{2,10},{10... | collective-permute-start | bytes 184328 | tf_op jit(solution)/shard_map/ppermute | solution.py:73
  27.7 4.6 %collective-permute-start.9 = (f32[120,128]{1,0:T(8,128)S(1)}, f32[120,128]{1,0:T(8,128)S(1)}, u32[]{:S(2)}, u32[]{:S(2)}) collective-permute-start(f32[120,128]{1,0:T(8,128)S(1)} %get-tuple-element.70), channel_id=1, source_target_pairs={{0,24},{8,0},{16,8},{24,16},{1,25},{9,1},{17,9},{25,17},{2,26},{10... | collective-permute-start | bytes 184328 | tf_op jit(solution)/shard_map/ppermute | solution.py:73
  28.2 4.1 %collective-permute-start.16 = (f32[96,128]{1,0:T(8,128)S(1)}, f32[96,128]{1,0:T(8,128)S(1)}, u32[]{:S(2)}, u32[]{:S(2)}) collective-permute-start(f32[96,128]{1,0:T(8,128)S(1)} %get-tuple-element.78), channel_id=1, source_target_pairs={{0,16},{8,24},{16,0},{24,8},{1,17},{9,25},{17,1},{25,9},{2,18},{10... | collective-permute-start | bytes 147464 | tf_op jit(solution)/shard_map/ppermute | solution.py:73
  33.3 11.5 %collective-permute-start.17 = (f32[104,128]{1,0:T(8,128)S(1)}, f32[104,128]{1,0:T(8,128)S(1)}, u32[]{:S(2)}, u32[]{:S(2)}) collective-permute-start(f32[104,128]{1,0:T(8,128)S(1)} %get-tuple-element.82), channel_id=1, source_target_pairs={{0,24},{8,0},{16,8},{24,16},{1,25},{9,1},{17,9},{25,17},{2,26},{10... | collective-permute-start | bytes 159752 | tf_op jit(solution)/shard_map/ppermute | solution.py:73
  35.5 9.4 %collective-permute-start.18 = (f32[104,128]{1,0:T(8,128)S(1)}, f32[104,128]{1,0:T(8,128)S(1)}, u32[]{:S(2)}, u32[]{:S(2)}) collective-permute-start(f32[104,128]{1,0:T(8,128)S(1)} %get-tuple-element.83), channel_id=1, source_target_pairs={{0,16},{8,24},{16,0},{24,8},{1,17},{9,25},{17,1},{25,9},{2,18},{10... | collective-permute-start | bytes 159752 | tf_op jit(solution)/shard_map/ppermute | solution.py:73
  36.6 8.3 %collective-permute-start.19 = (f32[104,128]{1,0:T(8,128)S(1)}, f32[104,128]{1,0:T(8,128)S(1)}, u32[]{:S(2)}, u32[]{:S(2)}) collective-permute-start(f32[104,128]{1,0:T(8,128)S(1)} %get-tuple-element.84), channel_id=1, source_target_pairs={{0,8},{8,16},{16,24},{24,0},{1,9},{9,17},{17,25},{25,1},{2,10},{10... | collective-permute-start | bytes 159752 | tf_op jit(solution)/shard_map/ppermute | solution.py:73
  37.5 5.0 %collective-permute-start.10 = (f32[8,768]{1,0:T(8,128)S(1)}, f32[8,768]{1,0:T(8,128)S(1)}, u32[]{:S(2)}, u32[]{:S(2)}) collective-permute-start(f32[8,768]{1,0:T(8,128)S(1)} %get-tuple-element.71), channel_id=1, source_target_pairs={{0,1},{1,2},{2,3},{3,4},{4,5},{5,6},{6,7},{7,0},{8,9},{9,10},{10,1... | collective-permute-start | bytes 73736 | tf_op jit(solution)/shard_map/ppermute | solution.py:73
  47.0 16.1 %collective-permute-start.21 = (f32[208,128]{1,0:T(8,128)S(1)}, f32[208,128]{1,0:T(8,128)S(1)}, u32[]{:S(2)}, u32[]{:S(2)}) collective-permute-start(f32[208,128]{1,0:T(8,128)S(1)} %get-tuple-element.88), channel_id=1, source_target_pairs={{0,2},{1,7},{2,0},{3,5},{4,6},{5,3},{6,4},{7,1},{8,10},{9,15},{10,... | collective-permute-start | bytes 319496 | tf_op jit(solution)/shard_map/ppermute | solution.py:82
  47.1 16.0 %collective-permute-start.22 = (f32[208,128]{1,0:T(8,128)S(1)}, f32[208,128]{1,0:T(8,128)S(1)}, u32[]{:S(2)}, u32[]{:S(2)}) collective-permute-start(f32[208,128]{1,0:T(8,128)S(1)} %get-tuple-element.89), channel_id=1, source_target_pairs={{0,4},{1,5},{2,6},{3,7},{4,0},{5,1},{6,2},{7,3},{8,12},{9,13},{10,... | collective-permute-start | bytes 319496 | tf_op jit(solution)/shard_map/ppermute | solution.py:82
  47.7 15.4 %collective-permute-start.23 = (f32[208,128]{1,0:T(8,128)S(1)}, f32[208,128]{1,0:T(8,128)S(1)}, u32[]{:S(2)}, u32[]{:S(2)}) collective-permute-start(f32[208,128]{1,0:T(8,128)S(1)} %get-tuple-element.90), channel_id=1, source_target_pairs={{0,6},{1,3},{2,4},{3,1},{4,2},{5,7},{6,0},{7,5},{8,14},{9,11},{10,... | collective-permute-start | bytes 319496 | tf_op jit(solution)/shard_map/ppermute | solution.py:82
  51.5 4.6 %collective-permute-start.12 = (f32[24,128]{1,0:T(8,128)S(1)}, f32[24,128]{1,0:T(8,128)S(1)}, u32[]{:S(2)}, u32[]{:S(2)}) collective-permute-start(f32[24,128]{1,0:T(8,128)S(1)} %get-tuple-element.73), channel_id=1, source_target_pairs={{0,8},{8,16},{16,24},{24,0},{1,9},{9,17},{17,25},{25,1},{2,10},{10... | collective-permute-start | bytes 36872 | tf_op jit(solution)/shard_map/ppermute | solution.py:73
  56.6 5.1 %collective-permute-start.14 = (f32[8,768]{1,0:T(8,128)S(1)}, f32[8,768]{1,0:T(8,128)S(1)}, u32[]{:S(2)}, u32[]{:S(2)}) collective-permute-start(f32[8,768]{1,0:T(8,128)S(1)} %get-tuple-element.75), channel_id=1, source_target_pairs={{0,1},{1,2},{2,3},{3,4},{4,5},{5,6},{6,7},{7,0},{8,9},{9,10},{10,1... | collective-permute-start | bytes 73736 | tf_op jit(solution)/shard_map/ppermute | solution.py:73
  63.4 6.7 %collective-permute-start.26 = (f32[192,128]{1,0:T(8,128)S(1)}, f32[192,128]{1,0:T(8,128)S(1)}, u32[]{:S(2)}, u32[]{:S(2)}) collective-permute-start(f32[192,128]{1,0:T(8,128)S(1)} %get-tuple-element.92.refs_3_.refs_0_), channel_id=1, source_target_pairs={{0,6},{1,3},{2,4},{3,1},{4,2},{5,7},{6,0},{7,5},{8,14},{9,11},{10,... | collective-permute-start | bytes 294920 | tf_op jit(solution)/shard_map/ppermute | solution.py:82
  63.5 9.5 %collective-permute-start.25 = (f32[192,128]{1,0:T(8,128)S(1)}, f32[192,128]{1,0:T(8,128)S(1)}, u32[]{:S(2)}, u32[]{:S(2)}) collective-permute-start(f32[192,128]{1,0:T(8,128)S(1)} %get-tuple-element.92.refs_3_.refs_0_), channel_id=1, source_target_pairs={{0,4},{1,5},{2,6},{3,7},{4,0},{5,1},{6,2},{7,3},{8,12},{9,13},{10,... | collective-permute-start | bytes 294920 | tf_op jit(solution)/shard_map/ppermute | solution.py:82
  63.5 9.5 %collective-permute-start.24 = (f32[192,128]{1,0:T(8,128)S(1)}, f32[192,128]{1,0:T(8,128)S(1)}, u32[]{:S(2)}, u32[]{:S(2)}) collective-permute-start(f32[192,128]{1,0:T(8,128)S(1)} %get-tuple-element.92.refs_3_.refs_0_), channel_id=1, source_target_pairs={{0,2},{1,7},{2,0},{3,5},{4,6},{5,3},{6,4},{7,1},{8,10},{9,15},{10,... | collective-permute-start | bytes 294920 | tf_op jit(solution)/shard_map/ppermute | solution.py:82
  75.0 7.1 %collective-permute-start.28 = (f32[120,128]{1,0:T(8,128)S(1)}, f32[120,128]{1,0:T(8,128)S(1)}, u32[]{:S(2)}, u32[]{:S(2)}) collective-permute-start(f32[120,128]{1,0:T(8,128)S(1)} %get-tuple-element.96), channel_id=1, source_target_pairs={{0,8},{8,16},{16,24},{24,0},{1,9},{9,17},{17,25},{25,1},{2,10},{10... | collective-permute-start | bytes 184328 | tf_op jit(solution)/shard_map/ppermute | solution.py:73
  76.0 6.1 %collective-permute-start.29 = (f32[120,128]{1,0:T(8,128)S(1)}, f32[120,128]{1,0:T(8,128)S(1)}, u32[]{:S(2)}, u32[]{:S(2)}) collective-permute-start(f32[120,128]{1,0:T(8,128)S(1)} %get-tuple-element.97), channel_id=1, source_target_pairs={{0,24},{8,0},{16,8},{24,16},{1,25},{9,1},{17,9},{25,17},{2,26},{10... | collective-permute-start | bytes 184328 | tf_op jit(solution)/shard_map/ppermute | solution.py:73
  78.0 4.1 %collective-permute-start.32 = (f32[96,128]{1,0:T(8,128)S(1)}, f32[96,128]{1,0:T(8,128)S(1)}, u32[]{:S(2)}, u32[]{:S(2)}) collective-permute-start(f32[96,128]{1,0:T(8,128)S(1)} %get-tuple-element.100), channel_id=1, source_target_pairs={{0,16},{8,24},{16,0},{24,8},{1,17},{9,25},{17,1},{25,9},{2,18},{10... | collective-permute-start | bytes 147464 | tf_op jit(solution)/shard_map/ppermute | solution.py:73
  83.6 4.5 %collective-permute-start.33 = (f32[96,128]{1,0:T(8,128)S(1)}, f32[96,128]{1,0:T(8,128)S(1)}, u32[]{:S(2)}, u32[]{:S(2)}) collective-permute-start(f32[96,128]{1,0:T(8,128)S(1)} %get-tuple-element.103), channel_id=1, source_target_pairs={{0,24},{8,0},{16,8},{24,16},{1,25},{9,1},{17,9},{25,17},{2,26},{10... | collective-permute-start | bytes 147464 | tf_op jit(solution)/shard_map/ppermute | solution.py:73
  85.1 4.1 %collective-permute-start.34 = (f32[96,128]{1,0:T(8,128)S(1)}, f32[96,128]{1,0:T(8,128)S(1)}, u32[]{:S(2)}, u32[]{:S(2)}) collective-permute-start(f32[96,128]{1,0:T(8,128)S(1)} %get-tuple-element.104), channel_id=1, source_target_pairs={{0,16},{8,24},{16,0},{24,8},{1,17},{9,25},{17,1},{25,9},{2,18},{10... | collective-permute-start | bytes 147464 | tf_op jit(solution)/shard_map/ppermute | solution.py:73
  85.9 5.0 %collective-permute-start.35 = (f32[96,128]{1,0:T(8,128)S(1)}, f32[96,128]{1,0:T(8,128)S(1)}, u32[]{:S(2)}, u32[]{:S(2)}) collective-permute-start(f32[96,128]{1,0:T(8,128)S(1)} %get-tuple-element.105), channel_id=1, source_target_pairs={{0,8},{8,16},{16,24},{24,0},{1,9},{9,17},{17,25},{25,1},{2,10},{10... | collective-permute-start | bytes 147464 | tf_op jit(solution)/shard_map/ppermute | solution.py:73
  92.8 11.9 %collective-permute-start.37 = (f32[192,128]{1,0:T(8,128)S(1)}, f32[192,128]{1,0:T(8,128)S(1)}, u32[]{:S(2)}, u32[]{:S(2)}) collective-permute-start(f32[192,128]{1,0:T(8,128)S(1)} %get-tuple-element.107), channel_id=1, source_target_pairs={{0,2},{1,7},{2,0},{3,5},{4,6},{5,3},{6,4},{7,1},{8,10},{9,15},{10,... | collective-permute-start | bytes 294920 | tf_op jit(solution)/shard_map/ppermute | solution.py:82
  93.0 11.8 %collective-permute-start.38 = (f32[192,128]{1,0:T(8,128)S(1)}, f32[192,128]{1,0:T(8,128)S(1)}, u32[]{:S(2)}, u32[]{:S(2)}) collective-permute-start(f32[192,128]{1,0:T(8,128)S(1)} %get-tuple-element.108), channel_id=1, source_target_pairs={{0,4},{1,5},{2,6},{3,7},{4,0},{5,1},{6,2},{7,3},{8,12},{9,13},{10,... | collective-permute-start | bytes 294920 | tf_op jit(solution)/shard_map/ppermute | solution.py:82
  95.3 9.4 %collective-permute-start.39 = (f32[192,128]{1,0:T(8,128)S(1)}, f32[192,128]{1,0:T(8,128)S(1)}, u32[]{:S(2)}, u32[]{:S(2)}) collective-permute-start(f32[192,128]{1,0:T(8,128)S(1)} %get-tuple-element.109), channel_id=1, source_target_pairs={{0,6},{1,3},{2,4},{3,1},{4,2},{5,7},{6,0},{7,5},{8,14},{9,11},{10,... | collective-permute-start | bytes 294920 | tf_op jit(solution)/shard_map/ppermute | solution.py:82
  98.1 5.2 %collective-permute-start.30 = (f32[8,768]{1,0:T(8,128)S(1)}, f32[8,768]{1,0:T(8,128)S(1)}, u32[]{:S(2)}, u32[]{:S(2)}) collective-permute-start(f32[8,768]{1,0:T(8,128)S(1)} %get-tuple-element.98), channel_id=1, source_target_pairs={{0,1},{1,2},{2,3},{3,4},{4,5},{5,6},{6,7},{7,0},{8,9},{9,10},{10,1... | collective-permute-start | bytes 73736 | tf_op jit(solution)/shard_map/ppermute | solution.py:73
  (17 other events, 136.2 us)

commit v3 on v2

--- a/solution.py
+++ b/solution.py
@@ -214,7 +214,7 @@
     return value + jnp.where(gap == 2, FAR, 0.0) - jnp.where(gap == -2, FAR, 0.0)
 
 
-def outer_weights(yb):
+def outer_weights(yb, where_ref):
     line, lane = iota((8, yb), 0), iota((8, yb), 1)
     left_gap = jnp.where((line == 2) | (line == 3), line - 4 - lane, 99)
     right_gap = jnp.where(line < 2, yb + line - lane, 99)
@@ -223,7 +223,9 @@
         near = jnp.where(gap == 1, NEAR, 0.0) - jnp.where(gap == -1, NEAR, 0.0)
         return near + jnp.where(gap == 2, FAR, 0.0) - jnp.where(gap == -2, FAR, 0.0)
 
-    return value(left_gap), value(right_gap)
+    left, right = value(left_gap), value(right_gap)
+    odd = (where_ref[1] & 1) == 1
+    return jnp.where(odd, left, right), jnp.where(odd, right, left)
 
 
 def put_borders(planes, row_planes, col_planes, edge_ref, first_ref, last_ref):
@@ -246,11 +248,10 @@
     return NEAR * near + FAR * far
 
 
-def col_deriv(stacked, left, right):
+def col_deriv(stacked, partner, across, partner_w, across_w):
     yb = stacked.shape[1]
-    left_w, right_w = outer_weights(yb)
     inner = dot6(stacked, inner_weights(yb), NN)
-    return inner + (dot6(left.T, left_w, NN) + dot6(right.T, right_w, NN))
+    return inner + (dot6(partner.T, partner_w, NN) + dot6(across.T, across_w, NN))
 
 
 def depth_deriv(at, layer, layers):
@@ -291,7 +292,9 @@
 
 
 def exchange_edges(edge):
-    return shift_perm(edge, "col", 1), shift_perm(edge, "col", -1)
+    count = lax.axis_size("col")
+    across = [(i, (i + 1 if i & 1 else i - 1) % count) for i in range(count)]
+    return partner_perm(edge), lax.ppermute(edge, "col", across)
 
 
 def exchange(borders):
@@ -330,8 +333,8 @@
 def push_top(velocity, inner, buoyancy, halo):
     comps, layers, xb, yb = inner.shape
 
-    def body(v_ref, f_ref, b_ref, up, dn, lf, rt, top_ref):
-        left_w, right_w = outer_weights(yb)
+    def body(v_ref, f_ref, b_ref, up, dn, lf, rt, lw, rw, top_ref):
+        left_w, right_w = lw[...], rw[...]
         for comp in range(comps):
             j = comp * layers
             pair, lane = slice(2 * j, 2 * j + 2), slice(j * xb, (j + 1) * xb)
@@ -346,8 +349,8 @@
 def push_rest(velocity, inner, buoyancy, halo, top):
     comps, layers, xb, yb = inner.shape
 
-    def body(v_ref, f_ref, b_ref, up, dn, lf, rt, top_ref, nv_ref, edge, first, last):
-        left_w, right_w = outer_weights(yb)
+    def body(v_ref, f_ref, b_ref, up, dn, lf, rt, lw, rw, top_ref, nv_ref, edge, first, last):
+        left_w, right_w = lw[...], rw[...]
         along_y = dot6(lf[...].T, left_w, NN) + dot6(rt[...].T, right_w, NN)
         for comp in range(comps):
             nv_ref[comp, 0] = top_ref[comp * xb : (comp + 1) * xb, :]
@@ -368,11 +371,11 @@
 def push_velocity(velocity, stress, buoyancy, halo):
     comps, layers, xb, yb = velocity.shape
 
-    def body(v_ref, s_ref, b_ref, up, dn, lf, rt, nv_ref, pad):
+    def body(v_ref, s_ref, b_ref, up, dn, lf, rt, lw, rw, nv_ref, pad):
         stacked = jnp.concatenate(
             [s_ref[p, l] for p, l in plane_list(COL_PARTS, layers)], axis=0
         )
-        along_y = col_deriv(stacked, lf[...], rt[...])
+        along_y = col_deriv(stacked, lf[...], rt[...], lw[...], rw[...])
         for comp in range(comps):
             for layer in range(layers):
                 j = comp * layers + layer
@@ -391,15 +394,15 @@
 def push_stress(stress, velocity, lame, shear, halo, traction=None):
     comps, layers, xb, yb = velocity.shape
 
-    def body(s_ref, v_ref, l_ref, m_ref, up, dn, lf, rt, *refs):
+    def body(s_ref, v_ref, l_ref, m_ref, up, dn, lf, rt, lw, rw, *refs):
         stacked = jnp.concatenate(
             [v_ref[c, l] for c, l in plane_list(range(comps), layers)], axis=0
         )
         if traction is None:
             ns_ref, *outs, pad = refs
         else:
-            t_ref, ns_ref, pad = refs
-        along_y = col_deriv(stacked, lf[...], rt[...])
+            t_ref, ns_ref, face_ref, pad = refs
+        along_y = col_deriv(stacked, lf[...], rt[...], lw[...], rw[...])
         skip = up.shape[0] - 2 * comps * layers
         for layer in range(layers):
             gx, gy, gz = [], [], []
@@ -425,9 +428,13 @@
         if traction is None:
             rows, cols = plane_list(ROW_PARTS, layers), plane_list(COL_PARTS, layers)
             put_borders(lambda w: ns_ref[w[0], w[1]], rows, cols, *outs)
+        else:
+            for comp, part in enumerate(DEPTH_PARTS):
+                face_ref[comp * xb : (comp + 1) * xb, :] = ns_ref[part, 0]
 
     args = [stress, velocity, lame, shear, *halo] + ([] if traction is None else [traction])
-    outs = [(stress.shape, F32)] + (borders_shapes(layers, xb, yb) if traction is None else [])
+    outs = [(stress.shape, F32)]
+    outs += borders_shapes(layers, xb, yb) if traction is None else [((comps * xb, yb), F32)]
     new, *borders = call(
         body, outs, *args,
         scratch=[pltpu.VMEM((comps * layers, xb + 16, yb), F32)],
@@ -490,17 +497,39 @@
     return new, borders
 
 
-def add_traction(stress, pieces):
-    xb = stress.shape[2]
-
-    def body(s_ref, *refs):
-        *piece_refs, ns_ref = refs
-        total = total_of(piece_refs)
-        ns_ref[...] = s_ref[...]
-        for comp, part in enumerate(DEPTH_PARTS):
-            ns_ref[part, 0] = s_ref[part, 0] + total[comp * xb : (comp + 1) * xb]
-
-    return call(body, [(stress.shape, F32)], stress, *pieces)[0]
+def add_traction(stress, faces, pieces):
+    xb, yb = stress.shape[2:]
+    comps = len(DEPTH_PARTS)
+
+    def body(s_ref, f_ref, *refs):
+        *piece_refs, ns_ref, new_ref, sems = refs
+        new_ref[...] = f_ref[...] + total_of(piece_refs)
+        copies = [
+            pltpu.make_async_copy(
+                new_ref.at[pl.ds(comp * xb, xb)], ns_ref.at[part, 0], sems.at[comp]
+            )
+            for comp, part in enumerate(DEPTH_PARTS)
+        ]
+        for copy in copies:
+            copy.start()
+        for copy in copies:
+            copy.wait()
+
+    anywhere = pl.BlockSpec(memory_space=pl.ANY)
+    inside = pl.BlockSpec(memory_space=pltpu.VMEM)
+    return pl.pallas_call(
+        body,
+        name="traction",
+        out_shape=jax.ShapeDtypeStruct(stress.shape, F32),
+        in_specs=[anywhere] + [inside] * (1 + len(pieces)),
+        out_specs=anywhere,
+        scratch_shapes=[pltpu.VMEM((comps * xb, yb), F32), pltpu.SemaphoreType.DMA((comps,))],
+        input_output_aliases={0: 0},
+        compiler_params=pltpu.CompilerParams(vmem_limit_bytes=VMEM_LIMIT),
+        cost_estimate=pl.CostEstimate(
+            flops=0, bytes_accessed=8 * comps * xb * yb, transcendentals=0
+        ),
+    )(stress, faces, *pieces)
 
 
 def part_forward(blocks, table, dims, after=()):
@@ -559,14 +588,8 @@
         for comp in range(comps):
             line = slice(comp * kyb, (comp + 1) * kyb)
             now = (spec[line, :nx], spec[line, nx:])
-            if step == STEPS - 1:
-                for n in range(step):
-                    spec_ref[n, comp] = olds[n][comp]
-                spec_ref[step, comp, 0] = now[0]
-                spec_ref[step, comp, 1] = now[1]
-            else:
-                spec_ref[comp, 0] = now[0]
-                spec_ref[comp, 1] = now[1]
+            spec_ref[comp, 0] = now[0]
+            spec_ref[comp, 1] = now[1]
             real, imag = past_ref[line, :nx], past_ref[line, nx:]
             terms = [now] + [(old[comp, 0], old[comp, 1]) for old in reversed(olds)]
             for lag, (sr, si) in enumerate(terms):
@@ -583,13 +606,21 @@
                 out[comps * kyb :, :] = jnp.zeros((8, 2 * xb), F32)
                 out[comps * kyb :, :kyb] = halo[8 * s : 8 * s + 8]
 
-    one = (comps, 2, kyb, nx)
-    spec_shape = (STEPS,) + one if step == STEPS - 1 else one
+    spec_shape = (comps, 2, kyb, nx)
     height = comps * kyb + (0 if side is None else 8)
     outs = [(spec_shape, F32)] + [((height, 2 * xb), F32)] * rows
     args = ([] if side is None else [side]) + [*blocks, *table, past, kernel, *before]
     spec, *pieces = call(body, outs, *args)
     return spec, pieces
+
+
+def collect(spectra):
+    def body(*refs):
+        *ins, out = refs
+        for n, ref in enumerate(ins):
+            out[n] = ref[...]
+
+    return call(body, [((len(spectra),) + spectra[0].shape, F32)], *spectra)[0]
 
 
 def turn(blocks, dims, comps, after):
@@ -690,6 +721,8 @@
 
     halo = exchange(first_borders(stress))
     inner = inner_force(stress, velocity.shape[0])
+    weights = outer_weights(yb, where)
+    halo = (*halo, *weights)
     top = push_top(velocity, inner, buoyancy, halo)
     faces = gather_depth(top)
     tables_ = tables(where, dims)
@@ -701,6 +734,7 @@
     for step in range(STEPS):
         last = step == STEPS - 1
         pieces, halo = forward(faces, borders, tables_, dims, () if last else past)
+        halo = (*halo, *weights)
         side = None if last else tables_[3][2]
         spec, pieces = convolve(
             pieces, tables_[2], past[step], recent, spectra, dims, side
@@ -709,7 +743,7 @@
         stress, next_borders = push_stress(stress, velocity, lame, shear, halo, traction)
         after = () if last else (next_borders[1],)
         if not last:
-            halo = exchange(next_borders)
+            halo = (*exchange(next_borders), *weights)
         pieces = inverse(pieces, tables_, dims, recent.shape[1], last, after)
         if last:
             break
@@ -717,8 +751,9 @@
         traction, top = top_after(pieces, velocity, buoyancy)
         faces = gather_depth(top)
         velocity, borders = finish_velocity(velocity, buoyancy, traction, top)
-    stress = add_traction(stress, pieces)
-    return (velocity, stress, spectra[-1])
+    spectra = collect(spectra)
+    stress = add_traction(stress, *next_borders, pieces)
+    return (velocity, stress, spectra)
 
 
 def solution(mesh):

time: 106 us -> 106 us (level)
  local copies, waits for them, and re-layouts: 1.17 us -> 2.4 us
  starting transfers between devices: 44.9 us -> 43.8 us
  waiting for transfers between devices: 39.4 us -> 38.3 us
    ppermute x0 -> x4, waiting for transfers between devices: none -> 14.1 us  [exchange_edges(): return (partner_perm(edge), lax.ppermute(edge, 'col', across))]
    ppermute x24 -> x16, waiting for transfers between devices: 29.2 us -> 15.1 us  [shift_perm(): lax.ppermute(x, axis, [(i, (i + shift) % count) for i in range(count)])]
    ppermute x24 -> x16, starting transfers between devices: 26.8 us -> 20.3 us  [shift_perm(): lax.ppermute(x, axis, [(i, (i + shift) % count) for i in range(count)])]
    ppermute x0 -> x4, starting transfers between devices: none -> 5.39 us  [exchange_edges(): return (partner_perm(edge), lax.ppermute(edge, 'col', across))]
    ppermute x12, waiting for transfers between devices: 6.16 us -> 4.92 us  [depth_perm(): lax.ppermute(x, 'col', [(i, i ^ 2 * depth_mask(t, i & 1, count // 2)) for...]
    unnamed x18, local copies, waits for them, and re-layouts: 1.16 us -> 2.39 us
    ppermute x4 -> x8, waiting for transfers between devices: 4.07 us -> 4.07 us  [partner_perm(): return lax.ppermute(x, 'col', [(i, i ^ 1) for i in range(count)])]
  transfers between devices with their start and end apart: 40 -> 40, of which waited for: 22 -> 19; matrix products, arithmetic and copies ran while one was open for 0% -> 0% of each run, Pallas kernels for 12% -> 13%
where the time goes in v3:
time: 106 us
  starting transfers between devices  43.8 us (41%)
  waiting for transfers between devices  38.3 us (36%)
  Pallas kernels  19.8 us (19%)
  local copies, waits for them, and re-layouts  2.4 us (2%)
  between operations  1.09 us (1%)
    ppermute x16, starting transfers between devices, shift_perm(): lax.ppermute(x, axis, [(i, (i + shift) % count) for i in range(count)])  20.3 us
    pallas_call x26, Pallas kernels, call(): pl.pallas_call(run, out_shape=[jax.ShapeDtypeStruct(s, d) for s, d in out...  19.1 us
    ppermute x12, starting transfers between devices, depth_perm(): lax.ppermute(x, 'col', [(i, i ^ 2 * depth_mask(t, i & 1, count // 2)) for...  17.8 us
    ppermute x16, waiting for transfers between devices, shift_perm(): lax.ppermute(x, axis, [(i, (i + shift) % count) for i in range(count)])  15.1 us
    ppermute x4, waiting for transfers between devices, exchange_edges(): return (partner_perm(edge), lax.ppermute(edge, 'col', across))  14.1 us
    ppermute x4, starting transfers between devices, exchange_edges(): return (partner_perm(edge), lax.ppermute(edge, 'col', across))  5.39 us
    ppermute x12, waiting for transfers between devices, depth_perm(): lax.ppermute(x, 'col', [(i, i ^ 2 * depth_mask(t, i & 1, count // 2)) for...  4.92 us
    ppermute x8, waiting for transfers between devices, partner_perm(): return lax.ppermute(x, 'col', [(i, i ^ 1) for i in range(count)])  4.07 us
  transfers between devices with their start and end apart: 40, of which 19 were waited for; matrix products, arithmetic and copies ran while one was open for 0% of the time, Pallas kernels for 13%

profile of v3, /device:TPU:0, one launch (start us, length us, event | category | flops | bytes accessed | tf_op | source)
XLA Modules:
  0.0 105.5 jit_solution(13439559023183497656)
XLA Ops:
  2.2 4.5 %collective-permute-start.3 = (f32[8,768]{1,0:T(8,128)S(1)}, f32[8,768]{1,0:T(8,128)S(1)}, u32[]{:S(2)}, u32[]{:S(2)}) collective-permute-start(f32[8,768]{1,0:T(8,128)S(1)} %get-tuple-element.61), channel_id=1, source_target_pairs={{0,7},{1,2},{2,1},{3,4},{4,3},{5,6},{6,5},{7,0},{8,15},{9,10},{10,... | collective-permute-start | bytes 73736 | tf_op jit(solution)/shard_map/ppermute | solution.py:297
  6.7 1.5 %collective-permute-start = (f32[24,128]{1,0:T(8,128)S(1)}, f32[24,128]{1,0:T(8,128)S(1)}, u32[]{:S(2)}, u32[]{:S(2)}) collective-permute-start(f32[24,128]{1,0:T(8,128)S(1)} %get-tuple-element.59), channel_id=1, source_target_pairs={{0,8},{8,16},{16,24},{24,0},{1,9},{9,17},{17,25},{25,1},{2,10},{10... | collective-permute-start | bytes 36872 | tf_op jit(solution)/shard_map/ppermute | solution.py:73
  8.2 1.4 %collective-permute-start.1 = (f32[24,128]{1,0:T(8,128)S(1)}, f32[24,128]{1,0:T(8,128)S(1)}, u32[]{:S(2)}, u32[]{:S(2)}) collective-permute-start(f32[24,128]{1,0:T(8,128)S(1)} %get-tuple-element.60), channel_id=1, source_target_pairs={{0,24},{8,0},{16,8},{24,16},{1,25},{9,1},{17,9},{25,17},{2,26},{10... | collective-permute-start | bytes 36872 | tf_op jit(solution)/shard_map/ppermute | solution.py:73
  14.1 2.7 %collective-permute-start.4 = (f32[192,128]{1,0:T(8,128)S(1)}, f32[192,128]{1,0:T(8,128)S(1)}, u32[]{:S(2)}, u32[]{:S(2)}) collective-permute-start(f32[192,128]{1,0:T(8,128)S(1)} %shard_map.96.refs_9_.refs_0_), channel_id=1, source_target_pairs={{0,2},{1,7},{2,0},{3,5},{4,6},{5,3},{6,4},{7,1},{8,10},{9,15},{10,... | collective-permute-start | bytes 294920 | tf_op jit(solution)/shard_map/ppermute | solution.py:82
  16.9 1.9 %shard_map.98 = (bf16[256,512]{1,0:T(8,128)(2,1)S(1)}, bf16[256,512]{1,0:T(8,128)(2,1)S(1)}, bf16[256,512]{1,0:T(8,128)(2,1)S(1)}, bf16[256,512]{1,0:T(8,128)(2,...) custom-call(s32[2]{0:T(128)S(1)} %pad_add_fusion.refs_0_), custom_call_target="tpu_custom_call" | custom-call | bytes 2228232 | tf_op jit(solution)/shard_map/pallas_call | solution.py:30
  20.9 1.8 %shard_map.97 = (f32[3,4,64,128]{3,2,1,0:T(8,128)S(1)}, f32[8,768]{1,0:T(8,128)S(1)}, f32[24,128]{1,0:T(8,128)S(1)}, f32[24,128]{1,0:T(8,128)S(1)}) custom-call(f32[3,4,64,128]{3,2,1,0:T(8,128)S(1)} %copy-done.4, f32[3,4,64,128]{3,2,1,0:T(8,128)S(1)} %shard_map.94.refs_1_, f32[4,64,128]{2,1,0:T(8,128)S(1)} %copy-done.2, ...), custom_call_target="tpu_custom_call" | custom-call | bytes 1540096 | tf_op jit(solution)/shard_map/pallas_call | solution.py:30
  25.8 2.1 %collective-permute-start.8 = (f32[120,128]{1,0:T(8,128)S(1)}, f32[120,128]{1,0:T(8,128)S(1)}, u32[]{:S(2)}, u32[]{:S(2)}) collective-permute-start(f32[120,128]{1,0:T(8,128)S(1)} %get-tuple-element.71), channel_id=1, source_target_pairs={{0,8},{8,16},{16,24},{24,0},{1,9},{9,17},{17,25},{25,1},{2,10},{10... | collective-permute-start | bytes 184328 | tf_op jit(solution)/shard_map/ppermute | solution.py:73
  28.7 1.5 %collective-permute-start.16 = (f32[96,128]{1,0:T(8,128)S(1)}, f32[96,128]{1,0:T(8,128)S(1)}, u32[]{:S(2)}, u32[]{:S(2)}) collective-permute-start(f32[96,128]{1,0:T(8,128)S(1)} %get-tuple-element.80), channel_id=1, source_target_pairs={{0,16},{8,24},{16,0},{24,8},{1,17},{9,25},{17,1},{25,9},{2,18},{10... | collective-permute-start | bytes 147464 | tf_op jit(solution)/shard_map/ppermute | solution.py:73
  30.3 2.6 %collective-permute-done.16.refs_3_ = f32[96,128]{1,0:T(8,128)S(1)} collective-permute-done((f32[96,128]{1,0:T(8,128)S(1)}, f32[96,128]{1,0:T(8,128)S(1)}, u32[]{:S(2)}, u32[]{:S(2)}) %collective-permute-start.16) | collective-permute-done | bytes 49184 | tf_op jit(solution)/shard_map/ppermute | solution.py:73
  33.9 1.8 %collective-permute-start.17 = (f32[104,128]{1,0:T(8,128)S(1)}, f32[104,128]{1,0:T(8,128)S(1)}, u32[]{:S(2)}, u32[]{:S(2)}) collective-permute-start(f32[104,128]{1,0:T(8,128)S(1)} %get-tuple-element.84), channel_id=1, source_target_pairs={{0,24},{8,0},{16,8},{24,16},{1,25},{9,1},{17,9},{25,17},{2,26},{10... | collective-permute-start | bytes 159752 | tf_op jit(solution)/shard_map/ppermute | solution.py:73
  35.7 1.3 %collective-permute-start.18 = (f32[104,128]{1,0:T(8,128)S(1)}, f32[104,128]{1,0:T(8,128)S(1)}, u32[]{:S(2)}, u32[]{:S(2)}) collective-permute-start(f32[104,128]{1,0:T(8,128)S(1)} %get-tuple-element.85), channel_id=1, source_target_pairs={{0,16},{8,24},{16,0},{24,8},{1,17},{9,25},{17,1},{25,9},{2,18},{10... | collective-permute-start | bytes 159752 | tf_op jit(solution)/shard_map/ppermute | solution.py:73
  37.6 4.9 %collective-permute-done.11.refs_7_ = f32[8,768]{1,0:T(8,128)S(1)} collective-permute-done((f32[8,768]{1,0:T(8,128)S(1)}, f32[8,768]{1,0:T(8,128)S(1)}, u32[]{:S(2)}, u32[]{:S(2)}) %collective-permute-start.11) | collective-permute-done | bytes 24608 | tf_op jit(solution)/shard_map/ppermute | solution.py:297
  42.5 2.2 %shard_map.103 = (f32[6,4,64,128]{3,2,1,0:T(8,128)S(1)}, f32[8,768]{1,0:T(8,128)S(1)}, f32[24,128]{1,0:T(8,128)S(1)}, f32[24,128]{1,0:T(8,128)S(1)}) custom-call(f32[6,4,64,128]{3,2,1,0:T(8,128)S(1)} %copy-done.1, f32[3,4,64,128]{3,2,1,0:T(8,128)S(1)} %get-tuple-element.62.refs_1_.refs_0_, f32[4,64,128]{2,1,0:T(8,128)S(1)} %copy-done.6, ...), custom_call_target="tpu_custom_call" | custom-call | bytes 2457600 | tf_op jit(solution)/shard_map/pallas_call | solution.py:30
  47.6 3.7 %collective-permute-start.23 = (f32[208,128]{1,0:T(8,128)S(1)}, f32[208,128]{1,0:T(8,128)S(1)}, u32[]{:S(2)}, u32[]{:S(2)}) collective-permute-start(f32[208,128]{1,0:T(8,128)S(1)} %get-tuple-element.92), channel_id=1, source_target_pairs={{0,6},{1,3},{2,4},{3,1},{4,2},{5,7},{6,0},{7,5},{8,14},{9,11},{10,... | collective-permute-start | bytes 319496 | tf_op jit(solution)/shard_map/ppermute | solution.py:82
  51.3 1.7 %collective-permute-start.12 = (f32[24,128]{1,0:T(8,128)S(1)}, f32[24,128]{1,0:T(8,128)S(1)}, u32[]{:S(2)}, u32[]{:S(2)}) collective-permute-start(f32[24,128]{1,0:T(8,128)S(1)} %get-tuple-element.75), channel_id=1, source_target_pairs={{0,8},{8,16},{16,24},{24,0},{1,9},{9,17},{17,25},{25,1},{2,10},{10... | collective-permute-start | bytes 36872 | tf_op jit(solution)/shard_map/ppermute | solution.py:73
  54.2 1.7 %collective-permute-done.12.refs_3_ = f32[24,128]{1,0:T(8,128)S(1)} collective-permute-done((f32[24,128]{1,0:T(8,128)S(1)}, f32[24,128]{1,0:T(8,128)S(1)}, u32[]{:S(2)}, u32[]{:S(2)}) %collective-permute-start.12) | collective-permute-done | bytes 12320 | tf_op jit(solution)/shard_map/ppermute | solution.py:73
  56.7 4.2 %collective-permute-done.15.refs_6_ = f32[8,768]{1,0:T(8,128)S(1)} collective-permute-done((f32[8,768]{1,0:T(8,128)S(1)}, f32[8,768]{1,0:T(8,128)S(1)}, u32[]{:S(2)}, u32[]{:S(2)}) %collective-permute-start.15) | collective-permute-done | bytes 24608 | tf_op jit(solution)/shard_map/ppermute | solution.py:297
  60.9 1.3 %shard_map.104.refs_0_ = f32[3,4,64,128]{3,2,1,0:T(8,128)S(1)} custom-call(f32[3,4,64,128]{3,2,1,0:T(8,128)S(1)} %get-tuple-element.62.refs_1_.refs_0_, f32[6,4,64,128]{3,2,1,0:T(8,128)S(1)} %get-tuple-element.74.refs_1_.refs_0_, f32[4,64,128]{2,1,0:T(8,128)S(1)} %copy-done.2, f32[24,128]{1,0:T(8,128)S(1)} %collective-permute-done.12.refs_3_, ...), custom_call_target="tpu_custom_call" | custom-call | bytes 1785856 | tf_op jit(solution)/shard_map/pallas_call | solution.py:30
  62.7 4.3 %collective-permute-start.24 = (f32[192,128]{1,0:T(8,128)S(1)}, f32[192,128]{1,0:T(8,128)S(1)}, u32[]{:S(2)}, u32[]{:S(2)}) collective-permute-start(f32[192,128]{1,0:T(8,128)S(1)} %get-tuple-element.94.refs_3_.refs_0_), channel_id=1, source_target_pairs={{0,2},{1,7},{2,0},{3,5},{4,6},{5,3},{6,4},{7,1},{8,10},{9,15},{10,... | collective-permute-start | bytes 294920 | tf_op jit(solution)/shard_map/ppermute | solution.py:82
  67.9 1.9 %collective-permute-done.26.refs_3_ = f32[192,128]{1,0:T(8,128)S(1)} collective-permute-done((f32[192,128]{1,0:T(8,128)S(1)}, f32[192,128]{1,0:T(8,128)S(1)}, u32[]{:S(2)}, u32[]{:S(2)}) %collective-permute-start.26) | collective-permute-done | bytes 98336 | tf_op jit(solution)/shard_map/ppermute | solution.py:82
  69.7 1.9 %collective-permute-done.25.refs_2_ = f32[192,128]{1,0:T(8,128)S(1)} collective-permute-done((f32[192,128]{1,0:T(8,128)S(1)}, f32[192,128]{1,0:T(8,128)S(1)}, u32[]{:S(2)}, u32[]{:S(2)}) %collective-permute-start.25) | collective-permute-done | bytes 98336 | tf_op jit(solution)/shard_map/ppermute | solution.py:82
  73.6 1.6 %collective-permute-start.28 = (f32[120,128]{1,0:T(8,128)S(1)}, f32[120,128]{1,0:T(8,128)S(1)}, u32[]{:S(2)}, u32[]{:S(2)}) collective-permute-start(f32[120,128]{1,0:T(8,128)S(1)} %get-tuple-element.98), channel_id=1, source_target_pairs={{0,8},{8,16},{16,24},{24,0},{1,9},{9,17},{17,25},{25,1},{2,10},{10... | collective-permute-start | bytes 184328 | tf_op jit(solution)/shard_map/ppermute | solution.py:73
  75.2 1.4 %collective-permute-start.29 = (f32[120,128]{1,0:T(8,128)S(1)}, f32[120,128]{1,0:T(8,128)S(1)}, u32[]{:S(2)}, u32[]{:S(2)}) collective-permute-start(f32[120,128]{1,0:T(8,128)S(1)} %get-tuple-element.99), channel_id=1, source_target_pairs={{0,24},{8,0},{16,8},{24,16},{1,25},{9,1},{17,9},{25,17},{2,26},{10... | collective-permute-start | bytes 184328 | tf_op jit(solution)/shard_map/ppermute | solution.py:73
  77.2 3.5 %collective-permute-done.32.refs_2_ = f32[96,128]{1,0:T(8,128)S(1)} collective-permute-done((f32[96,128]{1,0:T(8,128)S(1)}, f32[96,128]{1,0:T(8,128)S(1)}, u32[]{:S(2)}, u32[]{:S(2)}) %collective-permute-start.32) | collective-permute-done | bytes 49184 | tf_op jit(solution)/shard_map/ppermute | solution.py:73
  81.6 1.8 %collective-permute-start.33 = (f32[96,128]{1,0:T(8,128)S(1)}, f32[96,128]{1,0:T(8,128)S(1)}, u32[]{:S(2)}, u32[]{:S(2)}) collective-permute-start(f32[96,128]{1,0:T(8,128)S(1)} %get-tuple-element.107), channel_id=1, source_target_pairs={{0,24},{8,0},{16,8},{24,16},{1,25},{9,1},{17,9},{25,17},{2,26},{10... | collective-permute-start | bytes 147464 | tf_op jit(solution)/shard_map/ppermute | solution.py:73
  84.4 1.3 %collective-permute-done.33.refs_1_ = f32[96,128]{1,0:T(8,128)S(1)} collective-permute-done((f32[96,128]{1,0:T(8,128)S(1)}, f32[96,128]{1,0:T(8,128)S(1)}, u32[]{:S(2)}, u32[]{:S(2)}) %collective-permute-start.33) | collective-permute-done | bytes 49184 | tf_op jit(solution)/shard_map/ppermute | solution.py:73
  85.8 1.8 %collective-permute-done.34.refs_2_ = f32[96,128]{1,0:T(8,128)S(1)} collective-permute-done((f32[96,128]{1,0:T(8,128)S(1)}, f32[96,128]{1,0:T(8,128)S(1)}, u32[]{:S(2)}, u32[]{:S(2)}) %collective-permute-start.34) | collective-permute-done | bytes 49184 | tf_op jit(solution)/shard_map/ppermute | solution.py:73
  87.6 1.9 %collective-permute-done.35.refs_3_ = f32[96,128]{1,0:T(8,128)S(1)} collective-permute-done((f32[96,128]{1,0:T(8,128)S(1)}, f32[96,128]{1,0:T(8,128)S(1)}, u32[]{:S(2)}, u32[]{:S(2)}) %collective-permute-start.35) | collective-permute-done | bytes 49184 | tf_op jit(solution)/shard_map/ppermute | solution.py:73
  91.6 2.3 %collective-permute-start.38 = (f32[192,128]{1,0:T(8,128)S(1)}, f32[192,128]{1,0:T(8,128)S(1)}, u32[]{:S(2)}, u32[]{:S(2)}) collective-permute-start(f32[192,128]{1,0:T(8,128)S(1)} %get-tuple-element.112), channel_id=1, source_target_pairs={{0,4},{1,5},{2,6},{3,7},{4,0},{5,1},{6,2},{7,3},{8,12},{9,13},{10,... | collective-permute-start | bytes 294920 | tf_op jit(solution)/shard_map/ppermute | solution.py:82
  93.9 2.0 %collective-permute-start.39 = (f32[192,128]{1,0:T(8,128)S(1)}, f32[192,128]{1,0:T(8,128)S(1)}, u32[]{:S(2)}, u32[]{:S(2)}) collective-permute-start(f32[192,128]{1,0:T(8,128)S(1)} %get-tuple-element.113), channel_id=1, source_target_pairs={{0,6},{1,3},{2,4},{3,1},{4,2},{5,7},{6,0},{7,5},{8,14},{9,11},{10,... | collective-permute-start | bytes 294920 | tf_op jit(solution)/shard_map/ppermute | solution.py:82
  97.4 5.0 %collective-permute-done.31.refs_7_ = f32[8,768]{1,0:T(8,128)S(1)} collective-permute-done((f32[8,768]{1,0:T(8,128)S(1)}, f32[8,768]{1,0:T(8,128)S(1)}, u32[]{:S(2)}, u32[]{:S(2)}) %collective-permute-start.31) | collective-permute-done | bytes 24608 | tf_op jit(solution)/shard_map/ppermute | solution.py:297
  102.4 2.3 %shard_map.114 = (f32[6,4,64,128]{3,2,1,0:T(8,128)}, f32[192,128]{1,0:T(8,128)S(1)}) custom-call(f32[6,4,64,128]{3,2,1,0:T(8,128)S(1)} %get-tuple-element.74.refs_1_.refs_0_, f32[3,4,64,128]{3,2,1,0:T(8,128)S(1)} %copy-done.8, f32[4,64,128]{2,1,0:T(8,128)S(1)} %copy-done.6, f32[4,64,128]{2,1,0:T(8,128)S(1)} %copy-done.7, ...), custom_call_target="tpu_custom_call" | custom-call | bytes 2613248 | tf_op jit(solution)/shard_map/pallas_call | solution.py:30
  (98 shorter events, 28.6 us)
Async XLA Ops:
  2.2 9.7 %collective-permute-start.3 = (f32[8,768]{1,0:T(8,128)S(1)}, f32[8,768]{1,0:T(8,128)S(1)}, u32[]{:S(2)}, u32[]{:S(2)}) collective-permute-start(f32[8,768]{1,0:T(8,128)S(1)} %get-tuple-element.61), channel_id=1, source_target_pairs={{0,7},{1,2},{2,1},{3,4},{4,3},{5,6},{6,5},{7,0},{8,15},{9,10},{10,... | collective-permute-start | bytes 73736 | tf_op jit(solution)/shard_map/ppermute | solution.py:297
  6.7 5.2 %collective-permute-start.2 = (f32[8,768]{1,0:T(8,128)S(1)}, f32[8,768]{1,0:T(8,128)S(1)}, u32[]{:S(2)}, u32[]{:S(2)}) collective-permute-start(f32[8,768]{1,0:T(8,128)S(1)} %get-tuple-element.61), channel_id=1, source_target_pairs={{0,1},{1,0},{2,3},{3,2},{4,5},{5,4},{6,7},{7,6},{8,9},{9,8},{10,11... | collective-permute-start | bytes 73736 | tf_op jit(solution)/shard_map/ppermute | solution.py:89
  6.7 4.6 %collective-permute-start = (f32[24,128]{1,0:T(8,128)S(1)}, f32[24,128]{1,0:T(8,128)S(1)}, u32[]{:S(2)}, u32[]{:S(2)}) collective-permute-start(f32[24,128]{1,0:T(8,128)S(1)} %get-tuple-element.59), channel_id=1, source_target_pairs={{0,8},{8,16},{16,24},{24,0},{1,9},{9,17},{17,25},{25,1},{2,10},{10... | collective-permute-start | bytes 36872 | tf_op jit(solution)/shard_map/ppermute | solution.py:73
  12.3 10.3 %collective-permute-start.6 = (f32[192,128]{1,0:T(8,128)S(1)}, f32[192,128]{1,0:T(8,128)S(1)}, u32[]{:S(2)}, u32[]{:S(2)}) collective-permute-start(f32[192,128]{1,0:T(8,128)S(1)} %shard_map.96.refs_9_.refs_0_), channel_id=1, source_target_pairs={{0,6},{1,3},{2,4},{3,1},{4,2},{5,7},{6,0},{7,5},{8,14},{9,11},{10,... | collective-permute-start | bytes 294920 | tf_op jit(solution)/shard_map/ppermute | solution.py:82
  13.3 10.5 %collective-permute-start.5 = (f32[192,128]{1,0:T(8,128)S(1)}, f32[192,128]{1,0:T(8,128)S(1)}, u32[]{:S(2)}, u32[]{:S(2)}) collective-permute-start(f32[192,128]{1,0:T(8,128)S(1)} %shard_map.96.refs_9_.refs_0_), channel_id=1, source_target_pairs={{0,4},{1,5},{2,6},{3,7},{4,0},{5,1},{6,2},{7,3},{8,12},{9,13},{10,... | collective-permute-start | bytes 294920 | tf_op jit(solution)/shard_map/ppermute | solution.py:82
  14.1 9.7 %collective-permute-start.4 = (f32[192,128]{1,0:T(8,128)S(1)}, f32[192,128]{1,0:T(8,128)S(1)}, u32[]{:S(2)}, u32[]{:S(2)}) collective-permute-start(f32[192,128]{1,0:T(8,128)S(1)} %shard_map.96.refs_9_.refs_0_), channel_id=1, source_target_pairs={{0,2},{1,7},{2,0},{3,5},{4,6},{5,3},{6,4},{7,1},{8,10},{9,15},{10,... | collective-permute-start | bytes 294920 | tf_op jit(solution)/shard_map/ppermute | solution.py:82
  25.8 7.1 %collective-permute-start.8 = (f32[120,128]{1,0:T(8,128)S(1)}, f32[120,128]{1,0:T(8,128)S(1)}, u32[]{:S(2)}, u32[]{:S(2)}) collective-permute-start(f32[120,128]{1,0:T(8,128)S(1)} %get-tuple-element.71), channel_id=1, source_target_pairs={{0,8},{8,16},{16,24},{24,0},{1,9},{9,17},{17,25},{25,1},{2,10},{10... | collective-permute-start | bytes 184328 | tf_op jit(solution)/shard_map/ppermute | solution.py:73
  27.9 4.9 %collective-permute-start.9 = (f32[120,128]{1,0:T(8,128)S(1)}, f32[120,128]{1,0:T(8,128)S(1)}, u32[]{:S(2)}, u32[]{:S(2)}) collective-permute-start(f32[120,128]{1,0:T(8,128)S(1)} %get-tuple-element.72), channel_id=1, source_target_pairs={{0,24},{8,0},{16,8},{24,16},{1,25},{9,1},{17,9},{25,17},{2,26},{10... | collective-permute-start | bytes 184328 | tf_op jit(solution)/shard_map/ppermute | solution.py:73
  28.7 4.1 %collective-permute-start.16 = (f32[96,128]{1,0:T(8,128)S(1)}, f32[96,128]{1,0:T(8,128)S(1)}, u32[]{:S(2)}, u32[]{:S(2)}) collective-permute-start(f32[96,128]{1,0:T(8,128)S(1)} %get-tuple-element.80), channel_id=1, source_target_pairs={{0,16},{8,24},{16,0},{24,8},{1,17},{9,25},{17,1},{25,9},{2,18},{10... | collective-permute-start | bytes 147464 | tf_op jit(solution)/shard_map/ppermute | solution.py:73
  33.9 10.8 %collective-permute-start.17 = (f32[104,128]{1,0:T(8,128)S(1)}, f32[104,128]{1,0:T(8,128)S(1)}, u32[]{:S(2)}, u32[]{:S(2)}) collective-permute-start(f32[104,128]{1,0:T(8,128)S(1)} %get-tuple-element.84), channel_id=1, source_target_pairs={{0,24},{8,0},{16,8},{24,16},{1,25},{9,1},{17,9},{25,17},{2,26},{10... | collective-permute-start | bytes 159752 | tf_op jit(solution)/shard_map/ppermute | solution.py:73
  35.7 9.0 %collective-permute-start.18 = (f32[104,128]{1,0:T(8,128)S(1)}, f32[104,128]{1,0:T(8,128)S(1)}, u32[]{:S(2)}, u32[]{:S(2)}) collective-permute-start(f32[104,128]{1,0:T(8,128)S(1)} %get-tuple-element.85), channel_id=1, source_target_pairs={{0,16},{8,24},{16,0},{24,8},{1,17},{9,25},{17,1},{25,9},{2,18},{10... | collective-permute-start | bytes 159752 | tf_op jit(solution)/shard_map/ppermute | solution.py:73
  37.0 7.7 %collective-permute-start.19 = (f32[104,128]{1,0:T(8,128)S(1)}, f32[104,128]{1,0:T(8,128)S(1)}, u32[]{:S(2)}, u32[]{:S(2)}) collective-permute-start(f32[104,128]{1,0:T(8,128)S(1)} %get-tuple-element.86), channel_id=1, source_target_pairs={{0,8},{8,16},{16,24},{24,0},{1,9},{9,17},{17,25},{25,1},{2,10},{10... | collective-permute-start | bytes 159752 | tf_op jit(solution)/shard_map/ppermute | solution.py:73
  37.5 5.0 %collective-permute-start.11 = (f32[8,768]{1,0:T(8,128)S(1)}, f32[8,768]{1,0:T(8,128)S(1)}, u32[]{:S(2)}, u32[]{:S(2)}) collective-permute-start(f32[8,768]{1,0:T(8,128)S(1)} %get-tuple-element.73), channel_id=1, source_target_pairs={{0,7},{1,2},{2,1},{3,4},{4,3},{5,6},{6,5},{7,0},{8,15},{9,10},{10,... | collective-permute-start | bytes 73736 | tf_op jit(solution)/shard_map/ppermute | solution.py:297
  37.6 4.9 %collective-permute-start.10 = (f32[8,768]{1,0:T(8,128)S(1)}, f32[8,768]{1,0:T(8,128)S(1)}, u32[]{:S(2)}, u32[]{:S(2)}) collective-permute-start(f32[8,768]{1,0:T(8,128)S(1)} %get-tuple-element.73), channel_id=1, source_target_pairs={{0,1},{1,0},{2,3},{3,2},{4,5},{5,4},{6,7},{7,6},{8,9},{9,8},{10,11... | collective-permute-start | bytes 73736 | tf_op jit(solution)/shard_map/ppermute | solution.py:89
  46.8 15.4 %collective-permute-start.21 = (f32[208,128]{1,0:T(8,128)S(1)}, f32[208,128]{1,0:T(8,128)S(1)}, u32[]{:S(2)}, u32[]{:S(2)}) collective-permute-start(f32[208,128]{1,0:T(8,128)S(1)} %get-tuple-element.90), channel_id=1, source_target_pairs={{0,2},{1,7},{2,0},{3,5},{4,6},{5,3},{6,4},{7,1},{8,10},{9,15},{10,... | collective-permute-start | bytes 319496 | tf_op jit(solution)/shard_map/ppermute | solution.py:82
  46.9 15.3 %collective-permute-start.22 = (f32[208,128]{1,0:T(8,128)S(1)}, f32[208,128]{1,0:T(8,128)S(1)}, u32[]{:S(2)}, u32[]{:S(2)}) collective-permute-start(f32[208,128]{1,0:T(8,128)S(1)} %get-tuple-element.91), channel_id=1, source_target_pairs={{0,4},{1,5},{2,6},{3,7},{4,0},{5,1},{6,2},{7,3},{8,12},{9,13},{10,... | collective-permute-start | bytes 319496 | tf_op jit(solution)/shard_map/ppermute | solution.py:82
  47.6 14.7 %collective-permute-start.23 = (f32[208,128]{1,0:T(8,128)S(1)}, f32[208,128]{1,0:T(8,128)S(1)}, u32[]{:S(2)}, u32[]{:S(2)}) collective-permute-start(f32[208,128]{1,0:T(8,128)S(1)} %get-tuple-element.92), channel_id=1, source_target_pairs={{0,6},{1,3},{2,4},{3,1},{4,2},{5,7},{6,0},{7,5},{8,14},{9,11},{10,... | collective-permute-start | bytes 319496 | tf_op jit(solution)/shard_map/ppermute | solution.py:82
  51.3 4.6 %collective-permute-start.12 = (f32[24,128]{1,0:T(8,128)S(1)}, f32[24,128]{1,0:T(8,128)S(1)}, u32[]{:S(2)}, u32[]{:S(2)}) collective-permute-start(f32[24,128]{1,0:T(8,128)S(1)} %get-tuple-element.75), channel_id=1, source_target_pairs={{0,8},{8,16},{16,24},{24,0},{1,9},{9,17},{17,25},{25,1},{2,10},{10... | collective-permute-start | bytes 36872 | tf_op jit(solution)/shard_map/ppermute | solution.py:73
  55.9 5.0 %collective-permute-start.15 = (f32[8,768]{1,0:T(8,128)S(1)}, f32[8,768]{1,0:T(8,128)S(1)}, u32[]{:S(2)}, u32[]{:S(2)}) collective-permute-start(f32[8,768]{1,0:T(8,128)S(1)} %get-tuple-element.77), channel_id=1, source_target_pairs={{0,7},{1,2},{2,1},{3,4},{4,3},{5,6},{6,5},{7,0},{8,15},{9,10},{10,... | collective-permute-start | bytes 73736 | tf_op jit(solution)/shard_map/ppermute | solution.py:297
  56.7 4.2 %collective-permute-start.14 = (f32[8,768]{1,0:T(8,128)S(1)}, f32[8,768]{1,0:T(8,128)S(1)}, u32[]{:S(2)}, u32[]{:S(2)}) collective-permute-start(f32[8,768]{1,0:T(8,128)S(1)} %get-tuple-element.77), channel_id=1, source_target_pairs={{0,1},{1,0},{2,3},{3,2},{4,5},{5,4},{6,7},{7,6},{8,9},{9,8},{10,11... | collective-permute-start | bytes 73736 | tf_op jit(solution)/shard_map/ppermute | solution.py:89
  62.6 7.2 %collective-permute-start.26 = (f32[192,128]{1,0:T(8,128)S(1)}, f32[192,128]{1,0:T(8,128)S(1)}, u32[]{:S(2)}, u32[]{:S(2)}) collective-permute-start(f32[192,128]{1,0:T(8,128)S(1)} %get-tuple-element.94.refs_3_.refs_0_), channel_id=1, source_target_pairs={{0,6},{1,3},{2,4},{3,1},{4,2},{5,7},{6,0},{7,5},{8,14},{9,11},{10,... | collective-permute-start | bytes 294920 | tf_op jit(solution)/shard_map/ppermute | solution.py:82
  62.7 9.0 %collective-permute-start.25 = (f32[192,128]{1,0:T(8,128)S(1)}, f32[192,128]{1,0:T(8,128)S(1)}, u32[]{:S(2)}, u32[]{:S(2)}) collective-permute-start(f32[192,128]{1,0:T(8,128)S(1)} %get-tuple-element.94.refs_3_.refs_0_), channel_id=1, source_target_pairs={{0,4},{1,5},{2,6},{3,7},{4,0},{5,1},{6,2},{7,3},{8,12},{9,13},{10,... | collective-permute-start | bytes 294920 | tf_op jit(solution)/shard_map/ppermute | solution.py:82
  62.7 8.9 %collective-permute-start.24 = (f32[192,128]{1,0:T(8,128)S(1)}, f32[192,128]{1,0:T(8,128)S(1)}, u32[]{:S(2)}, u32[]{:S(2)}) collective-permute-start(f32[192,128]{1,0:T(8,128)S(1)} %get-tuple-element.94.refs_3_.refs_0_), channel_id=1, source_target_pairs={{0,2},{1,7},{2,0},{3,5},{4,6},{5,3},{6,4},{7,1},{8,10},{9,15},{10,... | collective-permute-start | bytes 294920 | tf_op jit(solution)/shard_map/ppermute | solution.py:82
  73.6 7.1 %collective-permute-start.28 = (f32[120,128]{1,0:T(8,128)S(1)}, f32[120,128]{1,0:T(8,128)S(1)}, u32[]{:S(2)}, u32[]{:S(2)}) collective-permute-start(f32[120,128]{1,0:T(8,128)S(1)} %get-tuple-element.98), channel_id=1, source_target_pairs={{0,8},{8,16},{16,24},{24,0},{1,9},{9,17},{17,25},{25,1},{2,10},{10... | collective-permute-start | bytes 184328 | tf_op jit(solution)/shard_map/ppermute | solution.py:73
  75.2 5.5 %collective-permute-start.29 = (f32[120,128]{1,0:T(8,128)S(1)}, f32[120,128]{1,0:T(8,128)S(1)}, u32[]{:S(2)}, u32[]{:S(2)}) collective-permute-start(f32[120,128]{1,0:T(8,128)S(1)} %get-tuple-element.99), channel_id=1, source_target_pairs={{0,24},{8,0},{16,8},{24,16},{1,25},{9,1},{17,9},{25,17},{2,26},{10... | collective-permute-start | bytes 184328 | tf_op jit(solution)/shard_map/ppermute | solution.py:73
  81.6 4.1 %collective-permute-start.33 = (f32[96,128]{1,0:T(8,128)S(1)}, f32[96,128]{1,0:T(8,128)S(1)}, u32[]{:S(2)}, u32[]{:S(2)}) collective-permute-start(f32[96,128]{1,0:T(8,128)S(1)} %get-tuple-element.107), channel_id=1, source_target_pairs={{0,24},{8,0},{16,8},{24,16},{1,25},{9,1},{17,9},{25,17},{2,26},{10... | collective-permute-start | bytes 147464 | tf_op jit(solution)/shard_map/ppermute | solution.py:73
  84.4 5.0 %collective-permute-start.35 = (f32[96,128]{1,0:T(8,128)S(1)}, f32[96,128]{1,0:T(8,128)S(1)}, u32[]{:S(2)}, u32[]{:S(2)}) collective-permute-start(f32[96,128]{1,0:T(8,128)S(1)} %get-tuple-element.109), channel_id=1, source_target_pairs={{0,8},{8,16},{16,24},{24,0},{1,9},{9,17},{17,25},{25,1},{2,10},{10... | collective-permute-start | bytes 147464 | tf_op jit(solution)/shard_map/ppermute | solution.py:73
  91.4 13.3 %collective-permute-start.37 = (f32[192,128]{1,0:T(8,128)S(1)}, f32[192,128]{1,0:T(8,128)S(1)}, u32[]{:S(2)}, u32[]{:S(2)}) collective-permute-start(f32[192,128]{1,0:T(8,128)S(1)} %get-tuple-element.111), channel_id=1, source_target_pairs={{0,2},{1,7},{2,0},{3,5},{4,6},{5,3},{6,4},{7,1},{8,10},{9,15},{10,... | collective-permute-start | bytes 294920 | tf_op jit(solution)/shard_map/ppermute | solution.py:82
  91.6 13.1 %collective-permute-start.38 = (f32[192,128]{1,0:T(8,128)S(1)}, f32[192,128]{1,0:T(8,128)S(1)}, u32[]{:S(2)}, u32[]{:S(2)}) collective-permute-start(f32[192,128]{1,0:T(8,128)S(1)} %get-tuple-element.112), channel_id=1, source_target_pairs={{0,4},{1,5},{2,6},{3,7},{4,0},{5,1},{6,2},{7,3},{8,12},{9,13},{10,... | collective-permute-start | bytes 294920 | tf_op jit(solution)/shard_map/ppermute | solution.py:82
  93.9 10.8 %collective-permute-start.39 = (f32[192,128]{1,0:T(8,128)S(1)}, f32[192,128]{1,0:T(8,128)S(1)}, u32[]{:S(2)}, u32[]{:S(2)}) collective-permute-start(f32[192,128]{1,0:T(8,128)S(1)} %get-tuple-element.113), channel_id=1, source_target_pairs={{0,6},{1,3},{2,4},{3,1},{4,2},{5,7},{6,0},{7,5},{8,14},{9,11},{10,... | collective-permute-start | bytes 294920 | tf_op jit(solution)/shard_map/ppermute | solution.py:82
  95.8 6.5 %collective-permute-start.31 = (f32[8,768]{1,0:T(8,128)S(1)}, f32[8,768]{1,0:T(8,128)S(1)}, u32[]{:S(2)}, u32[]{:S(2)}) collective-permute-start(f32[8,768]{1,0:T(8,128)S(1)} %get-tuple-element.100), channel_id=1, source_target_pairs={{0,7},{1,2},{2,1},{3,4},{4,3},{5,6},{6,5},{7,0},{8,15},{9,10},{10,... | collective-permute-start | bytes 73736 | tf_op jit(solution)/shard_map/ppermute | solution.py:297
  96.6 5.8 %collective-permute-start.30 = (f32[8,768]{1,0:T(8,128)S(1)}, f32[8,768]{1,0:T(8,128)S(1)}, u32[]{:S(2)}, u32[]{:S(2)}) collective-permute-start(f32[8,768]{1,0:T(8,128)S(1)} %get-tuple-element.100), channel_id=1, source_target_pairs={{0,1},{1,0},{2,3},{3,2},{4,5},{5,4},{6,7},{7,6},{8,9},{9,8},{10,11... | collective-permute-start | bytes 73736 | tf_op jit(solution)/shard_map/ppermute | solution.py:89
  (17 other events, 114.8 us)

commit v4 on v3

--- a/solution.py
+++ b/solution.py
@@ -141,10 +141,11 @@
                 put(hi_ref, lo_ref, (pl.ds(nk, nk), span), -(base_sin * tc + base_cos * ts))
             line, lane = iota((depth * 8, nk), 0), iota((depth * 8, nk), 1)
             wave = ((lane // kyb + r) & (rows - 1)) * (cols * kyb) + col * kyb + lane % kyb
-            spot = (met(line // 8)) * yb + beyond(line % 8, yb)
+            spot = (met(line // 8)) * yb + beyond(line % 8 - 4, yb)
             side_cos, side_sin = unit(wave * spot, ny)
-            side_ref[:, :nk] = side_cos * scale
-            side_ref[:, nk:] = -side_sin * scale
+            used = line % 8 >= 4
+            side_ref[:, :nk] = jnp.where(used, side_cos * scale, 0.0)
+            side_ref[:, nk:] = jnp.where(used, -side_sin * scale, 0.0)
         base_cos, base_sin = unit(iota((xb, nx), 0) * iota((xb, nx), 1), nx)
         tall = max(8, rows)
         start = ((r - iota((tall, nx), 0)) & (rows - 1)) * xb
@@ -459,9 +460,9 @@
         sum_ref[...] = total
         main = comps * xb
         force = row_deriv(pad, total[:xb], total[main : main + 2], total[main + 2 : main + 4])
-        side = total[main + 8 : main + 16, :xb].T
+        side = total[main : main + 8, :xb].T
         line, lane = iota((8, yb), 0), iota((8, yb), 1)
-        gap = jnp.where(line < 4, beyond(line, yb) - lane, 99)
+        gap = jnp.where(line >= 4, beyond(line - 4, yb) - lane, 99)
         near = jnp.where(gap == 1, NEAR, 0.0) - jnp.where(gap == -1, NEAR, 0.0)
         outer = near + jnp.where(gap == 2, FAR, 0.0) - jnp.where(gap == -2, FAR, 0.0)
         force = force + (dot6(total[xb : 2 * xb], inner_weights(yb), NN) + dot6(side, outer, NN))
@@ -651,7 +652,8 @@
     beside = dot6(side_ref[...], d_ref[xb : 2 * xb, :], NT)
     gap = jnp.zeros((8, yb - xb), F32)
     parts = [jnp.concatenate([beside[8 * t : 8 * t + 8], gap], axis=1) for t in range(depth)]
-    return jnp.concatenate([total, jnp.concatenate(parts, axis=1)], axis=0)
+    main = total.shape[0] - 8
+    return jnp.concatenate([total[:main], total[main:] + jnp.concatenate(parts, axis=1)], axis=0)
 
 
 def part_inverse(data, table, dims, side=None):
@@ -659,7 +661,7 @@
         out = refs[-1]
         out[...] = y_inverse(d_ref, hi, lo, dims, refs[0] if side is not None else None)
 
-    shape = (data.shape[0] + (0 if side is None else 8), dims[1] // 2 * dims[3])
+    shape = (data.shape[0], dims[1] // 2 * dims[3])
     extra = [] if side is None else [side]
     return call(body, [(shape, F32)], data, *table, *extra)[0]
 
@@ -689,10 +691,10 @@
     return [block] + in_turn([block] * (lax.axis_size("col") // 2 - 1))
 
 
-def forward(faces, borders, tables_, dims, after):
+def forward(faces, borders, tables_, dims):
     mine, other = tables_[:2]
     edge, first, last = borders
-    sent = part_forward(faces, other, dims, after=(first, *after))
+    sent = part_forward(faces, other, dims, after=(first,))
     came = partner_perm(sent)
     kept = part_forward(faces, mine, dims)
     pieces = join(kept, came, first, last, dims)
@@ -733,7 +735,7 @@
     traction = None
     for step in range(STEPS):
         last = step == STEPS - 1
-        pieces, halo = forward(faces, borders, tables_, dims, () if last else past)
+        pieces, halo = forward(faces, borders, tables_, dims)
         halo = (*halo, *weights)
         side = None if last else tables_[3][2]
         spec, pieces = convolve(

time: 106 us -> 106 us (level)
  local copies, waits for them, and re-layouts: 2.4 us -> 1.18 us
    ppermute x12, waiting for transfers between devices: 4.92 us -> 6.9 us  [depth_perm(): lax.ppermute(x, 'col', [(i, i ^ 2 * depth_mask(t, i & 1, count // 2)) for...]
    unnamed x18, local copies, waits for them, and re-layouts: 2.39 us -> 1.17 us
where the time goes in v4:
time: 106 us; the launch traced here: 105 us
  starting transfers between devices  43.8 us (41%)
  waiting for transfers between devices  39.3 us (37%)
  Pallas kernels  19.8 us (19%)
  local copies, waits for them, and re-layouts  1.18 us (1%)
  between operations  1.12 us (1%)
    ppermute x16, starting transfers between devices, shift_perm(): lax.ppermute(x, axis, [(i, (i + shift) % count) for i in range(count)])  20.2 us
    pallas_call x26, Pallas kernels, call(): pl.pallas_call(run, out_shape=[jax.ShapeDtypeStruct(s, d) for s, d in out...  19.1 us
    ppermute x12, starting transfers between devices, depth_perm(): lax.ppermute(x, 'col', [(i, i ^ 2 * depth_mask(t, i & 1, count // 2)) for...  17.8 us
    ppermute x16, waiting for transfers between devices, shift_perm(): lax.ppermute(x, axis, [(i, (i + shift) % count) for i in range(count)])  14.4 us
    ppermute x4, waiting for transfers between devices, exchange_edges(): return (partner_perm(edge), lax.ppermute(edge, 'col', across))  13.9 us
    ppermute x12, waiting for transfers between devices, depth_perm(): lax.ppermute(x, 'col', [(i, i ^ 2 * depth_mask(t, i & 1, count // 2)) for...  6.9 us
    ppermute x4, starting transfers between devices, exchange_edges(): return (partner_perm(edge), lax.ppermute(edge, 'col', across))  5.51 us
    ppermute x8, waiting for transfers between devices, partner_perm(): return lax.ppermute(x, 'col', [(i, i ^ 1) for i in range(count)])  4.07 us
  transfers between devices with their start and end apart: 40, of which 19 were waited for; matrix products, arithmetic and copies ran while one was open for 0% of the time, Pallas kernels for 13%

profile of v4, /device:TPU:0, one launch (start us, length us, event | category | flops | bytes accessed | tf_op | source)
XLA Modules:
  0.0 105.3 jit_solution(16553963121582231415)
XLA Ops:
  2.2 4.5 %collective-permute-start.3 = (f32[8,768]{1,0:T(8,128)S(1)}, f32[8,768]{1,0:T(8,128)S(1)}, u32[]{:S(2)}, u32[]{:S(2)}) collective-permute-start(f32[8,768]{1,0:T(8,128)S(1)} %get-tuple-element.61), channel_id=1, source_target_pairs={{0,7},{1,2},{2,1},{3,4},{4,3},{5,6},{6,5},{7,0},{8,15},{9,10},{10,... | collective-permute-start | bytes 73736 | tf_op jit(solution)/shard_map/ppermute | solution.py:298
  6.7 1.5 %collective-permute-start = (f32[24,128]{1,0:T(8,128)S(1)}, f32[24,128]{1,0:T(8,128)S(1)}, u32[]{:S(2)}, u32[]{:S(2)}) collective-permute-start(f32[24,128]{1,0:T(8,128)S(1)} %get-tuple-element.59), channel_id=1, source_target_pairs={{0,8},{8,16},{16,24},{24,0},{1,9},{9,17},{17,25},{25,1},{2,10},{10... | collective-permute-start | bytes 36872 | tf_op jit(solution)/shard_map/ppermute | solution.py:73
  8.2 1.4 %collective-permute-start.1 = (f32[24,128]{1,0:T(8,128)S(1)}, f32[24,128]{1,0:T(8,128)S(1)}, u32[]{:S(2)}, u32[]{:S(2)}) collective-permute-start(f32[24,128]{1,0:T(8,128)S(1)} %get-tuple-element.60), channel_id=1, source_target_pairs={{0,24},{8,0},{16,8},{24,16},{1,25},{9,1},{17,9},{25,17},{2,26},{10... | collective-permute-start | bytes 36872 | tf_op jit(solution)/shard_map/ppermute | solution.py:73
  14.1 2.7 %collective-permute-start.4 = (f32[192,128]{1,0:T(8,128)S(1)}, f32[192,128]{1,0:T(8,128)S(1)}, u32[]{:S(2)}, u32[]{:S(2)}) collective-permute-start(f32[192,128]{1,0:T(8,128)S(1)} %shard_map.96.refs_9_.refs_0_), channel_id=1, source_target_pairs={{0,2},{1,7},{2,0},{3,5},{4,6},{5,3},{6,4},{7,1},{8,10},{9,15},{10,... | collective-permute-start | bytes 294920 | tf_op jit(solution)/shard_map/ppermute | solution.py:82
  16.9 1.9 %shard_map.98 = (bf16[256,512]{1,0:T(8,128)(2,1)S(1)}, bf16[256,512]{1,0:T(8,128)(2,1)S(1)}, bf16[256,512]{1,0:T(8,128)(2,1)S(1)}, bf16[256,512]{1,0:T(8,128)(2,...) custom-call(s32[2]{0:T(128)S(1)} %pad_add_fusion.refs_0_), custom_call_target="tpu_custom_call" | custom-call | bytes 2228232 | tf_op jit(solution)/shard_map/pallas_call | solution.py:30
  18.8 1.8 %shard_map.97 = (f32[3,4,64,128]{3,2,1,0:T(8,128)S(1)}, f32[8,768]{1,0:T(8,128)S(1)}, f32[24,128]{1,0:T(8,128)S(1)}, f32[24,128]{1,0:T(8,128)S(1)}) custom-call(f32[3,4,64,128]{3,2,1,0:T(8,128)S(1)} %copy-done.4, f32[3,4,64,128]{3,2,1,0:T(8,128)S(1)} %shard_map.94.refs_1_, f32[4,64,128]{2,1,0:T(8,128)S(1)} %copy-done.2, ...), custom_call_target="tpu_custom_call" | custom-call | bytes 1540096 | tf_op jit(solution)/shard_map/pallas_call | solution.py:30
  20.6 3.2 %collective-permute-done.5.refs_2_ = f32[192,128]{1,0:T(8,128)S(1)} collective-permute-done((f32[192,128]{1,0:T(8,128)S(1)}, f32[192,128]{1,0:T(8,128)S(1)}, u32[]{:S(2)}, u32[]{:S(2)}) %collective-permute-start.5) | collective-permute-done | bytes 98336 | tf_op jit(solution)/shard_map/ppermute | solution.py:82
  25.8 2.1 %collective-permute-start.8 = (f32[120,128]{1,0:T(8,128)S(1)}, f32[120,128]{1,0:T(8,128)S(1)}, u32[]{:S(2)}, u32[]{:S(2)}) collective-permute-start(f32[120,128]{1,0:T(8,128)S(1)} %get-tuple-element.69), channel_id=1, source_target_pairs={{0,8},{8,16},{16,24},{24,0},{1,9},{9,17},{17,25},{25,1},{2,10},{10... | collective-permute-start | bytes 184328 | tf_op jit(solution)/shard_map/ppermute | solution.py:73
  28.8 1.5 %collective-permute-start.16 = (f32[96,128]{1,0:T(8,128)S(1)}, f32[96,128]{1,0:T(8,128)S(1)}, u32[]{:S(2)}, u32[]{:S(2)}) collective-permute-start(f32[96,128]{1,0:T(8,128)S(1)} %get-tuple-element.78), channel_id=1, source_target_pairs={{0,16},{8,24},{16,0},{24,8},{1,17},{9,25},{17,1},{25,9},{2,18},{10... | collective-permute-start | bytes 147464 | tf_op jit(solution)/shard_map/ppermute | solution.py:73
  31.1 1.7 %collective-permute-done.16.refs_3_ = f32[96,128]{1,0:T(8,128)S(1)} collective-permute-done((f32[96,128]{1,0:T(8,128)S(1)}, f32[96,128]{1,0:T(8,128)S(1)}, u32[]{:S(2)}, u32[]{:S(2)}) %collective-permute-start.16) | collective-permute-done | bytes 49184 | tf_op jit(solution)/shard_map/ppermute | solution.py:73
  33.9 1.8 %collective-permute-start.17 = (f32[104,128]{1,0:T(8,128)S(1)}, f32[104,128]{1,0:T(8,128)S(1)}, u32[]{:S(2)}, u32[]{:S(2)}) collective-permute-start(f32[104,128]{1,0:T(8,128)S(1)} %get-tuple-element.83), channel_id=1, source_target_pairs={{0,24},{8,0},{16,8},{24,16},{1,25},{9,1},{17,9},{25,17},{2,26},{10... | collective-permute-start | bytes 159752 | tf_op jit(solution)/shard_map/ppermute | solution.py:73
  35.7 1.3 %collective-permute-start.18 = (f32[104,128]{1,0:T(8,128)S(1)}, f32[104,128]{1,0:T(8,128)S(1)}, u32[]{:S(2)}, u32[]{:S(2)}) collective-permute-start(f32[104,128]{1,0:T(8,128)S(1)} %get-tuple-element.84), channel_id=1, source_target_pairs={{0,16},{8,24},{16,0},{24,8},{1,17},{9,25},{17,1},{25,9},{2,18},{10... | collective-permute-start | bytes 159752 | tf_op jit(solution)/shard_map/ppermute | solution.py:73
  37.6 4.9 %collective-permute-done.11.refs_7_ = f32[8,768]{1,0:T(8,128)S(1)} collective-permute-done((f32[8,768]{1,0:T(8,128)S(1)}, f32[8,768]{1,0:T(8,128)S(1)}, u32[]{:S(2)}, u32[]{:S(2)}) %collective-permute-start.11) | collective-permute-done | bytes 24608 | tf_op jit(solution)/shard_map/ppermute | solution.py:298
  42.5 2.2 %shard_map.102 = (f32[6,4,64,128]{3,2,1,0:T(8,128)S(1)}, f32[8,768]{1,0:T(8,128)S(1)}, f32[24,128]{1,0:T(8,128)S(1)}, f32[24,128]{1,0:T(8,128)S(1)}) custom-call(f32[6,4,64,128]{3,2,1,0:T(8,128)S(1)} %copy-done.1, f32[3,4,64,128]{3,2,1,0:T(8,128)S(1)} %get-tuple-element.62.refs_1_.refs_0_, f32[4,64,128]{2,1,0:T(8,128)S(1)} %copy-done.6, ...), custom_call_target="tpu_custom_call" | custom-call | bytes 2457600 | tf_op jit(solution)/shard_map/pallas_call | solution.py:30
  47.6 3.7 %collective-permute-start.23 = (f32[200,128]{1,0:T(8,128)S(1)}, f32[200,128]{1,0:T(8,128)S(1)}, u32[]{:S(2)}, u32[]{:S(2)}) collective-permute-start(f32[200,128]{1,0:T(8,128)S(1)} %get-tuple-element.91), channel_id=1, source_target_pairs={{0,6},{1,3},{2,4},{3,1},{4,2},{5,7},{6,0},{7,5},{8,14},{9,11},{10,... | collective-permute-start | bytes 307208 | tf_op jit(solution)/shard_map/ppermute | solution.py:82
  51.3 1.7 %collective-permute-start.12 = (f32[24,128]{1,0:T(8,128)S(1)}, f32[24,128]{1,0:T(8,128)S(1)}, u32[]{:S(2)}, u32[]{:S(2)}) collective-permute-start(f32[24,128]{1,0:T(8,128)S(1)} %get-tuple-element.73), channel_id=1, source_target_pairs={{0,8},{8,16},{16,24},{24,0},{1,9},{9,17},{17,25},{25,1},{2,10},{10... | collective-permute-start | bytes 36872 | tf_op jit(solution)/shard_map/ppermute | solution.py:73
  54.3 1.7 %collective-permute-done.12.refs_3_ = f32[24,128]{1,0:T(8,128)S(1)} collective-permute-done((f32[24,128]{1,0:T(8,128)S(1)}, f32[24,128]{1,0:T(8,128)S(1)}, u32[]{:S(2)}, u32[]{:S(2)}) %collective-permute-start.12) | collective-permute-done | bytes 12320 | tf_op jit(solution)/shard_map/ppermute | solution.py:73
  56.8 4.2 %collective-permute-done.15.refs_6_ = f32[8,768]{1,0:T(8,128)S(1)} collective-permute-done((f32[8,768]{1,0:T(8,128)S(1)}, f32[8,768]{1,0:T(8,128)S(1)}, u32[]{:S(2)}, u32[]{:S(2)}) %collective-permute-start.15) | collective-permute-done | bytes 24608 | tf_op jit(solution)/shard_map/ppermute | solution.py:298
  62.8 4.3 %collective-permute-start.24 = (f32[192,128]{1,0:T(8,128)S(1)}, f32[192,128]{1,0:T(8,128)S(1)}, u32[]{:S(2)}, u32[]{:S(2)}) collective-permute-start(f32[192,128]{1,0:T(8,128)S(1)} %get-tuple-element.93.refs_3_.refs_0_), channel_id=1, source_target_pairs={{0,2},{1,7},{2,0},{3,5},{4,6},{5,3},{6,4},{7,1},{8,10},{9,15},{10,... | collective-permute-start | bytes 294920 | tf_op jit(solution)/shard_map/ppermute | solution.py:82
  67.9 1.9 %collective-permute-done.26.refs_3_ = f32[192,128]{1,0:T(8,128)S(1)} collective-permute-done((f32[192,128]{1,0:T(8,128)S(1)}, f32[192,128]{1,0:T(8,128)S(1)}, u32[]{:S(2)}, u32[]{:S(2)}) %collective-permute-start.26) | collective-permute-done | bytes 98336 | tf_op jit(solution)/shard_map/ppermute | solution.py:82
  69.8 1.8 %collective-permute-done.25.refs_2_ = f32[192,128]{1,0:T(8,128)S(1)} collective-permute-done((f32[192,128]{1,0:T(8,128)S(1)}, f32[192,128]{1,0:T(8,128)S(1)}, u32[]{:S(2)}, u32[]{:S(2)}) %collective-permute-start.25) | collective-permute-done | bytes 98336 | tf_op jit(solution)/shard_map/ppermute | solution.py:82
  73.6 1.6 %collective-permute-start.28 = (f32[120,128]{1,0:T(8,128)S(1)}, f32[120,128]{1,0:T(8,128)S(1)}, u32[]{:S(2)}, u32[]{:S(2)}) collective-permute-start(f32[120,128]{1,0:T(8,128)S(1)} %get-tuple-element.97), channel_id=1, source_target_pairs={{0,8},{8,16},{16,24},{24,0},{1,9},{9,17},{17,25},{25,1},{2,10},{10... | collective-permute-start | bytes 184328 | tf_op jit(solution)/shard_map/ppermute | solution.py:73
  75.1 1.4 %collective-permute-start.29 = (f32[120,128]{1,0:T(8,128)S(1)}, f32[120,128]{1,0:T(8,128)S(1)}, u32[]{:S(2)}, u32[]{:S(2)}) collective-permute-start(f32[120,128]{1,0:T(8,128)S(1)} %get-tuple-element.98), channel_id=1, source_target_pairs={{0,24},{8,0},{16,8},{24,16},{1,25},{9,1},{17,9},{25,17},{2,26},{10... | collective-permute-start | bytes 184328 | tf_op jit(solution)/shard_map/ppermute | solution.py:73
  77.1 3.5 %collective-permute-done.32.refs_2_ = f32[96,128]{1,0:T(8,128)S(1)} collective-permute-done((f32[96,128]{1,0:T(8,128)S(1)}, f32[96,128]{1,0:T(8,128)S(1)}, u32[]{:S(2)}, u32[]{:S(2)}) %collective-permute-start.32) | collective-permute-done | bytes 49184 | tf_op jit(solution)/shard_map/ppermute | solution.py:73
  81.6 1.8 %collective-permute-start.33 = (f32[96,128]{1,0:T(8,128)S(1)}, f32[96,128]{1,0:T(8,128)S(1)}, u32[]{:S(2)}, u32[]{:S(2)}) collective-permute-start(f32[96,128]{1,0:T(8,128)S(1)} %get-tuple-element.107), channel_id=1, source_target_pairs={{0,24},{8,0},{16,8},{24,16},{1,25},{9,1},{17,9},{25,17},{2,26},{10... | collective-permute-start | bytes 147464 | tf_op jit(solution)/shard_map/ppermute | solution.py:73
  84.4 1.4 %collective-permute-done.33.refs_1_ = f32[96,128]{1,0:T(8,128)S(1)} collective-permute-done((f32[96,128]{1,0:T(8,128)S(1)}, f32[96,128]{1,0:T(8,128)S(1)}, u32[]{:S(2)}, u32[]{:S(2)}) %collective-permute-start.33) | collective-permute-done | bytes 49184 | tf_op jit(solution)/shard_map/ppermute | solution.py:73
  85.7 1.8 %collective-permute-done.34.refs_2_ = f32[96,128]{1,0:T(8,128)S(1)} collective-permute-done((f32[96,128]{1,0:T(8,128)S(1)}, f32[96,128]{1,0:T(8,128)S(1)}, u32[]{:S(2)}, u32[]{:S(2)}) %collective-permute-start.34) | collective-permute-done | bytes 49184 | tf_op jit(solution)/shard_map/ppermute | solution.py:73
  87.5 1.8 %collective-permute-done.35.refs_3_ = f32[96,128]{1,0:T(8,128)S(1)} collective-permute-done((f32[96,128]{1,0:T(8,128)S(1)}, f32[96,128]{1,0:T(8,128)S(1)}, u32[]{:S(2)}, u32[]{:S(2)}) %collective-permute-start.35) | collective-permute-done | bytes 49184 | tf_op jit(solution)/shard_map/ppermute | solution.py:73
  91.4 2.5 %collective-permute-start.38 = (f32[192,128]{1,0:T(8,128)S(1)}, f32[192,128]{1,0:T(8,128)S(1)}, u32[]{:S(2)}, u32[]{:S(2)}) collective-permute-start(f32[192,128]{1,0:T(8,128)S(1)} %get-tuple-element.112), channel_id=1, source_target_pairs={{0,4},{1,5},{2,6},{3,7},{4,0},{5,1},{6,2},{7,3},{8,12},{9,13},{10,... | collective-permute-start | bytes 294920 | tf_op jit(solution)/shard_map/ppermute | solution.py:82
  93.9 1.9 %collective-permute-start.39 = (f32[192,128]{1,0:T(8,128)S(1)}, f32[192,128]{1,0:T(8,128)S(1)}, u32[]{:S(2)}, u32[]{:S(2)}) collective-permute-start(f32[192,128]{1,0:T(8,128)S(1)} %get-tuple-element.113), channel_id=1, source_target_pairs={{0,6},{1,3},{2,4},{3,1},{4,2},{5,7},{6,0},{7,5},{8,14},{9,11},{10,... | collective-permute-start | bytes 294920 | tf_op jit(solution)/shard_map/ppermute | solution.py:82
  97.4 4.8 %collective-permute-done.31.refs_7_ = f32[8,768]{1,0:T(8,128)S(1)} collective-permute-done((f32[8,768]{1,0:T(8,128)S(1)}, f32[8,768]{1,0:T(8,128)S(1)}, u32[]{:S(2)}, u32[]{:S(2)}) %collective-permute-start.31) | collective-permute-done | bytes 24608 | tf_op jit(solution)/shard_map/ppermute | solution.py:298
  102.2 2.3 %shard_map.114 = (f32[6,4,64,128]{3,2,1,0:T(8,128)}, f32[192,128]{1,0:T(8,128)S(1)}) custom-call(f32[6,4,64,128]{3,2,1,0:T(8,128)S(1)} %get-tuple-element.72.refs_1_.refs_0_, f32[3,4,64,128]{3,2,1,0:T(8,128)S(1)} %copy-done.8, f32[4,64,128]{2,1,0:T(8,128)S(1)} %copy-done.6, f32[4,64,128]{2,1,0:T(8,128)S(1)} %copy-done.7, ...), custom_call_target="tpu_custom_call" | custom-call | bytes 2609152 | tf_op jit(solution)/shard_map/pallas_call | solution.py:30
  (98 shorter events, 27.4 us)
Async XLA Ops:
  2.2 9.7 %collective-permute-start.3 = (f32[8,768]{1,0:T(8,128)S(1)}, f32[8,768]{1,0:T(8,128)S(1)}, u32[]{:S(2)}, u32[]{:S(2)}) collective-permute-start(f32[8,768]{1,0:T(8,128)S(1)} %get-tuple-element.61), channel_id=1, source_target_pairs={{0,7},{1,2},{2,1},{3,4},{4,3},{5,6},{6,5},{7,0},{8,15},{9,10},{10,... | collective-permute-start | bytes 73736 | tf_op jit(solution)/shard_map/ppermute | solution.py:298
  6.7 5.2 %collective-permute-start.2 = (f32[8,768]{1,0:T(8,128)S(1)}, f32[8,768]{1,0:T(8,128)S(1)}, u32[]{:S(2)}, u32[]{:S(2)}) collective-permute-start(f32[8,768]{1,0:T(8,128)S(1)} %get-tuple-element.61), channel_id=1, source_target_pairs={{0,1},{1,0},{2,3},{3,2},{4,5},{5,4},{6,7},{7,6},{8,9},{9,8},{10,11... | collective-permute-start | bytes 73736 | tf_op jit(solution)/shard_map/ppermute | solution.py:89
  6.7 4.6 %collective-permute-start = (f32[24,128]{1,0:T(8,128)S(1)}, f32[24,128]{1,0:T(8,128)S(1)}, u32[]{:S(2)}, u32[]{:S(2)}) collective-permute-start(f32[24,128]{1,0:T(8,128)S(1)} %get-tuple-element.59), channel_id=1, source_target_pairs={{0,8},{8,16},{16,24},{24,0},{1,9},{9,17},{17,25},{25,1},{2,10},{10... | collective-permute-start | bytes 36872 | tf_op jit(solution)/shard_map/ppermute | solution.py:73
  12.3 8.2 %collective-permute-start.6 = (f32[192,128]{1,0:T(8,128)S(1)}, f32[192,128]{1,0:T(8,128)S(1)}, u32[]{:S(2)}, u32[]{:S(2)}) collective-permute-start(f32[192,128]{1,0:T(8,128)S(1)} %shard_map.96.refs_9_.refs_0_), channel_id=1, source_target_pairs={{0,6},{1,3},{2,4},{3,1},{4,2},{5,7},{6,0},{7,5},{8,14},{9,11},{10,... | collective-permute-start | bytes 294920 | tf_op jit(solution)/shard_map/ppermute | solution.py:82
  13.3 10.5 %collective-permute-start.5 = (f32[192,128]{1,0:T(8,128)S(1)}, f32[192,128]{1,0:T(8,128)S(1)}, u32[]{:S(2)}, u32[]{:S(2)}) collective-permute-start(f32[192,128]{1,0:T(8,128)S(1)} %shard_map.96.refs_9_.refs_0_), channel_id=1, source_target_pairs={{0,4},{1,5},{2,6},{3,7},{4,0},{5,1},{6,2},{7,3},{8,12},{9,13},{10,... | collective-permute-start | bytes 294920 | tf_op jit(solution)/shard_map/ppermute | solution.py:82
  14.1 9.7 %collective-permute-start.4 = (f32[192,128]{1,0:T(8,128)S(1)}, f32[192,128]{1,0:T(8,128)S(1)}, u32[]{:S(2)}, u32[]{:S(2)}) collective-permute-start(f32[192,128]{1,0:T(8,128)S(1)} %shard_map.96.refs_9_.refs_0_), channel_id=1, source_target_pairs={{0,2},{1,7},{2,0},{3,5},{4,6},{5,3},{6,4},{7,1},{8,10},{9,15},{10,... | collective-permute-start | bytes 294920 | tf_op jit(solution)/shard_map/ppermute | solution.py:82
  25.8 7.1 %collective-permute-start.8 = (f32[120,128]{1,0:T(8,128)S(1)}, f32[120,128]{1,0:T(8,128)S(1)}, u32[]{:S(2)}, u32[]{:S(2)}) collective-permute-start(f32[120,128]{1,0:T(8,128)S(1)} %get-tuple-element.69), channel_id=1, source_target_pairs={{0,8},{8,16},{16,24},{24,0},{1,9},{9,17},{17,25},{25,1},{2,10},{10... | collective-permute-start | bytes 184328 | tf_op jit(solution)/shard_map/ppermute | solution.py:73
  27.9 4.9 %collective-permute-start.9 = (f32[120,128]{1,0:T(8,128)S(1)}, f32[120,128]{1,0:T(8,128)S(1)}, u32[]{:S(2)}, u32[]{:S(2)}) collective-permute-start(f32[120,128]{1,0:T(8,128)S(1)} %get-tuple-element.70), channel_id=1, source_target_pairs={{0,24},{8,0},{16,8},{24,16},{1,25},{9,1},{17,9},{25,17},{2,26},{10... | collective-permute-start | bytes 184328 | tf_op jit(solution)/shard_map/ppermute | solution.py:73
  28.8 4.1 %collective-permute-start.16 = (f32[96,128]{1,0:T(8,128)S(1)}, f32[96,128]{1,0:T(8,128)S(1)}, u32[]{:S(2)}, u32[]{:S(2)}) collective-permute-start(f32[96,128]{1,0:T(8,128)S(1)} %get-tuple-element.78), channel_id=1, source_target_pairs={{0,16},{8,24},{16,0},{24,8},{1,17},{9,25},{17,1},{25,9},{2,18},{10... | collective-permute-start | bytes 147464 | tf_op jit(solution)/shard_map/ppermute | solution.py:73
  33.9 10.9 %collective-permute-start.17 = (f32[104,128]{1,0:T(8,128)S(1)}, f32[104,128]{1,0:T(8,128)S(1)}, u32[]{:S(2)}, u32[]{:S(2)}) collective-permute-start(f32[104,128]{1,0:T(8,128)S(1)} %get-tuple-element.83), channel_id=1, source_target_pairs={{0,24},{8,0},{16,8},{24,16},{1,25},{9,1},{17,9},{25,17},{2,26},{10... | collective-permute-start | bytes 159752 | tf_op jit(solution)/shard_map/ppermute | solution.py:73
  35.7 9.1 %collective-permute-start.18 = (f32[104,128]{1,0:T(8,128)S(1)}, f32[104,128]{1,0:T(8,128)S(1)}, u32[]{:S(2)}, u32[]{:S(2)}) collective-permute-start(f32[104,128]{1,0:T(8,128)S(1)} %get-tuple-element.84), channel_id=1, source_target_pairs={{0,16},{8,24},{16,0},{24,8},{1,17},{9,25},{17,1},{25,9},{2,18},{10... | collective-permute-start | bytes 159752 | tf_op jit(solution)/shard_map/ppermute | solution.py:73
  37.0 7.8 %collective-permute-start.19 = (f32[104,128]{1,0:T(8,128)S(1)}, f32[104,128]{1,0:T(8,128)S(1)}, u32[]{:S(2)}, u32[]{:S(2)}) collective-permute-start(f32[104,128]{1,0:T(8,128)S(1)} %get-tuple-element.85), channel_id=1, source_target_pairs={{0,8},{8,16},{16,24},{24,0},{1,9},{9,17},{17,25},{25,1},{2,10},{10... | collective-permute-start | bytes 159752 | tf_op jit(solution)/shard_map/ppermute | solution.py:73
  37.4 5.0 %collective-permute-start.11 = (f32[8,768]{1,0:T(8,128)S(1)}, f32[8,768]{1,0:T(8,128)S(1)}, u32[]{:S(2)}, u32[]{:S(2)}) collective-permute-start(f32[8,768]{1,0:T(8,128)S(1)} %get-tuple-element.71), channel_id=1, source_target_pairs={{0,7},{1,2},{2,1},{3,4},{4,3},{5,6},{6,5},{7,0},{8,15},{9,10},{10,... | collective-permute-start | bytes 73736 | tf_op jit(solution)/shard_map/ppermute | solution.py:298
  37.6 5.0 %collective-permute-start.10 = (f32[8,768]{1,0:T(8,128)S(1)}, f32[8,768]{1,0:T(8,128)S(1)}, u32[]{:S(2)}, u32[]{:S(2)}) collective-permute-start(f32[8,768]{1,0:T(8,128)S(1)} %get-tuple-element.71), channel_id=1, source_target_pairs={{0,1},{1,0},{2,3},{3,2},{4,5},{5,4},{6,7},{7,6},{8,9},{9,8},{10,11... | collective-permute-start | bytes 73736 | tf_op jit(solution)/shard_map/ppermute | solution.py:89
  46.9 15.4 %collective-permute-start.21 = (f32[200,128]{1,0:T(8,128)S(1)}, f32[200,128]{1,0:T(8,128)S(1)}, u32[]{:S(2)}, u32[]{:S(2)}) collective-permute-start(f32[200,128]{1,0:T(8,128)S(1)} %get-tuple-element.89), channel_id=1, source_target_pairs={{0,2},{1,7},{2,0},{3,5},{4,6},{5,3},{6,4},{7,1},{8,10},{9,15},{10,... | collective-permute-start | bytes 307208 | tf_op jit(solution)/shard_map/ppermute | solution.py:82
  47.0 15.3 %collective-permute-start.22 = (f32[200,128]{1,0:T(8,128)S(1)}, f32[200,128]{1,0:T(8,128)S(1)}, u32[]{:S(2)}, u32[]{:S(2)}) collective-permute-start(f32[200,128]{1,0:T(8,128)S(1)} %get-tuple-element.90), channel_id=1, source_target_pairs={{0,4},{1,5},{2,6},{3,7},{4,0},{5,1},{6,2},{7,3},{8,12},{9,13},{10,... | collective-permute-start | bytes 307208 | tf_op jit(solution)/shard_map/ppermute | solution.py:82
  47.6 14.7 %collective-permute-start.23 = (f32[200,128]{1,0:T(8,128)S(1)}, f32[200,128]{1,0:T(8,128)S(1)}, u32[]{:S(2)}, u32[]{:S(2)}) collective-permute-start(f32[200,128]{1,0:T(8,128)S(1)} %get-tuple-element.91), channel_id=1, source_target_pairs={{0,6},{1,3},{2,4},{3,1},{4,2},{5,7},{6,0},{7,5},{8,14},{9,11},{10,... | collective-permute-start | bytes 307208 | tf_op jit(solution)/shard_map/ppermute | solution.py:82
  51.3 4.6 %collective-permute-start.12 = (f32[24,128]{1,0:T(8,128)S(1)}, f32[24,128]{1,0:T(8,128)S(1)}, u32[]{:S(2)}, u32[]{:S(2)}) collective-permute-start(f32[24,128]{1,0:T(8,128)S(1)} %get-tuple-element.73), channel_id=1, source_target_pairs={{0,8},{8,16},{16,24},{24,0},{1,9},{9,17},{17,25},{25,1},{2,10},{10... | collective-permute-start | bytes 36872 | tf_op jit(solution)/shard_map/ppermute | solution.py:73
  55.9 5.0 %collective-permute-start.15 = (f32[8,768]{1,0:T(8,128)S(1)}, f32[8,768]{1,0:T(8,128)S(1)}, u32[]{:S(2)}, u32[]{:S(2)}) collective-permute-start(f32[8,768]{1,0:T(8,128)S(1)} %get-tuple-element.75), channel_id=1, source_target_pairs={{0,7},{1,2},{2,1},{3,4},{4,3},{5,6},{6,5},{7,0},{8,15},{9,10},{10,... | collective-permute-start | bytes 73736 | tf_op jit(solution)/shard_map/ppermute | solution.py:298
  56.8 4.2 %collective-permute-start.14 = (f32[8,768]{1,0:T(8,128)S(1)}, f32[8,768]{1,0:T(8,128)S(1)}, u32[]{:S(2)}, u32[]{:S(2)}) collective-permute-start(f32[8,768]{1,0:T(8,128)S(1)} %get-tuple-element.75), channel_id=1, source_target_pairs={{0,1},{1,0},{2,3},{3,2},{4,5},{5,4},{6,7},{7,6},{8,9},{9,8},{10,11... | collective-permute-start | bytes 73736 | tf_op jit(solution)/shard_map/ppermute | solution.py:89
  62.6 7.2 %collective-permute-start.26 = (f32[192,128]{1,0:T(8,128)S(1)}, f32[192,128]{1,0:T(8,128)S(1)}, u32[]{:S(2)}, u32[]{:S(2)}) collective-permute-start(f32[192,128]{1,0:T(8,128)S(1)} %get-tuple-element.93.refs_3_.refs_0_), channel_id=1, source_target_pairs={{0,6},{1,3},{2,4},{3,1},{4,2},{5,7},{6,0},{7,5},{8,14},{9,11},{10,... | collective-permute-start | bytes 294920 | tf_op jit(solution)/shard_map/ppermute | solution.py:82
  62.7 8.9 %collective-permute-start.25 = (f32[192,128]{1,0:T(8,128)S(1)}, f32[192,128]{1,0:T(8,128)S(1)}, u32[]{:S(2)}, u32[]{:S(2)}) collective-permute-start(f32[192,128]{1,0:T(8,128)S(1)} %get-tuple-element.93.refs_3_.refs_0_), channel_id=1, source_target_pairs={{0,4},{1,5},{2,6},{3,7},{4,0},{5,1},{6,2},{7,3},{8,12},{9,13},{10,... | collective-permute-start | bytes 294920 | tf_op jit(solution)/shard_map/ppermute | solution.py:82
  62.8 8.8 %collective-permute-start.24 = (f32[192,128]{1,0:T(8,128)S(1)}, f32[192,128]{1,0:T(8,128)S(1)}, u32[]{:S(2)}, u32[]{:S(2)}) collective-permute-start(f32[192,128]{1,0:T(8,128)S(1)} %get-tuple-element.93.refs_3_.refs_0_), channel_id=1, source_target_pairs={{0,2},{1,7},{2,0},{3,5},{4,6},{5,3},{6,4},{7,1},{8,10},{9,15},{10,... | collective-permute-start | bytes 294920 | tf_op jit(solution)/shard_map/ppermute | solution.py:82
  73.6 7.1 %collective-permute-start.28 = (f32[120,128]{1,0:T(8,128)S(1)}, f32[120,128]{1,0:T(8,128)S(1)}, u32[]{:S(2)}, u32[]{:S(2)}) collective-permute-start(f32[120,128]{1,0:T(8,128)S(1)} %get-tuple-element.97), channel_id=1, source_target_pairs={{0,8},{8,16},{16,24},{24,0},{1,9},{9,17},{17,25},{25,1},{2,10},{10... | collective-permute-start | bytes 184328 | tf_op jit(solution)/shard_map/ppermute | solution.py:73
  75.1 5.5 %collective-permute-start.29 = (f32[120,128]{1,0:T(8,128)S(1)}, f32[120,128]{1,0:T(8,128)S(1)}, u32[]{:S(2)}, u32[]{:S(2)}) collective-permute-start(f32[120,128]{1,0:T(8,128)S(1)} %get-tuple-element.98), channel_id=1, source_target_pairs={{0,24},{8,0},{16,8},{24,16},{1,25},{9,1},{17,9},{25,17},{2,26},{10... | collective-permute-start | bytes 184328 | tf_op jit(solution)/shard_map/ppermute | solution.py:73
  81.6 4.1 %collective-permute-start.33 = (f32[96,128]{1,0:T(8,128)S(1)}, f32[96,128]{1,0:T(8,128)S(1)}, u32[]{:S(2)}, u32[]{:S(2)}) collective-permute-start(f32[96,128]{1,0:T(8,128)S(1)} %get-tuple-element.107), channel_id=1, source_target_pairs={{0,24},{8,0},{16,8},{24,16},{1,25},{9,1},{17,9},{25,17},{2,26},{10... | collective-permute-start | bytes 147464 | tf_op jit(solution)/shard_map/ppermute | solution.py:73
  84.4 5.0 %collective-permute-start.35 = (f32[96,128]{1,0:T(8,128)S(1)}, f32[96,128]{1,0:T(8,128)S(1)}, u32[]{:S(2)}, u32[]{:S(2)}) collective-permute-start(f32[96,128]{1,0:T(8,128)S(1)} %get-tuple-element.109), channel_id=1, source_target_pairs={{0,8},{8,16},{16,24},{24,0},{1,9},{9,17},{17,25},{25,1},{2,10},{10... | collective-permute-start | bytes 147464 | tf_op jit(solution)/shard_map/ppermute | solution.py:73
  91.3 13.2 %collective-permute-start.37 = (f32[192,128]{1,0:T(8,128)S(1)}, f32[192,128]{1,0:T(8,128)S(1)}, u32[]{:S(2)}, u32[]{:S(2)}) collective-permute-start(f32[192,128]{1,0:T(8,128)S(1)} %get-tuple-element.111), channel_id=1, source_target_pairs={{0,2},{1,7},{2,0},{3,5},{4,6},{5,3},{6,4},{7,1},{8,10},{9,15},{10,... | collective-permute-start | bytes 294920 | tf_op jit(solution)/shard_map/ppermute | solution.py:82
  91.4 13.1 %collective-permute-start.38 = (f32[192,128]{1,0:T(8,128)S(1)}, f32[192,128]{1,0:T(8,128)S(1)}, u32[]{:S(2)}, u32[]{:S(2)}) collective-permute-start(f32[192,128]{1,0:T(8,128)S(1)} %get-tuple-element.112), channel_id=1, source_target_pairs={{0,4},{1,5},{2,6},{3,7},{4,0},{5,1},{6,2},{7,3},{8,12},{9,13},{10,... | collective-permute-start | bytes 294920 | tf_op jit(solution)/shard_map/ppermute | solution.py:82
  93.9 10.6 %collective-permute-start.39 = (f32[192,128]{1,0:T(8,128)S(1)}, f32[192,128]{1,0:T(8,128)S(1)}, u32[]{:S(2)}, u32[]{:S(2)}) collective-permute-start(f32[192,128]{1,0:T(8,128)S(1)} %get-tuple-element.113), channel_id=1, source_target_pairs={{0,6},{1,3},{2,4},{3,1},{4,2},{5,7},{6,0},{7,5},{8,14},{9,11},{10,... | collective-permute-start | bytes 294920 | tf_op jit(solution)/shard_map/ppermute | solution.py:82
  95.8 6.4 %collective-permute-start.31 = (f32[8,768]{1,0:T(8,128)S(1)}, f32[8,768]{1,0:T(8,128)S(1)}, u32[]{:S(2)}, u32[]{:S(2)}) collective-permute-start(f32[8,768]{1,0:T(8,128)S(1)} %get-tuple-element.99), channel_id=1, source_target_pairs={{0,7},{1,2},{2,1},{3,4},{4,3},{5,6},{6,5},{7,0},{8,15},{9,10},{10,... | collective-permute-start | bytes 73736 | tf_op jit(solution)/shard_map/ppermute | solution.py:298
  96.6 5.5 %collective-permute-start.30 = (f32[8,768]{1,0:T(8,128)S(1)}, f32[8,768]{1,0:T(8,128)S(1)}, u32[]{:S(2)}, u32[]{:S(2)}) collective-permute-start(f32[8,768]{1,0:T(8,128)S(1)} %get-tuple-element.99), channel_id=1, source_target_pairs={{0,1},{1,0},{2,3},{3,2},{4,5},{5,4},{6,7},{7,6},{8,9},{9,8},{10,11... | collective-permute-start | bytes 73736 | tf_op jit(solution)/shard_map/ppermute | solution.py:89
  (17 other events, 98.7 us)
